TPU v7x, 128 devices: a whole 4x4x4 slice. The times are simulated.
128 devices in a mesh: depth: 16 (over z, y), col: 8 (over x, core).
Axes of the slice: x: 4, y: 4, z: 4, core: 2. Of those that a mesh axis runs over, the one named last changes fastest.
Arguments:
- features: bfloat16 [16, 8, 8192, 256], P('depth', None, 'col'), may hold values from -6 to 6
- counts: int32 [16, 8192], P('depth', 'col'), may hold values from 0 to 8
- steps: float32 [16, 8192], P('depth', 'col'), may hold values from 0.01875 to 0.15
- target: float32 [8192, 512], P('col'), may hold values from -3 to 3
- w_in: bfloat16 [16, 256, 256], P('depth'), may hold values from -0.375 to 0.375
- w_density: bfloat16 [16, 256], P('depth'), may hold values from -0.375 to 0.375
- w_out: bfloat16 [16, 256, 512], P('depth'), may hold values from -0.375 to 0.375
Outputs:
- residual: float32 [8192, 512], P('col')
- density_grad: float32 [16, 8, 8192], P('depth', None, 'col')
- grad_in: float32 [16, 256, 256], P('depth', 'col')
- grad_density: float32 [16, 256], P('depth', 'col')
- grad_out: float32 [16, 256, 512], P('depth', 'col')
Inputs may be any that keep to these rules, and one draw needn't show every extreme that they name: `counts`: a count of 0 means that the ray misses the brick.
All inputs are finite; a program needn't handle non-finite values.
Results may differ from a plain program's by a relative error of at most 0.0019.
Values sent between devices are 32-bit elements; how exact they have to be, the bound alone decides.
A program may use at most 128 MiB of HBM per device.

v0:
```python
import jax
import jax.numpy as jnp
from jax import lax
from jax.sharding import PartitionSpec as P


def sent_to_all(shard, axis):
    count = lax.axis_size(axis)
    return lax.all_to_all(
        jnp.broadcast_to(shard[None], (count, *shard.shape)), axis, 0, 0, tiled=True
    )


def combined_pairwise(pieces, combine):
    while len(jax.tree.leaves(pieces)[0]) > 1:
        pieces = jax.vmap(combine)(*(pieces[side::2] for side in (0, 1)))
    return pieces[0]


def carried_in(shard, axis, combine, identity, reverse):
    count, index = (lax.axis_size(axis), lax.axis_index(axis))
    passed = jnp.arange(count) > index if reverse else jnp.arange(count) < index

    def kept(part, zero, own):
        part = jnp.where(
            passed.reshape(-1, *(1 for _ in own.shape)), part, jnp.asarray(zero, own.dtype)
        )
        return part[::-1] if reverse else part

    pieces = sent_to_all(shard, axis)
    return combined_pairwise(kept(pieces, identity, shard), combine)


def split_up(shard, dim, count):
    dims = shard.shape
    tiles = shard.reshape(*dims[:dim], count, dims[dim] // count, *dims[dim + 1 :])
    return jnp.moveaxis(tiles, dim, 0)


def sent_and_summed(shard, axis, dim):
    count = lax.axis_size(axis)
    tiles = lax.all_to_all(split_up(shard, dim, count), axis, 0, 0, tiled=True)
    return jnp.sum(tiles, axis=0)


def joined_along(tiles, dim):
    dims = list(tiles.shape[1:])
    dims[dim] *= tiles.shape[0]
    return jnp.moveaxis(tiles, 0, dim).reshape(dims)


def gathered_copies(shard, axis, dim):
    return joined_along(sent_to_all(shard, axis), dim)


def in_one_piece(arrays, axis, dim, along):
    both = jnp.concatenate(arrays, axis=along)
    result, at, outs = (lax.psum_scatter(both, axis, scatter_dimension=dim, tiled=True), 0, [])
    for a in arrays:
        outs.append(lax.slice_in_dim(result, at, at + a.shape[along], axis=along))
        at += a.shape[along]
    return tuple(outs)


def exclusive(values):
    total = jnp.cumsum(values, 0)
    return jnp.concatenate([jnp.zeros_like(values[:1]), total[:-1]], 0)


def adding(earlier, later_val):
    return earlier + later_val


def per_device(features, counts, steps, target, w_in, w_density, w_out):
    smp = features.shape[1]
    nray = features.shape[2]
    width = w_out.shape[2]
    rows = features.reshape(smp * nray, features.shape[3])
    pre = jnp.dot(rows, w_in[0], preferred_element_type=jnp.float32)
    hidden = jnp.maximum(pre, 0.0).astype(jnp.bfloat16)
    sig_pre = jnp.dot(hidden, w_density[0], preferred_element_type=jnp.float32).reshape(smp, nray)
    feat = jnp.dot(hidden, w_out[0], preferred_element_type=jnp.float32).reshape(smp, nray, width)
    valid = (lax.broadcasted_iota(jnp.int32, (smp, nray), 0) < counts[0][None, :]).astype(
        jnp.float32
    )
    step_row = steps[0][None, :]
    tau = jax.nn.softplus(sig_pre) * step_row * valid
    inner = exclusive(tau)
    brick_total = jnp.sum(tau, 0)
    position = lax.axis_index("depth")
    before = carried_in(brick_total, "depth", adding, jnp.zeros_like(brick_total), False)
    trans = jnp.exp(-(before[None, :] + inner))
    keep = jnp.exp(-tau)
    wgt = trans * (1.0 - keep)
    partial_value = jnp.sum(wgt[:, :, None] * feat, 0)
    share = sent_and_summed(partial_value, "depth", 0)
    owned = share.shape[0]
    mine = lax.dynamic_slice_in_dim(target, position * owned, owned, 0)
    residual = gathered_copies(share - mine, "depth", 0)
    emission = jnp.sum(feat * residual[None], 2)
    part = wgt * emission
    own = jnp.sum(part, 0)
    after = carried_in(own, "depth", adding, jnp.zeros_like(own), True)
    later_local = jnp.flip(exclusive(jnp.flip(part, 0)), 0)
    dens = (trans * keep * emission - (later_local + after[None, :])) * step_row * valid
    dsig = dens * jax.nn.sigmoid(sig_pre)
    dfeat = (wgt[:, :, None] * residual[None]).astype(jnp.bfloat16).reshape(smp * nray, width)
    dhid = jnp.einsum("nc,hc->nh", dfeat, w_out[0], preferred_element_type=jnp.float32)
    dhid = dhid + dsig.reshape(-1)[:, None] * w_density[0].astype(jnp.float32)[None, :]
    dpre = jnp.where(pre > 0, dhid, 0.0).astype(jnp.bfloat16)
    g_out = jnp.einsum("nh,nc->hc", hidden, dfeat, preferred_element_type=jnp.float32)
    g_in = jnp.einsum("nd,nh->dh", rows, dpre, preferred_element_type=jnp.float32)
    g_den = jnp.dot(dsig.reshape(-1), hidden.astype(jnp.float32))
    sum_in, sum_out, sum_den = (
        *in_one_piece((g_in, g_out), "col", 0, 1),
        lax.psum_scatter(g_den, "col", scatter_dimension=0, tiled=True),
    )
    return (residual, dens[None], sum_in[None], sum_den[None], sum_out[None])


def solution(mesh):
    return jax.shard_map(
        per_device,
        mesh=mesh,
        in_specs=(
            P("depth", None, "col", None),
            P("depth", "col"),
            P("depth", "col"),
            P("col", None),
            P("depth", None, None),
            P("depth", None),
            P("depth", None, None),
        ),
        out_specs=(
            P("col", None),
            P("depth", None, "col"),
            P("depth", "col", None),
            P("depth", "col"),
            P("depth", "col", None),
        ),
        check_vma=False,
    )
```

profile of v0, /device:TPU:1, one launch (start us, length us, event | category | flops | bytes accessed | tf_op | source)
XLA Modules:
  0.0 200.8 jit_solution(15003027408210064687)
XLA Ops:
  7.2 0.0 copy-start
  7.2 0.0 copy-start.6
  7.2 0.0 copy-start.4
  7.2 0.0 copy-start.5
  7.2 6.7 %maximum_convert_fusion = (bf16[8192,256]{1,0:T(8,128)(2,1)S(1)}, f32[8192,256]{1,0:T(8,128)}) fusion(bf16[8192,256]{1,0:T(8,128)(2,1)} %bitcast.108, bf16[1,256,256]{2,1,0:T(8,128)(2,1)} %param.11), kind=kOutput, calls=%fused_computation.8 | convolution fusion | flops 1077936128 | bytes 16908288 | tf_op jit(solution)/shard_map/dot_general | solution.py:79
  13.9 0.0 copy-start.1
  13.9 2.0 %copy-done.1 = bf16[8192,256]{1,0:T(8,128)(2,1)} copy-done((bf16[8192,256]{1,0:T(8,128)(2,1)}, bf16[8192,256]{1,0:T(8,128)(2,1)S(1)}, u32[]{:S(2)}) %copy-start.1) | copy-done | bytes 4194328
  16.0 0.0 copy-done.6
  16.0 1.2 fusion.24
  17.1 0.0 copy-done.4
  17.1 0.0 copy-done.5
  17.1 0.1 fusion.30
  17.2 0.7 broadcast_in_dim.54
  17.9 8.6 %all-to-all-start = ((f32[16,1,1024]{2,1,0:T(1,128)}), f32[16,1,1024]{2,1,0:T(1,128)S(1)}, u32[]{:S(2)}, u32[]{:S(2)}) async-start(f32[16,1,1024]{2,1,0:T(1,128)} %broadcast_in_dim.54), calls=%async_computation | async-start | bytes 131072 | tf_op jit(solution)/shard_map/all_to_all | solution.py:9
  26.5 6.5 %all-to-all-done = f32[16,1,1024]{2,1,0:T(1,128)S(1)} async-done(((f32[16,1,1024]{2,1,0:T(1,128)}), f32[16,1,1024]{2,1,0:T(1,128)S(1)}, u32[]{:S(2)}, u32[]{:S(2)}) %all-to-all-start) | async-done | bytes 65568 | tf_op jit(solution)/shard_map/all_to_all | solution.py:9
  33.0 0.1 bitcast_select_fusion.1
  33.3 0.0 copy-done
  33.3 9.4 %multiply_reduce_fusion.1 = (f32[1024,512]{0,1:T(8,128)S(1)}, f32[8,1024,512]{1,2,0:T(8,128)}) fusion(f32[8,1024]{1,0:T(8,128)S(1)} %subtract_multiply_fusion, bf16[8,1024,256]{2,1,0:T(8,128)(2,1)} %bitcast.102, bf16[1,256,512]{2,1,0:T(8,128)(2,1)S(1)} %copy-done), kind=kOutput, calls=%fused_computation.4 | convolution fusion | flops 2155347968 | bytes 23363584 | tf_op jit(solution)/shard_map/dot_general | solution.py:82
  42.7 1.8 copy.26
  44.5 3.7 %all-to-all-start.1 = ((f32[16,64,512]{2,1,0:T(8,128)}), f32[16,64,512]{2,1,0:T(8,128)S(1)}, u32[]{:S(2)}, u32[]{:S(2)}) async-start(f32[16,64,512]{2,1,0:T(8,128)} %bitcast.107), calls=%async_computation.1 | async-start | bytes 4194304 | tf_op jit(solution)/shard_map/all_to_all | solution.py:42
  48.2 27.1 %all-to-all-done.1 = f32[16,64,512]{2,1,0:T(8,128)S(1)} async-done(((f32[16,64,512]{2,1,0:T(8,128)}), f32[16,64,512]{2,1,0:T(8,128)S(1)}, u32[]{:S(2)}, u32[]{:S(2)}) %all-to-all-start.1) | async-done | bytes 2097184 | tf_op jit(solution)/shard_map/all_to_all | solution.py:42
  75.3 0.2 reduce_sum.47
  75.5 0.9 dynamic-slice_subtract_fusion
  76.4 1.6 broadcast_in_dim.56
  78.0 6.5 %all-to-all-start.2 = ((f32[16,64,512]{2,1,0:T(8,128)}), f32[16,64,512]{2,1,0:T(8,128)S(1)}, u32[]{:S(2)}, u32[]{:S(2)}) async-start(f32[16,64,512]{2,1,0:T(8,128)} %broadcast_in_dim.56), calls=%async_computation.2 | async-start | bytes 4194304 | tf_op jit(solution)/shard_map/all_to_all | solution.py:9
  84.5 28.5 %all-to-all-done.2 = f32[16,64,512]{2,1,0:T(8,128)S(1)} async-done(((f32[16,64,512]{2,1,0:T(8,128)}), f32[16,64,512]{2,1,0:T(8,128)S(1)}, u32[]{:S(2)}, u32[]{:S(2)}) %all-to-all-start.2) | async-done | bytes 2097184 | tf_op jit(solution)/shard_map/all_to_all | solution.py:9
  113.1 1.8 copy.27
  114.9 10.1 %multiply_convert_fusion = (bf16[8,1024,512]{1,2,0:T(8,128)(2,1)}, f32[8,1024]{1,0:T(8,128)S(1)}) fusion(f32[1024,512]{0,1:T(8,128)} %copy.27, f32[8,1024]{1,0:T(8,128)S(1)} %subtract_multiply_fusion, f32[8,1024,512]{1,2,0:T(8,128)} %get-tuple-element.16), kind=kLoop, calls=%fused_computation.2 | loop fusion | flops 16769024 | bytes 27328512 | tf_op jit(solution)/shard_map/convert_element_type | solution.py:107
  125.0 0.7 broadcast_in_dim.58
  125.7 5.5 %all-to-all-start.3 = ((f32[16,1,1024]{2,1,0:T(1,128)}), f32[16,1,1024]{2,1,0:T(1,128)S(1)}, u32[]{:S(2)}, u32[]{:S(2)}) async-start(f32[16,1,1024]{2,1,0:T(1,128)} %broadcast_in_dim.58), calls=%async_computation.3 | async-start | bytes 131072 | tf_op jit(solution)/shard_map/all_to_all | solution.py:9
  131.2 0.0 reduce-scatter.2.cloned.1.call-start
  131.2 0.0 copy-start.2
  131.2 1.4 fusion
  132.7 0.8 copy-done.2
  133.4 2.3 %fusion.32 = f32[256,512]{1,0:T(8,128)S(1)} fusion(bf16[8192,256]{1,0:T(8,128)(2,1)S(1)} %copy-done.2, bf16[8192,512]{1,0:T(8,128)(2,1)S(1)} %fusion), kind=kOutput, calls=%fused_computation.58 | convolution fusion | flops 2147483648 | bytes 13107200 | tf_op jit(solution)/shard_map/nh,nc->hc/dot_general | solution.py:111
  135.8 0.2 rev.8
  136.0 0.2 rev.9
  136.1 11.4 %copy.28 = bf16[8,1024,512]{2,1,0:T(8,128)(2,1)} copy(bf16[8,1024,512]{1,2,0:T(8,128)(2,1)} %get-tuple-element.11) | data formatting | bytes 16777216 | tf_op jit(solution)/shard_map/convert_element_type | solution.py:107
  147.5 0.0 all-to-all-done.3
  147.5 0.1 bitcast_select_fusion
  147.7 0.2 slice.81
  147.8 0.2 slice.83
  148.2 0.0 copy-start.3
  148.3 0.0 copy-start.7
  148.3 9.1 %fusion.7 = f32[256,256]{0,1:T(8,128)S(1)} fusion(bf16[8192,256]{1,0:T(8,128)(2,1)} %bitcast.109, bf16[8192,512]{1,0:T(8,128)(2,1)} %bitcast.106, f32[8192,256]{1,0:T(8,128)} %get-tuple-element.14, f32[256]{0:T(256)S(1)} %mul.118, f32[8192]{0:T(1024)S(1)} %bitcast.119, bf16[1,256,512]{2,1,0:T(8,128)(2,1)S(1)} %copy-done), kind=kOutput, calls=%fused_computation.13 | convolution fusion | flops 3231711232 | bytes 21529600 | tf_op jit(solution)/shard_map/nd,nh->dh/dot_general | solution.py:112
  157.4 0.0 copy-done.3
  157.4 0.1 copy.30
  157.6 0.9 pad_maximum_fusion
  158.5 0.0 reduce-scatter.2.cloned.1.call-update
  158.5 0.0 copy-done.7
  158.5 0.6 dynamic-slice
  159.8 2.8 %fusion.33 = f32[1,256]{1,0:T(1,128)S(1)} fusion(bf16[8192,1]{0,1:T(2,128)(2,1)S(1)} %bitcast.114, bf16[8192,256]{1,0:T(8,128)(2,1)} %copy-done.1), kind=kOutput, calls=%fused_computation.59 | convolution fusion | flops 4194304 | bytes 4211712 | tf_op jit(solution)/shard_map/dot_general | solution.py:113
  162.6 13.0 %all-reduce.2 = f32[256]{0:T(256)S(1)} all-reduce(f32[256]{0:T(256)S(1)} %bitcast.125), channel_id=3, replica_groups=mesh['depth'=16,'col'=8] {'col'}, use_global_device_ids=true, to_apply=%region_8.9.clone | all-reduce | flops 256 | bytes 2048
  175.6 0.6 dynamic-slice_bitcast_fusion
  176.2 13.6 %reduce-scatter.2.cloned.1.call-done = f32[32,768]{1,0:T(8,128)} async-done(((f32[256,768]{1,0:T(8,128)}), f32[32,768]{1,0:T(8,128)}) %reduce-scatter.2.cloned.1.call-update) | async-done | bytes 98320 | tf_op jit(solution)/shard_map/reduce_scatter | solution.py:58
  189.8 1.5 slice_bitcast_fusion
  191.2 1.4 slice_bitcast_fusion.1
  192.6 1.3 copy.54
  (34 shorter events, 0.6 us)
Async XLA Ops:
  7.2 26.1 %copy-start = (bf16[1,256,512]{2,1,0:T(8,128)(2,1)S(1)}, bf16[1,256,512]{2,1,0:T(8,128)(2,1)}, u32[]{:S(2)}) copy-start(bf16[1,256,512]{2,1,0:T(8,128)(2,1)} %param.13) | copy-start | bytes 786436
  7.2 8.8 %copy-start.6 = (bf16[1,256]{1,0:T(2,128)(2,1)S(1)}, bf16[1,256]{1,0:T(2,128)(2,1)}, u32[]{:S(2)}) copy-start(bf16[1,256]{1,0:T(2,128)(2,1)} %param.12) | copy-start | bytes 1540
  7.2 9.9 %copy-start.4 = (f32[1,1024]{1,0:T(1,128)S(1)}, f32[1,1024]{1,0:T(1,128)}, u32[]{:S(2)}) copy-start(f32[1,1024]{1,0:T(1,128)} %param.9) | copy-start | bytes 12292
  7.2 9.9 %copy-start.5 = (s32[1,1024]{1,0:T(1,128)S(1)}, s32[1,1024]{1,0:T(1,128)}, u32[]{:S(2)}) copy-start(s32[1,1024]{1,0:T(1,128)} %param.8) | copy-start | bytes 12292
  13.9 2.0 %copy-start.1 = (bf16[8192,256]{1,0:T(8,128)(2,1)}, bf16[8192,256]{1,0:T(8,128)(2,1)S(1)}, u32[]{:S(2)}) copy-start(bf16[8192,256]{1,0:T(8,128)(2,1)S(1)} %get-tuple-element.13) | copy-start | bytes 12582916
  17.9 15.1 %all-to-all-start = ((f32[16,1,1024]{2,1,0:T(1,128)}), f32[16,1,1024]{2,1,0:T(1,128)S(1)}, u32[]{:S(2)}, u32[]{:S(2)}) async-start(f32[16,1,1024]{2,1,0:T(1,128)} %broadcast_in_dim.54), calls=%async_computation | async-start | bytes 131072 | tf_op jit(solution)/shard_map/all_to_all | solution.py:9
  44.5 30.8 %all-to-all-start.1 = ((f32[16,64,512]{2,1,0:T(8,128)}), f32[16,64,512]{2,1,0:T(8,128)S(1)}, u32[]{:S(2)}, u32[]{:S(2)}) async-start(f32[16,64,512]{2,1,0:T(8,128)} %bitcast.107), calls=%async_computation.1 | async-start | bytes 4194304 | tf_op jit(solution)/shard_map/all_to_all | solution.py:42
  78.0 35.1 %all-to-all-start.2 = ((f32[16,64,512]{2,1,0:T(8,128)}), f32[16,64,512]{2,1,0:T(8,128)S(1)}, u32[]{:S(2)}, u32[]{:S(2)}) async-start(f32[16,64,512]{2,1,0:T(8,128)} %broadcast_in_dim.56), calls=%async_computation.2 | async-start | bytes 4194304 | tf_op jit(solution)/shard_map/all_to_all | solution.py:9
  125.7 21.9 %all-to-all-start.3 = ((f32[16,1,1024]{2,1,0:T(1,128)}), f32[16,1,1024]{2,1,0:T(1,128)S(1)}, u32[]{:S(2)}, u32[]{:S(2)}) async-start(f32[16,1,1024]{2,1,0:T(1,128)} %broadcast_in_dim.58), calls=%async_computation.3 | async-start | bytes 131072 | tf_op jit(solution)/shard_map/all_to_all | solution.py:9
  131.2 58.6 %reduce-scatter.2.cloned.1.call-start = ((), (), s32[]{:S(2)}) async-start(), calls=%async_computation.5 | async-start | bytes 884736 | tf_op jit(solution)/shard_map/reduce_scatter | solution.py:58
  131.2 2.2 %copy-start.2 = (bf16[8192,256]{1,0:T(8,128)(2,1)S(1)}, bf16[8192,256]{1,0:T(8,128)(2,1)}, u32[]{:S(2)}) copy-start(bf16[8192,256]{1,0:T(8,128)(2,1)} %copy-done.1) | copy-start | bytes 12582916
  148.2 9.2 %copy-start.3 = (f32[8,1024]{1,0:T(8,128)}, f32[8,1024]{1,0:T(8,128)S(1)}, u32[]{:S(2)}) copy-start(f32[8,1024]{1,0:T(8,128)S(1)} %get-tuple-element.6) | copy-start | bytes 98308
  148.3 10.3 %copy-start.7 = (u32[128]{0:T(128)S(1)}, u32[128]{0:T(128)}, u32[]{:S(2)}) copy-start(u32[128]{0:T(128)} %constant.39) | copy-start | bytes 1540
Sparse Core Ops, SparseCore 0:
  158.6 31.0 reduce-scatter.1
where the time goes:
time: 204 us; the launch traced here: 201 us
  waiting for transfers between devices  75.7 us (37%)
  matrix products  31.6 us (15%)
  local copies, waits for them, and re-layouts  27.2 us (13%)
  starting transfers between devices  24.3 us (12%)
  between operations  15 us (7%)
  other arithmetic  14 us (7%)
  blocking collectives  13 us (6%)
    all_to_all x3, waiting for transfers between devices, sent_to_all(): lax.all_to_all(jnp.broadcast_to(shard[None], (count, *shard.shape)), axis...  35 us
    all_to_all x1, waiting for transfers between devices, sent_and_summed(): tiles = lax.all_to_all(split_up(shard, dim, count), axis, 0, 0, tiled=True)  27.1 us
    all_to_all x3, starting transfers between devices, sent_to_all(): lax.all_to_all(jnp.broadcast_to(shard[None], (count, *shard.shape)), axis...  20.6 us
    reduce_scatter x1, waiting for transfers between devices, in_one_piece(): lax.psum_scatter(both, axis, scatter_dimension=dim, tiled=True)  13.6 us
    unnamed x1, blocking collectives  13 us
    convert_element_type x2, other arithmetic, per_device(): (wgt[:, :, None] * residual[None]).astype(jnp.bfloat16)  11.5 us
    convert_element_type x1, local copies, waits for them, and re-layouts, per_device(): (wgt[:, :, None] * residual[None]).astype(jnp.bfloat16)  11.4 us
    dot_general x1, matrix products, per_device(): jnp.dot(hidden, w_out[0], preferred_element_type=jnp.float32)  9.39 us
  transfers between devices with their start and end apart: 5, of which 4 were waited for; matrix products, arithmetic and copies ran while one was open for 10% of the time, Pallas kernels for 0%

commit v1 on v0

--- a/solution.py
+++ b/solution.py
@@ -71,15 +71,23 @@
     return earlier + later_val
 
 
+def split_two(x):
+    high = lax.reduce_precision(x, 8, 7)
+    low = x - high
+    return high.astype(jnp.bfloat16), low.astype(jnp.bfloat16)
+
+
+def dot_of(a, b, dims):
+    return lax.dot_general(a, b, (dims, ((), ())), preferred_element_type=jnp.float32)
+
+
 def per_device(features, counts, steps, target, w_in, w_density, w_out):
     smp = features.shape[1]
     nray = features.shape[2]
-    width = w_out.shape[2]
     rows = features.reshape(smp * nray, features.shape[3])
     pre = jnp.dot(rows, w_in[0], preferred_element_type=jnp.float32)
     hidden = jnp.maximum(pre, 0.0).astype(jnp.bfloat16)
     sig_pre = jnp.dot(hidden, w_density[0], preferred_element_type=jnp.float32).reshape(smp, nray)
-    feat = jnp.dot(hidden, w_out[0], preferred_element_type=jnp.float32).reshape(smp, nray, width)
     valid = (lax.broadcasted_iota(jnp.int32, (smp, nray), 0) < counts[0][None, :]).astype(
         jnp.float32
     )
@@ -89,33 +97,36 @@
     brick_total = jnp.sum(tau, 0)
     position = lax.axis_index("depth")
     before = carried_in(brick_total, "depth", adding, jnp.zeros_like(brick_total), False)
+    keep = jnp.exp(-tau)
     trans = jnp.exp(-(before[None, :] + inner))
-    keep = jnp.exp(-tau)
     wgt = trans * (1.0 - keep)
-    partial_value = jnp.sum(wgt[:, :, None] * feat, 0)
+    hid3 = hidden.reshape(smp, nray, -1)
+    hbar = jnp.sum(wgt[:, :, None] * hid3, 0)
+    hb_hi, hb_lo = split_two(hbar)
+    by_cols = ((1,), (0,))
+    partial_value = dot_of(hb_hi, w_out[0], by_cols) + dot_of(hb_lo, w_out[0], by_cols)
     share = sent_and_summed(partial_value, "depth", 0)
     owned = share.shape[0]
     mine = lax.dynamic_slice_in_dim(target, position * owned, owned, 0)
     residual = gathered_copies(share - mine, "depth", 0)
-    emission = jnp.sum(feat * residual[None], 2)
+    re_hi, re_lo = split_two(residual)
+    v = dot_of(re_hi, w_out[0], ((1,), (1,))) + dot_of(re_lo, w_out[0], ((1,), (1,)))
+    emission = jnp.sum(hid3 * v[None], 2)
     part = wgt * emission
     own = jnp.sum(part, 0)
     after = carried_in(own, "depth", adding, jnp.zeros_like(own), True)
     later_local = jnp.flip(exclusive(jnp.flip(part, 0)), 0)
     dens = (trans * keep * emission - (later_local + after[None, :])) * step_row * valid
     dsig = dens * jax.nn.sigmoid(sig_pre)
-    dfeat = (wgt[:, :, None] * residual[None]).astype(jnp.bfloat16).reshape(smp * nray, width)
-    dhid = jnp.einsum("nc,hc->nh", dfeat, w_out[0], preferred_element_type=jnp.float32)
-    dhid = dhid + dsig.reshape(-1)[:, None] * w_density[0].astype(jnp.float32)[None, :]
-    dpre = jnp.where(pre > 0, dhid, 0.0).astype(jnp.bfloat16)
-    g_out = jnp.einsum("nh,nc->hc", hidden, dfeat, preferred_element_type=jnp.float32)
-    g_in = jnp.einsum("nd,nh->dh", rows, dpre, preferred_element_type=jnp.float32)
-    g_den = jnp.dot(dsig.reshape(-1), hidden.astype(jnp.float32))
-    sum_in, sum_out, sum_den = (
-        *in_one_piece((g_in, g_out), "col", 0, 1),
-        lax.psum_scatter(g_den, "col", scatter_dimension=0, tiled=True),
-    )
-    return (residual, dens[None], sum_in[None], sum_den[None], sum_out[None])
+    dhid = wgt[:, :, None] * v[None] + dsig[:, :, None] * w_density[0].astype(jnp.float32)
+    dpre = jnp.where(hid3 > 0, dhid, 0.0).astype(jnp.bfloat16).reshape(smp * nray, -1)
+    first = ((0,), (0,))
+    g_out = dot_of(hb_hi, re_hi, first) + dot_of(hb_lo, re_hi, first) + dot_of(hb_hi, re_lo, first)
+    g_in = dot_of(rows, dpre, first)
+    g_den = jnp.sum(dsig.reshape(-1)[:, None] * hidden.astype(jnp.float32), 0)
+    tiles = lax.all_to_all(jnp.concatenate([g_in, g_out, jnp.broadcast_to(g_den[:, None], (256, 128))], 1), "col", 0, 0, tiled=True)
+    got = jnp.sum(tiles.reshape(8, 32, -1), 0)
+    return (residual, dens[None], got[None, :, :256], got[None, :, 768], got[None, :, 256:768])
 
 
 def solution(mesh):

time: 204 us -> 154 us (0.75); the launches traced: 201 us -> 153 us
  matrix products: 31.6 us -> 13.1 us
  waiting for transfers between devices: 75.7 us -> 61.1 us
  between operations: 15 us -> 0.97 us
  local copies, waits for them, and re-layouts: 27.2 us -> 14.7 us
  blocking collectives: 13 us -> 20.7 us
  other arithmetic: 14 us -> 18.5 us
    all_to_all x0 -> x1, blocking collectives: none -> 20.7 us  [per_device(): lax.all_to_all(jnp.concatenate([g_in, g_out, jnp.broadcast_to(g_den[:, No...]
    dot_general x4 -> x8, matrix products: 23.7 us -> 8.44 us  [dot_of(): lax.dot_general(a, b, (dims, ((), ())), preferred_element_type=jnp.float32)]
    reduce_scatter x1 -> x0, waiting for transfers between devices: 13.6 us -> none  [in_one_piece(): lax.psum_scatter(both, axis, scatter_dimension=dim, tiled=True)]
    unnamed x1 -> x0, blocking collectives: 13 us -> none
    convert_element_type x1 -> x0, local copies, waits for them, and re-layouts: 11.4 us -> none  [per_device(): (wgt[:, :, None] * residual[None]).astype(jnp.bfloat16)]
    reduce_sum x0 -> x3, other arithmetic: none -> 4.73 us  [the longest x1 2.92 us: per_device(): hbar = jnp.sum(wgt[:, :, None] * hid3, 0)]
    convert_element_type x2 -> x3, other arithmetic: 11.5 us -> 7.57 us  [the longest x1 6.49 us: per_device(): jnp.where(hid3 > 0, dhid, 0.0).astype(jnp.bfloat16).reshape(smp * nray, -1)]
    dot_general x1, matrix products: 6.7 us -> 3.49 us  [per_device(): pre = jnp.dot(rows, w_in[0], preferred_element_type=jnp.float32)]
  transfers between devices with their start and end apart: 5 -> 4, of which waited for: 4 -> 4; matrix products, arithmetic and copies ran while one was open for 10% -> 5% of each run, Pallas kernels for 0% -> 0%
where the time goes in v1:
time: 154 us; the launch traced here: 153 us
  waiting for transfers between devices  61.1 us (40%)
  starting transfers between devices  24.4 us (16%)
  blocking collectives  20.7 us (13%)
  other arithmetic  18.5 us (12%)
  local copies, waits for them, and re-layouts  14.7 us (10%)
  matrix products  13.1 us (9%)
    all_to_all x3, waiting for transfers between devices, sent_to_all(): lax.all_to_all(jnp.broadcast_to(shard[None], (count, *shard.shape)), axis...  34 us
    all_to_all x1, waiting for transfers between devices, sent_and_summed(): tiles = lax.all_to_all(split_up(shard, dim, count), axis, 0, 0, tiled=True)  27.1 us
    all_to_all x1, blocking collectives, per_device(): lax.all_to_all(jnp.concatenate([g_in, g_out, jnp.broadcast_to(g_den[:, No...  20.7 us
    all_to_all x3, starting transfers between devices, sent_to_all(): lax.all_to_all(jnp.broadcast_to(shard[None], (count, *shard.shape)), axis...  20.6 us
    dot_general x8, matrix products, dot_of(): lax.dot_general(a, b, (dims, ((), ())), preferred_element_type=jnp.float32)  8.44 us
    convert_element_type x1, other arithmetic, per_device(): jnp.where(hid3 > 0, dhid, 0.0).astype(jnp.bfloat16).reshape(smp * nray, -1)  6.49 us
    unnamed x23, local copies, waits for them, and re-layouts  4.83 us
    all_to_all x1, starting transfers between devices, sent_and_summed(): tiles = lax.all_to_all(split_up(shard, dim, count), axis, 0, 0, tiled=True)  3.72 us
  transfers between devices with their start and end apart: 4, of which 4 were waited for; matrix products, arithmetic and copies ran while one was open for 5% of the time, Pallas kernels for 0%

profile of v1, /device:TPU:1, one launch (start us, length us, event | category | flops | bytes accessed | tf_op | source)
XLA Modules:
  0.0 153.4 jit_solution(10212523119330878821)
XLA Ops:
  0.6 0.0 copy-start
  0.6 0.0 copy-start.9
  0.7 3.5 %fusion = bf16[8192,256]{1,0:T(8,128)(2,1)S(1)} fusion(bf16[8192,256]{1,0:T(8,128)(2,1)} %bitcast.100, bf16[1,256,256]{2,1,0:T(8,128)(2,1)} %param.11), kind=kOutput, calls=%fused_computation.4 | convolution fusion | flops 1077936128 | bytes 8519680 | tf_op jit(solution)/shard_map/dot_general | solution.py:88
  4.2 0.0 copy-start.1
  4.2 0.0 copy-start.7
  4.2 0.0 copy-start.8
  4.2 1.9 %copy-done.1 = bf16[8192,256]{1,0:T(8,128)(2,1)} copy-done((bf16[8192,256]{1,0:T(8,128)(2,1)}, bf16[8192,256]{1,0:T(8,128)(2,1)S(1)}, u32[]{:S(2)}) %copy-start.1) | copy-done | bytes 4194328
  6.1 0.0 copy-done.9
  6.1 1.2 fusion.31
  7.3 0.0 copy-done.7
  7.3 0.0 copy-done.8
  7.3 0.1 fusion.34
  7.3 0.7 broadcast_in_dim.60
  8.0 8.6 %all-to-all-start = ((f32[16,1,1024]{2,1,0:T(1,128)}), f32[16,1,1024]{2,1,0:T(1,128)S(1)}, u32[]{:S(2)}, u32[]{:S(2)}) async-start(f32[16,1,1024]{2,1,0:T(1,128)} %broadcast_in_dim.60), calls=%async_computation | async-start | bytes 131072 | tf_op jit(solution)/shard_map/all_to_all | solution.py:9
  16.6 6.5 %all-to-all-done = f32[16,1,1024]{2,1,0:T(1,128)S(1)} async-done(((f32[16,1,1024]{2,1,0:T(1,128)}), f32[16,1,1024]{2,1,0:T(1,128)S(1)}, u32[]{:S(2)}, u32[]{:S(2)}) %all-to-all-start) | async-done | bytes 65568 | tf_op jit(solution)/shard_map/all_to_all | solution.py:9
  23.1 0.1 bitcast_select_fusion.1
  23.4 2.9 %multiply_reduce_fusion = f32[1024,256]{1,0:T(8,128)S(1)} fusion(bf16[8,1024,256]{2,1,0:T(8,128)(2,1)} %bitcast.95, f32[8,1024]{1,0:T(8,128)S(1)} %subtract_multiply_fusion), kind=kLoop, calls=%fused_computation.10 | loop fusion | flops 6029312 | bytes 5275648 | tf_op jit(solution)/shard_map/reduce_sum | solution.py:104
  26.3 0.0 copy-done
  26.3 0.4 fusion.15
  26.8 1.8 %convolution_add_fusion = f32[1024,512]{1,0:T(8,128)} fusion(f32[1024,512]{1,0:T(8,128)S(1)} %fusion.15, bf16[1,256,512]{2,1,0:T(8,128)(2,1)S(1)} %copy-done, f32[1024,256]{1,0:T(8,128)S(1)} %multiply_reduce_fusion), kind=kOutput, calls=%fused_computation.17 | convolution fusion | flops 269746176 | bytes 5505024 | tf_op jit(solution)/shard_map/dot_general | solution.py:81
  28.5 3.7 %all-to-all-start.1 = ((f32[16,64,512]{2,1,0:T(8,128)}), f32[16,64,512]{2,1,0:T(8,128)S(1)}, u32[]{:S(2)}, u32[]{:S(2)}) async-start(f32[16,64,512]{2,1,0:T(8,128)} %bitcast.102), calls=%async_computation.1 | async-start | bytes 4194304 | tf_op jit(solution)/shard_map/all_to_all | solution.py:42
  32.3 27.1 %all-to-all-done.1 = f32[16,64,512]{2,1,0:T(8,128)S(1)} async-done(((f32[16,64,512]{2,1,0:T(8,128)}), f32[16,64,512]{2,1,0:T(8,128)S(1)}, u32[]{:S(2)}, u32[]{:S(2)}) %all-to-all-start.1) | async-done | bytes 2097184 | tf_op jit(solution)/shard_map/all_to_all | solution.py:42
  59.3 0.8 reduce_sum.67
  60.2 1.0 dynamic-slice_subtract_fusion
  61.1 1.6 %broadcast_in_dim.62 = f32[16,64,512]{2,1,0:T(8,128)} broadcast(f32[64,512]{1,0:T(8,128)S(1)} %dynamic-slice_subtract_fusion), dimensions={1,2} | broadcast | bytes 2228224 | tf_op jit(solution)/shard_map/broadcast_in_dim | solution.py:10
  62.7 6.5 %all-to-all-start.2 = ((f32[16,64,512]{2,1,0:T(8,128)}), f32[16,64,512]{2,1,0:T(8,128)S(1)}, u32[]{:S(2)}, u32[]{:S(2)}) async-start(f32[16,64,512]{2,1,0:T(8,128)} %broadcast_in_dim.62), calls=%async_computation.2 | async-start | bytes 4194304 | tf_op jit(solution)/shard_map/all_to_all | solution.py:9
  69.2 0.5 reduce.2
  69.7 0.7 convert_element_type.54
  70.4 0.5 iota_compare_fusion.1
  70.9 0.6 copy.28
  71.5 26.3 %all-to-all-done.2 = f32[16,64,512]{2,1,0:T(8,128)S(1)} async-done(((f32[16,64,512]{2,1,0:T(8,128)}), f32[16,64,512]{2,1,0:T(8,128)S(1)}, u32[]{:S(2)}, u32[]{:S(2)}) %all-to-all-start.2) | async-done | bytes 2097184 | tf_op jit(solution)/shard_map/all_to_all | solution.py:9
  97.8 0.5 fusion.10
  98.3 1.3 convolution_add_fusion.3
  99.6 0.4 fusion.6
  100.0 0.5 fusion.12
  100.5 0.5 convolution_add_fusion.1
  100.9 0.0 copy-start.4
  100.9 1.0 copy-done.4
  101.9 0.0 copy-done.2
  101.9 1.8 %fusion.2 = f32[8192]{0:T(1024)} fusion(bf16[8192,256]{1,0:T(8,128)(2,1)S(1)} %copy-done.2, f32[1024,256]{1,0:T(8,128)S(1)} %convolution_add_fusion.1), kind=kLoop, calls=%fused_computation.6 | loop fusion | flops 6283264 | bytes 5275648 | tf_op jit(solution)/shard_map/reduce_sum | solution.py:114
  103.7 1.4 reduce_sum.69
  105.1 1.4 fusion.33
  106.4 0.7 broadcast_in_dim.64
  107.1 5.6 %all-to-all-start.3 = ((f32[16,1,1024]{2,1,0:T(1,128)}), f32[16,1,1024]{2,1,0:T(1,128)}, u32[]{:S(2)}, u32[]{:S(2)}) async-start(f32[16,1,1024]{2,1,0:T(1,128)} %broadcast_in_dim.64), calls=%async_computation.3 | async-start | bytes 131072 | tf_op jit(solution)/shard_map/all_to_all | solution.py:9
  112.7 2.3 %convolution_add_fusion.2 = f32[256,512]{1,0:T(8,128)} fusion(f32[256,512]{1,0:T(8,128)} %convolution_add_fusion.3, f32[1024,512]{1,0:T(8,128)S(1)} %bitcast.98, f32[1024,256]{1,0:T(8,128)S(1)} %multiply_reduce_fusion), kind=kOutput, calls=%fused_computation.21 | convolution fusion | flops 270663680 | bytes 4194304 | tf_op jit(solution)/shard_map/dot_general | solution.py:81
  115.0 2.8 %rev.8 = f32[8,1024]{1,0:T(8,128)S(1)} reverse(f32[8,1024]{1,0:T(8,128)} %get-tuple-element.8), dimensions={0} | reverse | bytes 65536 | tf_op jit(solution)/shard_map/jit(_flip)/rev | solution.py:118
  117.8 0.2 rev.9
  118.0 1.3 all-to-all-done.3
  119.3 0.9 bitcast_select_fusion
  120.2 0.2 slice.84
  120.4 0.2 slice.86
  120.7 0.7 fusion.26
  121.4 6.5 %fusion.5 = (bf16[8192,256]{1,0:T(8,128)(2,1)S(1)}, f32[256]{0:T(256)S(1)}) fusion(bf16[8192,256]{1,0:T(8,128)(2,1)} %copy-done.1, f32[256]{0:T(256)S(1)} %convert_element_type.54, f32[8192]{0:T(1024)S(1)} %bitcast.110, f32[8192]{0:T(1024)} %bitcast.109, f32[1024,256]{1,0:T(8,128)} %copy-done.4), kind=kLoop, calls=%fused_computation.9 | loop fusion | flops 18874112 | bytes 9504768 | tf_op jit(solution)/shard_map/convert_element_type | solution.py:122
  127.9 0.0 copy-done.3
  127.9 0.0 copy-start.5
  127.9 1.3 convolution_bitcast_fusion
  129.2 0.1 copy.14
  129.3 0.1 broadcast_in_dim.66
  129.4 0.1 pad_maximum_fusion
  129.5 20.7 %all_to_all.37 = f32[8,32,896]{2,1,0:T(8,128)S(1)} all-to-all(f32[8,32,896]{2,1,0:T(8,128)S(1)} %bitcast.105), channel_id=1, replica_groups=mesh['depth'=16,'col'=8] {'col'}, dimensions={0} | all-to-all | bytes 1835008 | tf_op jit(solution)/shard_map/all_to_all | solution.py:127
  150.2 0.6 slice_bitcast_fusion
  150.9 0.6 slice_bitcast_fusion.1
  151.5 0.6 slice_reduce_fusion
  152.1 1.3 copy.30
  (32 shorter events, 0.5 us)
Async XLA Ops:
  0.6 25.7 %copy-start = (bf16[1,256,512]{2,1,0:T(8,128)(2,1)S(1)}, bf16[1,256,512]{2,1,0:T(8,128)(2,1)}, u32[]{:S(2)}) copy-start(bf16[1,256,512]{2,1,0:T(8,128)(2,1)} %param.13) | copy-start | bytes 786436
  0.6 5.4 %copy-start.9 = (bf16[1,256]{1,0:T(2,128)(2,1)S(1)}, bf16[1,256]{1,0:T(2,128)(2,1)}, u32[]{:S(2)}) copy-start(bf16[1,256]{1,0:T(2,128)(2,1)} %param.12) | copy-start | bytes 1540
  4.2 1.9 %copy-start.1 = (bf16[8192,256]{1,0:T(8,128)(2,1)}, bf16[8192,256]{1,0:T(8,128)(2,1)S(1)}, u32[]{:S(2)}) copy-start(bf16[8192,256]{1,0:T(8,128)(2,1)S(1)} %fusion) | copy-start | bytes 12582916
  4.2 3.1 %copy-start.7 = (f32[1,1024]{1,0:T(1,128)S(1)}, f32[1,1024]{1,0:T(1,128)}, u32[]{:S(2)}) copy-start(f32[1,1024]{1,0:T(1,128)} %param.9) | copy-start | bytes 12292
  4.2 3.1 %copy-start.8 = (s32[1,1024]{1,0:T(1,128)S(1)}, s32[1,1024]{1,0:T(1,128)}, u32[]{:S(2)}) copy-start(s32[1,1024]{1,0:T(1,128)} %param.8) | copy-start | bytes 12292
  8.0 15.1 %all-to-all-start = ((f32[16,1,1024]{2,1,0:T(1,128)}), f32[16,1,1024]{2,1,0:T(1,128)S(1)}, u32[]{:S(2)}, u32[]{:S(2)}) async-start(f32[16,1,1024]{2,1,0:T(1,128)} %broadcast_in_dim.60), calls=%async_computation | async-start | bytes 131072 | tf_op jit(solution)/shard_map/all_to_all | solution.py:9
  28.5 30.8 %all-to-all-start.1 = ((f32[16,64,512]{2,1,0:T(8,128)}), f32[16,64,512]{2,1,0:T(8,128)S(1)}, u32[]{:S(2)}, u32[]{:S(2)}) async-start(f32[16,64,512]{2,1,0:T(8,128)} %bitcast.102), calls=%async_computation.1 | async-start | bytes 4194304 | tf_op jit(solution)/shard_map/all_to_all | solution.py:42
  62.7 35.1 %all-to-all-start.2 = ((f32[16,64,512]{2,1,0:T(8,128)}), f32[16,64,512]{2,1,0:T(8,128)S(1)}, u32[]{:S(2)}, u32[]{:S(2)}) async-start(f32[16,64,512]{2,1,0:T(8,128)} %broadcast_in_dim.62), calls=%async_computation.2 | async-start | bytes 4194304 | tf_op jit(solution)/shard_map/all_to_all | solution.py:9
  99.6 2.3 %copy-start.2 = (bf16[8192,256]{1,0:T(8,128)(2,1)S(1)}, bf16[8192,256]{1,0:T(8,128)(2,1)}, u32[]{:S(2)}) copy-start(bf16[8192,256]{1,0:T(8,128)(2,1)} %copy-done.1) | copy-start | bytes 12582916
  100.9 1.0 copy-start.4
  106.4 14.3 %copy-start.6 = (f32[8,1024]{1,0:T(8,128)S(1)}, f32[8,1024]{1,0:T(8,128)}, u32[]{:S(2)}) copy-start(f32[8,1024]{1,0:T(8,128)} %reduce_sum.69) | copy-start | bytes 98308
  107.1 12.2 %all-to-all-start.3 = ((f32[16,1,1024]{2,1,0:T(1,128)}), f32[16,1,1024]{2,1,0:T(1,128)}, u32[]{:S(2)}, u32[]{:S(2)}) async-start(f32[16,1,1024]{2,1,0:T(1,128)} %broadcast_in_dim.64), calls=%async_computation.3 | async-start | bytes 131072 | tf_op jit(solution)/shard_map/all_to_all | solution.py:9
  121.4 6.5 %copy-start.3 = (bf16[1,8,1024,256]{3,2,1,0:T(8,128)(2,1)S(1)}, bf16[1,8,1024,256]{3,2,1,0:T(8,128)(2,1)}, u32[]{:S(2)}) copy-start(bf16[1,8,1024,256]{3,2,1,0:T(8,128)(2,1)} %param.7) | copy-start | bytes 12582916
  127.9 1.5 copy-start.5

commit v2 on v0

v2 whole, which is shorter than its diff:
```python
import functools

import jax
import jax.numpy as jnp
from jax import lax
from jax.experimental import pallas as pl
from jax.experimental.pallas import tpu as pltpu
from jax.sharding import PartitionSpec as P

STREAMS = 2
PARTS = 4
BLOCKS = 16
LANES = 128
F32 = jnp.float32
BF16 = jnp.bfloat16
NT = (((1,), (1,)), ((), ()))
TN = (((0,), (0,)), ((), ()))
NN = (((1,), (0,)), ((), ()))


def mm(a, b, dims):
    return lax.dot_general(a, b, dims, preferred_element_type=F32)


def halves(x):
    high = x.astype(BF16)
    return high, (x - high.astype(F32)).astype(BF16)


def place(part, block):
    at = 0
    for turn in range(4):
        at = at * 2 + (block // 2 ** ((part + turn) % 4)) % 2
    return at


def block_at(part, at):
    block = 0
    for turn in range(4):
        block = block + (at // 2 ** (3 - turn)) % 2 * 2 ** ((part + turn) % 4)
    return block


def running(x, reverse):
    rows = x.shape[0]
    row = lax.broadcasted_iota(jnp.int32, x.shape, 0)
    total = x
    hop = 1
    while hop < rows:
        moved = pltpu.roll(total, rows - hop if reverse else hop, 0)
        total = total + jnp.where(row < rows - hop if reverse else row >= hop, moved, 0.0)
        hop *= 2
    edge = row < rows - 1 if reverse else row >= 1
    return jnp.where(edge, pltpu.roll(total, rows - 1 if reverse else 1, 0), 0.0)


def body(f_hbm, cnt_ref, step_ref, tgt_hbm, win_ref, wden_ref, wout_ref,
         res_hbm, dens_ref, gin_ref, gden_ref, gout_ref,
         f_ref, hid_ref, lwt_ref, hbar_ref, p_ref, acc_ref, recv_ref, r_ref, res_ref, tgt_ref,
         t_all, own_all, ecol_ref, keep_ref, v_ref, emt_ref, wt_ref, dt_ref, dpre_ref,
         gi_ref, go_ref, gi_recv, go_recv,
         f_sem, tgt_sem, res_sem, s_sem, r_sem, as_sem, ar_sem, ts_sem, tr_sem, os_sem, or_sem,
         gs_sem, gr_sem):
    smp, ray, rows = f_ref.shape[1], f_ref.shape[2], f_ref.shape[2] // BLOCKS
    hid = win_ref.shape[1]
    slab = gin_ref.shape[0]
    me = lax.axis_index("depth")
    col = lax.axis_index("col")
    y, z = me % 4, me // 4
    bits = ((y // 2 + y % 2) % 2, y // 2, (z // 2 + z % 2) % 2, z // 2)
    partners = (z * 4 + y + 1 - 2 * (y % 2), z * 4 + 3 - y,
                (z + 1 - 2 * (z % 2)) * 4 + y, (3 - z) * 4 + y)
    home = bits[0] + 2 * bits[1] + 4 * bits[2] + 8 * bits[3]
    mesh_id = pl.DeviceIdType.MESH

    barrier = pltpu.get_barrier_semaphore()

    def greet_depth(j, _):
        pl.semaphore_signal(barrier, inc=1, device_id={"depth": (me + j) % BLOCKS}, device_id_type=mesh_id)
        return 0

    def greet_col(j, _):
        pl.semaphore_signal(barrier, inc=1, device_id={"col": (col + j) % 8}, device_id_type=mesh_id)
        return 0

    lax.fori_loop(1, BLOCKS, greet_depth, 0)
    lax.fori_loop(1, 8, greet_col, 0)

    def fetch(s, i):
        return pltpu.make_async_copy(
            f_hbm.at[i, pl.ds(s * ray, ray)], f_ref.at[s, i], f_sem.at[s, i])

    def fetch_target(s):
        return pltpu.make_async_copy(
            tgt_hbm.at[s, home], tgt_ref.at[s], tgt_sem.at[s])

    for s in range(STREAMS):
        for i in range(smp):
            fetch(s, i).start()
    for s in range(STREAMS):
        fetch_target(s).start()

    def to_depth(src, dst, send, recv, who):
        return pltpu.make_async_remote_copy(
            src_ref=src, dst_ref=dst, send_sem=send, recv_sem=recv,
            device_id={"depth": who}, device_id_type=mesh_id)

    def spread(store, s, send, recv, j):
        return to_depth(store.at[s, me], store.at[s, me], send.at[s, j], recv.at[s, j], (me + j) % BLOCKS)

    def spread_start(store, s, send, recv):
        def one(j, _):
            spread(store, s, send, recv, j).start()
            return 0
        lax.fori_loop(1, BLOCKS, one, 0)

    def spread_wait(store, s, send, recv):
        def one(j, _):
            spread(store, s, send, recv, j).wait()
            return 0
        lax.fori_loop(1, BLOCKS, one, 0)

    recv_at = (0, 8, 12, 14)

    def span(p, turn):
        at = 0
        for t in range(turn):
            at = at + bits[(p + t) % 4] * (8 >> t)
        return at

    def reduce_copy(s, p, turn):
        half = 8 >> turn
        d = (p + turn) % 4
        away = (1 - bits[d]) * half
        if turn == 0:
            src = p_ref.at[s, p, pl.ds(away, half)]
        else:
            base = span(p, turn) - span(p, 1)
            src = acc_ref.at[s, p, pl.ds(base + away, half)]
        return to_depth(src, recv_ref.at[s, p, pl.ds(recv_at[turn], half)],
                        s_sem.at[s, p, turn], r_sem.at[s, p, turn], partners[d])

    def gather_copy(s, p, turn):
        half = 8 >> turn
        d = (p + turn) % 4
        mine = r_ref.at[s, p, pl.ds(span(p, turn + 1), half)]
        return to_depth(mine, mine, as_sem.at[s, p, turn], ar_sem.at[s, p, turn], partners[d])

    wden = jnp.broadcast_to(wden_ref[...].astype(F32), (smp, hid))
    sample = lax.broadcasted_iota(jnp.int32, (smp, hid), 0)

    def forward(s):
        sig = jnp.zeros((smp, ray), F32)
        for i in range(smp):
            fetch(s, i).wait()
            pre = mm(f_ref[s, i], win_ref[...], NN)
            h = jnp.maximum(pre, 0.0).astype(BF16)
            hid_ref[s, i] = h
            sig = sig + mm(jnp.where(sample == i, wden, 0.0).astype(BF16), h, NT)
        here = pl.ds(s * ray, ray)
        row = lax.broadcasted_iota(jnp.int32, (smp, ray), 0)
        gate = jnp.where(row < cnt_ref[:, here], jnp.broadcast_to(step_ref[:, here], (smp, ray)), 0.0)
        soft = jnp.maximum(sig, 0.0) + jnp.log1p(jnp.exp(-jnp.abs(sig)))
        tau = soft * gate
        inner = running(tau, False)
        t_all[s, me] = (inner + tau)[smp - 1:smp]
        keep = jnp.exp(-tau)
        light = jnp.exp(-inner)
        lw = light * (1.0 - keep)
        keep_ref[s, 0] = lw
        keep_ref[s, 1] = light * keep
        keep_ref[s, 2] = sig
        keep_ref[s, 3] = gate
        lwt_ref[...] = lw.T

    def weigh(s):
        def tile(t, _):
            at = pl.ds(pl.multiple_of(t * 64, 64), 64)
            w = lwt_ref[at]
            total = jnp.zeros((64, hid), F32)
            for i in range(smp):
                total = total + w[:, i:i + 1] * hid_ref[s, i, at].astype(F32)
            hbar_ref[s, at] = total
            return 0
        lax.fori_loop(0, ray // 64, tile, 0)
        high, low = halves(hbar_ref[s])
        value = mm(high, wout_ref[...], NN) + mm(low, wout_ref[...], NN)
        for n in range(BLOCKS):
            for p in range(PARTS):
                p_ref[s, p, place(p, n)] = value[n * rows:(n + 1) * rows, p * LANES:(p + 1) * LANES]

    def depths(s):
        spread_wait(t_all, s, ts_sem, tr_sem)
        whole = t_all[s]
        brick = lax.broadcasted_iota(jnp.int32, whole.shape, 0)
        out = [jnp.exp(-jnp.sum(jnp.where(brick < who, whole, 0.0), 0)) for who in (me, *partners)]
        row = lax.broadcasted_iota(jnp.int32, (smp, ray), 0)
        table = jnp.zeros((smp, ray), F32)
        for i, e in enumerate(out):
            table = jnp.where(row == i, jnp.broadcast_to(e, (smp, ray)), table)
        keep_ref[s, 4] = jnp.broadcast_to(out[0], (smp, ray))
        ecol_ref[s] = table.T.reshape(BLOCKS, rows, smp)

    def combine_first(s, p):
        first = span(p, 1)

        def one(i, _):
            e = ecol_ref[s, block_at(p, first + i)]
            acc_ref[s, p, i] = (e[:, :1] * p_ref[s, p, first + i]
                                + e[:, p + 1:p + 2] * recv_ref[s, p, i])
            return 0
        lax.fori_loop(0, 8, one, 0, unroll=True)

    def combine(s, p, turn):
        base = span(p, turn + 1) - span(p, 1)
        half = 8 >> turn
        here = pl.ds(base, half)
        acc_ref[s, p, here] = acc_ref[s, p, here] + recv_ref[s, p, pl.ds(recv_at[turn], half)]

    def reduce_turn(s, turn):
        for p in range(PARTS):
            reduce_copy(s, p, turn).wait()
            if turn == 0:
                combine_first(s, p)
            else:
                combine(s, p, turn)
            if turn < 3:
                reduce_copy(s, p, turn + 1).start()
            else:
                if p == 0:
                    fetch_target(s).wait()
                at = span(p, 4)
                r_ref[s, p, at] = (acc_ref[s, p, at - span(p, 1)]
                                   - tgt_ref[s, :, p * LANES:(p + 1) * LANES])
                gather_copy(s, p, 3).start()

    def gather_turn(s, turn):
        for p in range(PARTS):
            gather_copy(s, p, turn).wait()
            if turn > 0:
                gather_copy(s, p, turn - 1).start()

    def put_residual(s):
        return pltpu.make_async_copy(res_ref.at[s], res_hbm.at[s], res_sem.at[s])

    def own_terms(s):
        def one(n, _):
            here = pl.ds(pl.multiple_of(n * rows, rows), rows)
            total = jnp.zeros((rows, LANES), F32)
            for p in range(PARTS):
                at = place(p, n)
                r = r_ref[s, p, at]
                res_ref[s, here, p * LANES:(p + 1) * LANES] = r
                total = total + r * p_ref[s, p, at]
            emt_ref[here] = total
            return 0
        lax.fori_loop(0, BLOCKS, one, 0)
        put_residual(s).start()
        high, low = halves(emt_ref[...])
        ones = jnp.ones((smp, LANES), BF16)
        own = (mm(ones, high, NT) + mm(ones, low, NT)) * keep_ref[s, 4]
        own_all[s, me] = own[:1]
        spread_start(own_all, s, os_sem, or_sem)

    def emissions(s):
        r_high, r_low = halves(res_ref[s])
        v_ref[s] = mm(r_high, wout_ref[...], NT) + mm(r_low, wout_ref[...], NT)
        scaled = hbar_ref[s] * jnp.concatenate(
            [ecol_ref[s, n][:, :1] for n in range(BLOCKS)], 0)
        b_high, b_low = halves(scaled)
        out = mm(b_high, r_high, TN) + mm(b_low, r_high, TN) + mm(b_high, r_low, TN)
        for c in range(8):
            mine = out[c * slab:(c + 1) * slab]
            go_ref[c] = mine if s == 0 else go_ref[c] + mine

        def tile(t, _):
            at = pl.ds(pl.multiple_of(t * 64, 64), 64)
            v = v_ref[s, at]
            lane = lax.broadcasted_iota(jnp.int32, (64, smp), 1)
            found = jnp.zeros((64, smp), F32)
            for i in range(smp):
                e = jnp.sum(v * hid_ref[s, i, at].astype(F32), 1, keepdims=True)
                found = jnp.where(lane == i, e, found)
            wt_ref[at] = found
            return 0
        lax.fori_loop(0, ray // 64, tile, 0)
        keep_ref[s, 5] = wt_ref[...].T

    def gradients(s):
        spread_wait(own_all, s, os_sem, or_sem)
        whole = own_all[s]
        brick = lax.broadcasted_iota(jnp.int32, whole.shape, 0)
        after = jnp.sum(jnp.where(brick > me, whole, 0.0), 0)
        e = keep_ref[s, 4]
        em = keep_ref[s, 5]
        wgt = keep_ref[s, 0] * e
        later = running(wgt * em, True) + after
        dens = (keep_ref[s, 1] * e * em - later) * keep_ref[s, 3]
        dens_ref[:, pl.ds(s * ray, ray)] = dens
        dsig = dens / (1.0 + jnp.exp(-keep_ref[s, 2]))
        wt_ref[...] = wgt.T
        dt_ref[...] = dsig.T
        wden_row = wden_ref[...].astype(F32)

        def tile(t, _):
            at = pl.ds(pl.multiple_of(t * 32, 32), 32)
            v = v_ref[s, at]
            w = wt_ref[at]
            d = dt_ref[at]
            for i in range(smp):
                dh = w[:, i:i + 1] * v + d[:, i:i + 1] * wden_row
                h = hid_ref[s, i, at].astype(F32)
                dpre_ref[i, at] = jnp.where(h > 0.0, dh, 0.0).astype(BF16)
            return 0
        lax.fori_loop(0, ray // 32, tile, 0)
        g_in = mm(f_ref[s].reshape(smp * ray, -1), dpre_ref[...].reshape(smp * ray, hid), TN)
        d_high, d_low = halves(dsig)
        stacked = jnp.concatenate([d_high.astype(F32), d_low.astype(F32)], 0)
        row = lax.broadcasted_iota(jnp.int32, stacked.shape, 0)
        g_den = jnp.zeros((2 * smp, hid), F32)
        for i in range(smp):
            g_den = g_den + mm(jnp.where(row % smp == i, stacked, 0.0).astype(BF16), hid_ref[s, i], NN)
        g_den = g_den[:smp] + g_den[smp:]
        for c in range(8):
            mine = g_in[c * slab:(c + 1) * slab]
            if s == 0:
                gi_ref[c, :slab] = mine
                gi_ref[c, slab:] = g_den
            else:
                gi_ref[c, :slab] = gi_ref[c, :slab] + mine
                gi_ref[c, slab:] = gi_ref[c, slab:] + g_den

    def share(kind, j):
        src, dst = ((gi_ref, gi_recv), (go_ref, go_recv))[kind]
        to = (col + j) % 8
        return pltpu.make_async_remote_copy(
            src_ref=src.at[to], dst_ref=dst.at[j - 1], send_sem=gs_sem.at[kind, j],
            recv_sem=gr_sem.at[kind, j], device_id={"col": to}, device_id_type=mesh_id)

    def share_all(kind, wait):
        def one(j, _):
            if wait:
                share(kind, j).wait()
            else:
                share(kind, j).start()
            return 0
        lax.fori_loop(1, 8, one, 0)

    for s in range(STREAMS):
        forward(s)
        if s == 0:
            pl.semaphore_wait(barrier, BLOCKS - 1 + 7)
        spread_start(t_all, s, ts_sem, tr_sem)
        weigh(s)
        for p in range(PARTS):
            reduce_copy(s, p, 0).start()
    for turn in range(4):
        for s in range(STREAMS):
            if turn == 0:
                depths(s)
            reduce_turn(s, turn)
    for turn in (3, 2, 1):
        for s in range(STREAMS):
            gather_turn(s, turn)
    gather_turn(0, 0)
    own_terms(0)
    emissions(0)
    for s in range(1, STREAMS):
        gather_turn(s, 0)
        own_terms(s)
        gradients(s - 1)
        emissions(s)
    share_all(1, False)
    gradients(STREAMS - 1)
    share_all(0, False)
    share_all(1, True)
    total = go_ref[col]
    for j in range(7):
        total = total + go_recv[j]
    gout_ref[...] = total
    share_all(0, True)
    total = gi_ref[col]
    for j in range(7):
        total = total + gi_recv[j]
    gin_ref[...] = total[:slab]
    den = jnp.sum(total[slab:], 0, keepdims=True)
    mine = den[:, :slab]
    for c in range(1, 8):
        mine = jnp.where(col == c, den[:, c * slab:(c + 1) * slab], mine)
    gden_ref[...] = mine
    for s in range(STREAMS):
        put_residual(s).wait()


def per_device(features, counts, steps, target, w_in, w_density, w_out):
    _, smp, nray, din = features.shape
    hid, width = w_out.shape[1:]
    ray = nray // STREAMS
    rows = ray // BLOCKS
    slab = din // 8
    vmem = pl.BlockSpec(memory_space=pltpu.VMEM)
    hbm = pl.BlockSpec(memory_space=pl.ANY)
    dma = pltpu.SemaphoreType.DMA
    stage = (STREAMS, PARTS)
    scratch = [
        pltpu.VMEM((STREAMS, smp, ray, din), BF16),
        pltpu.VMEM((STREAMS, smp, ray, hid), BF16),
        pltpu.VMEM((ray, smp), F32),
        pltpu.VMEM((STREAMS, ray, hid), F32),
        pltpu.VMEM((*stage, BLOCKS, rows, LANES), F32),
        pltpu.VMEM((*stage, BLOCKS // 2, rows, LANES), F32),
        pltpu.VMEM((*stage, BLOCKS - 1, rows, LANES), F32),
        pltpu.VMEM((*stage, BLOCKS, rows, LANES), F32),
        pltpu.VMEM((STREAMS, ray, width), F32),
        pltpu.VMEM((STREAMS, rows, width), F32),
        pltpu.VMEM((STREAMS, BLOCKS, 1, ray), F32),
        pltpu.VMEM((STREAMS, BLOCKS, 1, ray), F32),
        pltpu.VMEM((STREAMS, BLOCKS, rows, smp), F32),
        pltpu.VMEM((STREAMS, 6, smp, ray), F32),
        pltpu.VMEM((STREAMS, ray, hid), F32),
        pltpu.VMEM((ray, LANES), F32),
        pltpu.VMEM((ray, smp), F32),
        pltpu.VMEM((ray, smp), F32),
        pltpu.VMEM((smp, ray, hid), BF16),
        pltpu.VMEM((8, slab + smp, hid), F32),
        pltpu.VMEM((8, slab, width), F32),
        pltpu.VMEM((7, slab + smp, hid), F32),
        pltpu.VMEM((7, slab, width), F32),
        dma((STREAMS, smp)), dma((STREAMS,)), dma((STREAMS,)),
        dma((*stage, 4)), dma((*stage, 4)), dma((*stage, 4)), dma((*stage, 4)),
        dma((STREAMS, BLOCKS)), dma((STREAMS, BLOCKS)), dma((STREAMS, BLOCKS)), dma((STREAMS, BLOCKS)),
        dma((2, 8)), dma((2, 8)),
    ]
    residual, dens, g_in, g_den, g_out = pl.pallas_call(
        body,
        out_shape=(
            jax.ShapeDtypeStruct((STREAMS, ray, width), F32),
            jax.ShapeDtypeStruct((smp, nray), F32),
            jax.ShapeDtypeStruct((slab, hid), F32),
            jax.ShapeDtypeStruct((1, slab), F32),
            jax.ShapeDtypeStruct((slab, width), F32),
        ),
        in_specs=[hbm, vmem, vmem, hbm, vmem, vmem, vmem],
        out_specs=(hbm, vmem, vmem, vmem, vmem),
        scratch_shapes=scratch,
        compiler_params=pltpu.CompilerParams(
            collective_id=0, has_side_effects=True, vmem_limit_bytes=60 * 1024 * 1024),
        name="brick_step",
    )(features[0], counts, steps, target.reshape(STREAMS, BLOCKS, rows, width),
      w_in[0], w_density, w_out[0])
    return residual.reshape(nray, width), dens[None], g_in[None], g_den, g_out[None]


def solution(mesh):
    return jax.shard_map(
        per_device,
        mesh=mesh,
        in_specs=(
            P("depth", None, "col", None),
            P("depth", "col"),
            P("depth", "col"),
            P("col", None),
            P("depth", None, None),
            P("depth", None),
            P("depth", None, None),
        ),
        out_specs=(
            P("col", None),
            P("depth", None, "col"),
            P("depth", "col", None),
            P("depth", "col"),
            P("depth", "col", None),
        ),
        check_vma=False,
    )
```

time: 204 us -> 77.5 us (0.38); the launches traced: 201 us -> 77.4 us
  waiting for transfers between devices: 75.7 us -> 0 us
  Pallas kernels: 0 us -> 71.2 us
  matrix products: 31.6 us -> 0 us
  starting transfers between devices: 24.3 us -> 0 us
  local copies, waits for them, and re-layouts: 27.2 us -> 5.5 us
  between operations: 15 us -> 0.68 us
  other arithmetic: 14 us -> 0 us
  blocking collectives: 13 us -> 0 us
    pallas_call x0 -> x1, Pallas kernels: none -> 71.2 us  [per_device(): pl.pallas_call(body, out_shape=(jax.ShapeDtypeStruct((STREAMS, ray, width...]
    all_to_all x4 -> x0, waiting for transfers between devices: 62.1 us -> none  [the longest x3 35 us: sent_to_all(): lax.all_to_all(jnp.broadcast_to(shard[None], (count, *shard.shape)), axis...]
    dot_general x6 -> x0, matrix products: 31.6 us -> none  [the longest x1 9.39 us: per_device(): jnp.dot(hidden, w_out[0], preferred_element_type=jnp.float32)]
    all_to_all x4 -> x0, starting transfers between devices: 24.3 us -> none  [the longest x3 20.6 us: sent_to_all(): lax.all_to_all(jnp.broadcast_to(shard[None], (count, *shard.shape)), axis...]
    reduce_scatter x1 -> x0, waiting for transfers between devices: 13.6 us -> none  [in_one_piece(): lax.psum_scatter(both, axis, scatter_dimension=dim, tiled=True)]
    unnamed x1 -> x0, blocking collectives: 13 us -> none
    convert_element_type x2 -> x0, other arithmetic: 11.5 us -> none  [per_device(): (wgt[:, :, None] * residual[None]).astype(jnp.bfloat16)]
    convert_element_type x1 -> x0, local copies, waits for them, and re-layouts: 11.4 us -> none  [per_device(): (wgt[:, :, None] * residual[None]).astype(jnp.bfloat16)]
  transfers between devices with their start and end apart: 5 -> 0, of which waited for: 4 -> 0; matrix products, arithmetic and copies ran while one was open for 10% -> 0% of each run, Pallas kernels for 0% -> 0%
where the time goes in v2:
time: 77.5 us; the launch traced here: 77.4 us
  Pallas kernels  71.2 us (92%)
  local copies, waits for them, and re-layouts  5.5 us (7%)
    pallas_call x1, Pallas kernels, per_device(): pl.pallas_call(body, out_shape=(jax.ShapeDtypeStruct((STREAMS, ray, width...  71.2 us
    unnamed x13, local copies, waits for them, and re-layouts  5.5 us

profile of v2, /device:TPU:1, one launch (start us, length us, event | category | flops | bytes accessed | tf_op | source)
XLA Modules:
  0.0 77.4 jit_solution(639476889690928293)
XLA Ops:
  0.6 71.2 %brick_step.1 = (f32[2,512,512]{2,1,0:T(8,128)}, f32[8,1024]{1,0:T(8,128)}, f32[32,256]{1,0:T(8,128)}, f32[1,32]{1,0:T(1,128)}, f32[32,512]{1,0:T(8,128)}) custom-call(bf16[8,1024,256]{2,1,0:T(8,128)(2,1)} %bitcast.8, s32[1,1024]{1,0:T(1,128)} %cnt_ref.1, f32[1,1024]{1,0:T(1,128)} %step_ref.1, f32[2,16,32,512]{3,2,1,0:T(8,128)} %bitcast.10, ...), custom_call_target="tpu_custom_call" | custom-call | tf_op jit(solution)/shard_map/brick_step/pallas_call | solution.py:434
  71.8 0.0 copy-start.2
  71.8 0.0 copy-start.1
  71.9 0.0 copy-start.3
  71.9 0.0 copy-start
  71.9 3.1 %copy.17 = f32[1024,512]{1,0:T(8,128)} copy(f32[1024,512]{1,0:T(8,128)} %bitcast.9) | data formatting | bytes 4194304
  75.0 0.0 copy-done.2
  75.0 0.6 copy.18
  75.6 0.0 copy-done.1
  75.6 0.6 copy.19
  76.2 0.0 copy-done.3
  76.2 0.5 copy.20
  76.7 0.0 copy-done
  76.7 0.6 copy.21
Async XLA Ops:
  71.8 3.2 %copy-start.2 = (f32[8,1024]{1,0:T(8,128)S(1)}, f32[8,1024]{1,0:T(8,128)}, u32[]{:S(2)}) copy-start(f32[8,1024]{1,0:T(8,128)} %get-tuple-element.11) | copy-start | bytes 98308
  71.8 3.8 %copy-start.1 = (f32[32,256]{1,0:T(8,128)S(1)}, f32[32,256]{1,0:T(8,128)}, u32[]{:S(2)}) copy-start(f32[32,256]{1,0:T(8,128)} %get-tuple-element.12) | copy-start | bytes 98308
  71.9 4.4 %copy-start.3 = (f32[1,32]{1,0:T(1,128)S(1)}, f32[1,32]{1,0:T(1,128)}, u32[]{:S(2)}) copy-start(f32[1,32]{1,0:T(1,128)} %get-tuple-element.23) | copy-start | bytes 388
  71.9 4.9 %copy-start = (f32[32,512]{1,0:T(8,128)S(1)}, f32[32,512]{1,0:T(8,128)}, u32[]{:S(2)}) copy-start(f32[32,512]{1,0:T(8,128)} %get-tuple-element.14) | copy-start | bytes 196612

commit v3 on v2

v3 whole, which is shorter than its diff:
```python
import functools

import jax
import jax.numpy as jnp
from jax import lax
from jax.experimental import pallas as pl
from jax.experimental.pallas import tpu as pltpu
from jax.sharding import PartitionSpec as P

STREAMS = 4
RING = 4
BRICKS = 16
COLS = 8
ORDER = ((0, 0), (0, 1), (0, 2), (1, 0), (0, 3), (1, 1), (1, 2), (2, 0), (1, 3), (2, 1), (2, 2), (2, 3))
F32 = jnp.float32
BF16 = jnp.bfloat16
NT = (((1,), (1,)), ((), ()))
TN = (((0,), (0,)), ((), ()))
NN = (((1,), (0,)), ((), ()))


def mm(a, b, dims):
    return lax.dot_general(a, b, dims, preferred_element_type=F32)


def halves(x):
    high = x.astype(BF16)
    return high, (x - high.astype(F32)).astype(BF16)


def running(x, reverse):
    rows = x.shape[0]
    row = lax.broadcasted_iota(jnp.int32, x.shape, 0)
    total = x
    hop = 1
    while hop < rows:
        moved = pltpu.roll(total, rows - hop if reverse else hop, 0)
        total = total + jnp.where(row < rows - hop if reverse else row >= hop, moved, 0.0)
        hop *= 2
    edge = row < rows - 1 if reverse else row >= 1
    return jnp.where(edge, pltpu.roll(total, rows - 1 if reverse else 1, 0), 0.0)


def body(f_hbm, cnt_ref, step_ref, tgt_hbm, win_ref, wden_ref, wout_ref,
         res_hbm, dens_ref, gin_ref, gout_ref,
         f_ref, hid_ref, lwt_ref, hbar_ref, p_ref, ps_ref, acc_ref, recv1_ref, recv2_ref, r_ref, prod_ref, tgt_ref,
         t_all, e_all, own_all, ecol_ref, keep_ref, v_ref, wt_ref, dt_ref, dpre_ref,
         gi_ref, go_ref, gi_recv, go_recv,
         f_sem, tgt_sem, res_sem, s_sem, r_sem, ts_sem, tr_sem, os_sem, or_sem, gs_sem, gr_sem):
    smp, ray = f_ref.shape[1], f_ref.shape[2]
    hid, width = win_ref.shape[1], wout_ref.shape[1]
    part_rays = ray // 2
    quarter = part_rays // RING
    slab = gout_ref.shape[0]
    me = lax.axis_index("depth")
    col = lax.axis_index("col")
    y, z = me % RING, me // RING
    first, second = (y, z), (z, y)
    mesh_id = pl.DeviceIdType.MESH

    barrier = pltpu.get_barrier_semaphore()

    def greet_depth(j, _):
        pl.semaphore_signal(barrier, inc=1, device_id={"depth": (me + j) % BRICKS}, device_id_type=mesh_id)
        return 0

    def greet_col(j, _):
        pl.semaphore_signal(barrier, inc=1, device_id={"col": (col + j) % COLS}, device_id_type=mesh_id)
        return 0

    lax.fori_loop(1, BRICKS, greet_depth, 0)
    lax.fori_loop(1, COLS, greet_col, 0)

    def fetch(s, i):
        return pltpu.make_async_copy(
            f_hbm.at[i, pl.ds(s * ray, ray)], f_ref.at[s, i], f_sem.at[s, i])

    def fetch_target(s, part):
        return pltpu.make_async_copy(
            tgt_hbm.at[s, part, first[part], second[part]], tgt_ref.at[s, part], tgt_sem.at[s, part])

    for s in range(STREAMS):
        for i in range(smp):
            fetch(s, i).start()
    for s in range(STREAMS):
        for part in range(2):
            fetch_target(s, part).start()

    def to_depth(src, dst, send, recv, who):
        return pltpu.make_async_remote_copy(
            src_ref=src, dst_ref=dst, send_sem=send, recv_sem=recv,
            device_id={"depth": who}, device_id_type=mesh_id)

    def spread(store, s, send, recv, j):
        return to_depth(store.at[s, me], store.at[s, me], send.at[s, j], recv.at[s, j], (me + j) % BRICKS)

    def spread_start(store, s, send, recv):
        def one(j, _):
            spread(store, s, send, recv, j).start()
            return 0
        lax.fori_loop(1, BRICKS, one, 0)

    def spread_wait(store, s, send, recv):
        def one(j, _):
            spread(store, s, send, recv, j).wait()
            return 0
        lax.fori_loop(1, BRICKS, one, 0)

    def along(axis, j):
        at = (first[axis] + j) % RING
        return at, (z * RING + at if axis == 0 else at * RING + y)

    def hop(stage, s, part, j):
        near, far = first[part], second[part]
        at, who = along(part if stage in (0, 3) else 1 - part, j)
        if stage == 0:
            src, dst = p_ref.at[s, part, at], recv1_ref.at[s, part, j - 1]
        elif stage == 1:
            src, dst = acc_ref.at[s, part, at], recv2_ref.at[s, part, j - 1]
        elif stage == 2:
            src = dst = r_ref.at[s, part, near, far]
        else:
            src = dst = r_ref.at[s, part, near]
        return to_depth(src, dst, s_sem.at[stage, s, part, j], r_sem.at[stage, s, part, j], who)

    def hops(stage, s, part, what):
        for j in (2, 1, 3):
            getattr(hop(stage, s, part, j), what)()

    wden = jnp.broadcast_to(wden_ref[...].astype(F32), (smp, hid))
    sample = lax.broadcasted_iota(jnp.int32, (smp, hid), 0)

    def forward(s):
        sig = jnp.zeros((smp, ray), F32)
        for i in range(smp):
            fetch(s, i).wait()
            pre = mm(f_ref[s, i], win_ref[...], NN)
            h = jnp.maximum(pre, 0.0).astype(BF16)
            hid_ref[s, i] = h
            sig = sig + mm(jnp.where(sample == i, wden, 0.0).astype(BF16), h, NT)
        here = pl.ds(s * ray, ray)
        row = lax.broadcasted_iota(jnp.int32, (smp, ray), 0)
        gate = jnp.where(row < cnt_ref[:, here], jnp.broadcast_to(step_ref[:, here], (smp, ray)), 0.0)
        soft = jnp.maximum(sig, 0.0) + jnp.log1p(jnp.exp(-jnp.abs(sig)))
        tau = soft * gate
        inner = running(tau, False)
        t_all[s, me] = (inner + tau)[smp - 1:smp]
        keep = jnp.exp(-tau)
        light = jnp.exp(-inner)
        lw = light * (1.0 - keep)
        keep_ref[s, 0] = lw
        keep_ref[s, 1] = light * keep
        keep_ref[s, 2] = sig
        keep_ref[s, 3] = gate
        lwt_ref[...] = lw.T

    def weigh(s):
        def tile(t, _):
            at = pl.ds(pl.multiple_of(t * 64, 64), 64)
            w = lwt_ref[at]
            total = jnp.zeros((64, hid), F32)
            for i in range(smp):
                total = total + w[:, i:i + 1] * hid_ref[s, i, at].astype(F32)
            hbar_ref[s, at] = total
            return 0
        lax.fori_loop(0, ray // 64, tile, 0)
        high, low = halves(hbar_ref[s])
        value = mm(high, wout_ref[...], NN) + mm(low, wout_ref[...], NN)
        p_ref[s] = value.reshape(2, RING, quarter, width)

    def reduce_near(s):
        spread_wait(t_all, s, ts_sem, tr_sem)
        before = jnp.zeros((1, ray), F32)
        for b in range(BRICKS):
            e_all[s, b] = jnp.exp(-before)
            before = before + t_all[s, b]
        row = lax.broadcasted_iota(jnp.int32, (smp, ray), 0)
        table = jnp.broadcast_to(e_all[s, me], (smp, ray))
        for part in range(2):
            for j in range(1, RING):
                mine = e_all[s, along(part, RING - j)[1]]
                table = jnp.where(row == part * RING + j, jnp.broadcast_to(mine, (smp, ray)), table)
        ecol_ref[s] = table.T.reshape(2, RING, quarter, smp)
        for part in range(2):
            near = first[part]
            e = ecol_ref[s, part, near]
            hops(0, s, part, "wait_recv")
            total = None
            for j in range(RING):
                got = p_ref[s, part, near] if j == 0 else recv1_ref[s, part, j - 1]
                got = e[:, part * RING + j:part * RING + j + 1] * got
                ps_ref[s, part, j] = got
                total = got if j == 0 else total + got
            acc_ref[s, part] = total.reshape(RING, quarter // RING, width)
            hops(1, s, part, "start")

    def reduce_far(s):
        for part in range(2):
            fetch_target(s, part).wait()
            hops(1, s, part, "wait_recv")
            total = acc_ref[s, part, second[part]] - tgt_ref[s, part]
            for j in range(1, RING):
                total = total + recv2_ref[s, part, j - 1]
            r_ref[s, part, first[part], second[part]] = total
            hops(2, s, part, "start")

    def gather_far(s):
        for part in range(2):
            hops(2, s, part, "wait_recv")
            hops(3, s, part, "start")
        for part in range(2):
            r = r_ref[s, part, first[part]].reshape(quarter, width)
            for j in range(RING):
                prod_ref[pl.ds((part * RING + j) * quarter, quarter)] = ps_ref[s, part, j] * r
        high, low = halves(prod_ref[...])
        ones = jnp.ones((smp, width), BF16)
        own_all[s, me] = (mm(ones, high, NT) + mm(ones, low, NT))[:1]
        spread_start(own_all, s, os_sem, or_sem)

    def put_residual(s):
        return pltpu.make_async_copy(r_ref.at[s], res_hbm.at[s], res_sem.at[s])

    def gather_near(s):
        for part in range(2):
            hops(3, s, part, "wait_recv")
        put_residual(s).start()

    def emissions(s):
        r_high, r_low = halves(r_ref[s].reshape(ray, width))
        v_ref[...] = mm(r_high, wout_ref[...], NT) + mm(r_low, wout_ref[...], NT)
        scaled = hbar_ref[s] * ecol_ref[s].reshape(ray, smp)[:, :1]
        b_high, b_low = halves(scaled)
        out = mm(b_high, r_high, TN) + mm(b_low, r_high, TN) + mm(b_high, r_low, TN)
        out = out.reshape(COLS, slab, width)
        go_ref[...] = out if s == 0 else go_ref[...] + out

        def tile(t, _):
            at = pl.ds(pl.multiple_of(t * 64, 64), 64)
            v = v_ref[at]
            lane = lax.broadcasted_iota(jnp.int32, (64, smp), 1)
            found = jnp.zeros((64, smp), F32)
            for i in range(smp):
                e = jnp.sum(v * hid_ref[s, i, at].astype(F32), 1, keepdims=True)
                found = jnp.where(lane == i, e, found)
            wt_ref[at] = found
            return 0
        lax.fori_loop(0, ray // 64, tile, 0)
        return wt_ref[...].T

    def later_bricks(s):
        spread_wait(own_all, s, os_sem, or_sem)
        lane = lax.broadcasted_iota(jnp.int32, (1, part_rays), 1)
        slot = lane // quarter
        out = []
        for part in range(2):
            whole = jnp.zeros((1, part_rays), F32)
            for near in range(RING):
                total = jnp.zeros((1, part_rays), F32)
                for far in range(RING):
                    source = (near + RING * far, near * RING + far)[part]
                    from_near = (near - slot + RING) % RING
                    brick = (far * RING + from_near, from_near * RING + far)[part]
                    term = own_all[s, source][:, part * part_rays:(part + 1) * part_rays]
                    total = total + jnp.where(brick > me, term, 0.0)
                total = total + pltpu.roll(total, quarter, 1)
                total = total + pltpu.roll(total, 2 * quarter, 1)
                whole = jnp.where(slot == near, total, whole)
            out.append(whole)
        return jnp.concatenate(out, 1)

    def gradients(s, em):
        e = jnp.broadcast_to(e_all[s, me], (smp, ray))
        wgt = keep_ref[s, 0] * e
        later = running(wgt * em, True) + later_bricks(s)
        dens = (keep_ref[s, 1] * e * em - later) * keep_ref[s, 3]
        dens_ref[:, pl.ds(s * ray, ray)] = dens
        dsig = dens / (1.0 + jnp.exp(-keep_ref[s, 2]))
        wt_ref[...] = wgt.T
        dt_ref[...] = dsig.T
        wden_row = wden_ref[...].astype(F32)

        def tile(t, _):
            at = pl.ds(pl.multiple_of(t * 32, 32), 32)
            v = v_ref[at]
            w = wt_ref[at]
            d = dt_ref[at]
            for i in range(smp):
                dh = w[:, i:i + 1] * v + d[:, i:i + 1] * wden_row
                h = hid_ref[s, i, at].astype(F32)
                dpre_ref[i, at] = jnp.where(h > 0.0, dh, 0.0).astype(BF16)
            return 0
        lax.fori_loop(0, ray // 32, tile, 0)
        g_in = mm(f_ref[s].reshape(smp * ray, -1), dpre_ref[...].reshape(smp * ray, hid), TN)
        d_high, d_low = halves(dsig)
        stacked = jnp.concatenate([d_high.astype(F32), d_low.astype(F32)], 0)
        row = lax.broadcasted_iota(jnp.int32, stacked.shape, 0)
        g_den = jnp.zeros((2 * smp, hid), F32)
        for i in range(smp):
            g_den = g_den + mm(jnp.where(row % smp == i, stacked, 0.0).astype(BF16), hid_ref[s, i], NN)
        g_den = g_den[:smp] + g_den[smp:]
        for c in range(COLS):
            mine = g_in[c * slab:(c + 1) * slab]
            if s == 0:
                gi_ref[c, :slab] = mine
                gi_ref[c, slab:] = g_den
            else:
                gi_ref[c, :slab] = gi_ref[c, :slab] + mine
                gi_ref[c, slab:] = gi_ref[c, slab:] + g_den

    def share(kind, j):
        src, dst = ((gi_ref, gi_recv), (go_ref, go_recv))[kind]
        to = (col + j) % COLS
        return pltpu.make_async_remote_copy(
            src_ref=src.at[to], dst_ref=dst.at[j - 1], send_sem=gs_sem.at[kind, j],
            recv_sem=gr_sem.at[kind, j], device_id={"col": to}, device_id_type=mesh_id)

    def share_all(kind, wait):
        def one(j, _):
            if wait:
                share(kind, j).wait()
            else:
                share(kind, j).start()
            return 0
        lax.fori_loop(1, COLS, one, 0)

    for s in range(STREAMS):
        forward(s)
        if s == 0:
            pl.semaphore_wait(barrier, BRICKS - 1 + COLS - 1)
        spread_start(t_all, s, ts_sem, tr_sem)
        weigh(s)
        for part in range(2):
            hops(0, s, part, "start")
    for step, s in ORDER:
        (reduce_near, reduce_far, gather_far)[step](s)
    for s in range(STREAMS):
        gather_near(s)
        em = emissions(s)
        if s == STREAMS - 1:
            share_all(1, False)
        gradients(s, em)
    share_all(0, False)
    share_all(1, True)
    total = go_ref[col]
    for j in range(COLS - 1):
        total = total + go_recv[j]
    gout_ref[...] = total
    for s in range(STREAMS):
        for part in range(2):
            for stage in range(4):
                hops(stage, s, part, "wait_send")
        put_residual(s).wait()
    share_all(0, True)
    total = gi_ref[col]
    for j in range(COLS - 1):
        total = total + gi_recv[j]
    gin_ref[...] = total


def finish(res_in, dens_in, gin_in, gout_in, res_hbm, dens_ref, gin_ref, gden_ref, gout_ref, held, in_sem, out_sem):
    parts = res_in.shape[0]

    def take(i):
        return pltpu.make_async_copy(res_in.at[i], held.at[i], in_sem.at[i])

    def put(i):
        return pltpu.make_async_copy(held.at[i], res_hbm.at[i], out_sem.at[i])

    for i in range(parts):
        take(i).start()
    dens_ref[...] = dens_in[...]
    gout_ref[...] = gout_in[...]
    slab = gin_ref.shape[0]
    gin_ref[...] = gin_in[:slab]
    den = jnp.sum(gin_in[slab:], 0, keepdims=True)
    col = lax.axis_index("col")
    mine = den[:, :slab]
    for c in range(1, COLS):
        mine = jnp.where(col == c, den[:, c * slab:(c + 1) * slab], mine)
    gden_ref[...] = mine
    for i in range(parts):
        take(i).wait()
        put(i).start()
    for i in range(parts):
        put(i).wait()


def per_device(features, counts, steps, target, w_in, w_density, w_out):
    _, smp, nray, din = features.shape
    hid, width = w_out.shape[1:]
    ray = nray // STREAMS
    quarter = ray // 2 // RING
    piece = quarter // RING
    slab = din // COLS
    vmem = pl.BlockSpec(memory_space=pltpu.VMEM)
    hbm = pl.BlockSpec(memory_space=pl.ANY)
    dma = pltpu.SemaphoreType.DMA
    split = (STREAMS, 2, RING, RING, piece, width)
    scratch = [
        pltpu.VMEM((STREAMS, smp, ray, din), BF16),
        pltpu.VMEM((STREAMS, smp, ray, hid), BF16),
        pltpu.VMEM((ray, smp), F32),
        pltpu.VMEM((STREAMS, ray, hid), F32),
        pltpu.VMEM((STREAMS, 2, RING, quarter, width), F32),
        pltpu.VMEM((STREAMS, 2, RING, quarter, width), F32),
        pltpu.VMEM((STREAMS, 2, RING, piece, width), F32),
        pltpu.VMEM((STREAMS, 2, RING - 1, quarter, width), F32),
        pltpu.VMEM((STREAMS, 2, RING - 1, piece, width), F32),
        pltpu.VMEM(split, F32),
        pltpu.VMEM((ray, width), F32),
        pltpu.VMEM((STREAMS, 2, piece, width), F32),
        pltpu.VMEM((STREAMS, BRICKS, 1, ray), F32),
        pltpu.VMEM((STREAMS, BRICKS, 1, ray), F32),
        pltpu.VMEM((STREAMS, BRICKS, 1, ray), F32),
        pltpu.VMEM((STREAMS, 2, RING, quarter, smp), F32),
        pltpu.VMEM((STREAMS, 4, smp, ray), F32),
        pltpu.VMEM((ray, hid), F32),
        pltpu.VMEM((ray, smp), F32),
        pltpu.VMEM((ray, smp), F32),
        pltpu.VMEM((smp, ray, hid), BF16),
        pltpu.VMEM((COLS, slab + smp, hid), F32),
        pltpu.VMEM((COLS, slab, width), F32),
        pltpu.VMEM((COLS - 1, slab + smp, hid), F32),
        pltpu.VMEM((COLS - 1, slab, width), F32),
        dma((STREAMS, smp)), dma((STREAMS, 2)), dma((STREAMS,)),
        dma((4, STREAMS, 2, RING)), dma((4, STREAMS, 2, RING)),
        dma((STREAMS, BRICKS)), dma((STREAMS, BRICKS)), dma((STREAMS, BRICKS)), dma((STREAMS, BRICKS)),
        dma((2, COLS)), dma((2, COLS)),
    ]
    residual, dens, g_in, g_out = pl.pallas_call(
        body,
        out_shape=(
            jax.ShapeDtypeStruct(split, F32),
            jax.ShapeDtypeStruct((smp, nray), F32),
            jax.ShapeDtypeStruct((slab + smp, hid), F32),
            jax.ShapeDtypeStruct((slab, width), F32),
        ),
        in_specs=[hbm, vmem, vmem, hbm, vmem, vmem, vmem],
        out_specs=(hbm, vmem, vmem, vmem),
        scratch_shapes=scratch,
        compiler_params=pltpu.CompilerParams(
            collective_id=0, has_side_effects=True, vmem_limit_bytes=60 * 1024 * 1024),
        name="brick_step",
    )(features[0], counts, steps, target.reshape(split), w_in[0], w_density, w_out[0])
    residual, dens, g_in, g_den, g_out = pl.pallas_call(
        finish,
        out_shape=(
            jax.ShapeDtypeStruct((STREAMS, ray, width), F32),
            jax.ShapeDtypeStruct((smp, nray), F32),
            jax.ShapeDtypeStruct((slab, hid), F32),
            jax.ShapeDtypeStruct((1, slab), F32),
            jax.ShapeDtypeStruct((slab, width), F32),
        ),
        in_specs=[hbm, vmem, vmem, vmem],
        out_specs=(hbm, vmem, vmem, vmem, vmem),
        scratch_shapes=[pltpu.VMEM((STREAMS, ray, width), F32), dma((STREAMS,)), dma((STREAMS,))],
        name="brick_finish",
    )(residual.reshape(STREAMS, ray, width), dens, g_in, g_out)
    return residual.reshape(nray, width), dens[None], g_in[None], g_den, g_out[None]


def solution(mesh):
    return jax.shard_map(
        per_device,
        mesh=mesh,
        in_specs=(
            P("depth", None, "col", None),
            P("depth", "col"),
            P("depth", "col"),
            P("col", None),
            P("depth", None, None),
            P("depth", None),
            P("depth", None, None),
        ),
        out_specs=(
            P("col", None),
            P("depth", None, "col"),
            P("depth", "col", None),
            P("depth", "col"),
            P("depth", "col", None),
        ),
        check_vma=False,
    )
```

time: 77.5 us -> 69.4 us (0.90)
  local copies, waits for them, and re-layouts: 5.5 us -> 0 us
  Pallas kernels: 71.2 us -> 68.6 us
    unnamed x13 -> x0, local copies, waits for them, and re-layouts: 5.5 us -> none
    pallas_call x1 -> x2, Pallas kernels: 71.2 us -> 68.6 us  [the longest x1 64.6 us: per_device(): pl.pallas_call(body, out_shape=(jax.ShapeDtypeStruct(split, F32), jax.Sha...]
where the time goes in v3:
time: 69.4 us; the launch traced here: 69.2 us
  Pallas kernels  68.6 us (99%)
    pallas_call x1, Pallas kernels, per_device(): pl.pallas_call(body, out_shape=(jax.ShapeDtypeStruct(split, F32), jax.Sha...  64.6 us
    pallas_call x1, Pallas kernels, per_device(): pl.pallas_call(finish, out_shape=(jax.ShapeDtypeStruct((STREAMS, ray, wid...  3.96 us

profile of v3, /device:TPU:1, one launch (start us, length us, event | category | flops | bytes accessed | tf_op | source)
XLA Modules:
  0.0 69.2 jit_solution(7630623576782844893)
XLA Ops:
  0.6 64.6 %brick_step.1 = (f32[4,2,4,4,8,512]{5,4,3,2,1,0:T(8,128)}, f32[8,1024]{1,0:T(8,128)}, f32[40,256]{1,0:T(8,128)}, f32[32,512]{1,0:T(8,128)}) custom-call(bf16[8,1024,256]{2,1,0:T(8,128)(2,1)} %bitcast.9, s32[1,1024]{1,0:T(1,128)} %cnt_ref.1, f32[1,1024]{1,0:T(1,128)} %step_ref.1, f32[4,2,4,4,8,512]{5,4,3,2,1,0:T(8,128)} %bitcast.11, ...), custom_call_target="tpu_custom_call" | custom-call | tf_op jit(solution)/shard_map/brick_step/pallas_call | solution.py:430
  65.2 4.0 %brick_finish.1 = (f32[4,256,512]{2,1,0:T(8,128)}, f32[8,1024]{1,0:T(8,128)}, f32[32,256]{1,0:T(8,128)}, f32[1,32]{1,0:T(1,128)}, f32[32,512]{1,0:T(8,128)}) custom-call(f32[4,256,512]{2,1,0:T(8,128)} %bitcast.10, f32[8,1024]{1,0:T(8,128)} %get-tuple-element.15.dens_in, f32[40,256]{1,0:T(8,128)} %get-tuple-element.16.gin_in, f32[32,512]{1,0:T(8,128)} %get-tuple-element.17.gout_in), custom_call_target="tpu_custom_call" | custom-call | tf_op jit(solution)/shard_map/brick_finish/pallas_call | solution.py:445

commit v4 on v3

--- a/solution.py
+++ b/solution.py
@@ -41,12 +41,12 @@
     return jnp.where(edge, pltpu.roll(total, rows - 1 if reverse else 1, 0), 0.0)
 
 
-def body(f_hbm, cnt_ref, step_ref, tgt_hbm, win_ref, wden_ref, wout_ref,
-         res_hbm, dens_ref, gin_ref, gout_ref,
-         f_ref, hid_ref, lwt_ref, hbar_ref, p_ref, ps_ref, acc_ref, recv1_ref, recv2_ref, r_ref, prod_ref, tgt_ref,
+def body(f_hbm, cnt_hbm, step_hbm, tgt_hbm, win_hbm, wden_hbm, wout_hbm,
+         res_hbm, dens_hbm, gin_hbm, gout_hbm,
+         cnt_ref, step_ref, win_ref, wden_ref, wout_ref, dens_ref, gin_ref, gout_ref, f_ref, hid_ref, lwt_ref, hbar_ref, p_ref, ps_ref, acc_ref, recv1_ref, recv2_ref, r_ref, prod_ref, tgt_ref,
          t_all, e_all, own_all, ecol_ref, keep_ref, v_ref, wt_ref, dt_ref, dpre_ref,
-         gi_ref, go_ref, gi_recv, go_recv,
-         f_sem, tgt_sem, res_sem, s_sem, r_sem, ts_sem, tr_sem, os_sem, or_sem, gs_sem, gr_sem):
+         gi_ref, go_ref, gi_recv, go_pair, go_sum, go_recv,
+         in_sem, f_sem, tgt_sem, out_sem, s_sem, r_sem, ts_sem, tr_sem, os_sem, or_sem, gs_sem, gr_sem):
     smp, ray = f_ref.shape[1], f_ref.shape[2]
     hid, width = win_ref.shape[1], wout_ref.shape[1]
     part_rays = ray // 2
@@ -71,38 +71,40 @@
     lax.fori_loop(1, BRICKS, greet_depth, 0)
     lax.fori_loop(1, COLS, greet_col, 0)
 
-    def fetch(s, i):
-        return pltpu.make_async_copy(
-            f_hbm.at[i, pl.ds(s * ray, ray)], f_ref.at[s, i], f_sem.at[s, i])
+    weights = [
+        pltpu.make_async_copy(src, dst, in_sem.at[i])
+        for i, (src, dst) in enumerate((
+            (win_hbm, win_ref), (wden_hbm, wden_ref), (cnt_hbm, cnt_ref), (step_hbm, step_ref),
+            (wout_hbm, wout_ref)))
+    ]
+
+    def fetch(s):
+        return pltpu.make_async_copy(f_hbm.at[:, pl.ds(s * ray, ray)], f_ref.at[s], f_sem.at[s])
 
     def fetch_target(s, part):
         return pltpu.make_async_copy(
-            tgt_hbm.at[s, part, first[part], second[part]], tgt_ref.at[s, part], tgt_sem.at[s, part])
-
+            tgt_hbm.at[s, part, first[part], second[part]], tgt_ref.at[s, part], tgt_sem.at[0])
+
+    fetch(0).start()
+    for copy in weights:
+        copy.start()
+    for s in range(1, STREAMS):
+        fetch(s).start()
     for s in range(STREAMS):
-        for i in range(smp):
-            fetch(s, i).start()
-    for s in range(STREAMS):
         for part in range(2):
             fetch_target(s, part).start()
+
+    def arrived(ref, sem):
+        pltpu.make_async_copy(ref, ref, sem).wait()
 
     def to_depth(src, dst, send, recv, who):
         return pltpu.make_async_remote_copy(
             src_ref=src, dst_ref=dst, send_sem=send, recv_sem=recv,
             device_id={"depth": who}, device_id_type=mesh_id)
 
-    def spread(store, s, send, recv, j):
-        return to_depth(store.at[s, me], store.at[s, me], send.at[s, j], recv.at[s, j], (me + j) % BRICKS)
-
-    def spread_start(store, s, send, recv):
+    def spread_start(row, send, recv):
         def one(j, _):
-            spread(store, s, send, recv, j).start()
-            return 0
-        lax.fori_loop(1, BRICKS, one, 0)
-
-    def spread_wait(store, s, send, recv):
-        def one(j, _):
-            spread(store, s, send, recv, j).wait()
+            to_depth(row, row, send, recv, (me + j) % BRICKS).start()
             return 0
         lax.fori_loop(1, BRICKS, one, 0)
 
@@ -121,19 +123,27 @@
             src = dst = r_ref.at[s, part, near, far]
         else:
             src = dst = r_ref.at[s, part, near]
-        return to_depth(src, dst, s_sem.at[stage, s, part, j], r_sem.at[stage, s, part, j], who)
-
-    def hops(stage, s, part, what):
+        return to_depth(src, dst, s_sem.at[stage], r_sem.at[stage, s, part], who)
+
+    def send(stage, s, part):
         for j in (2, 1, 3):
-            getattr(hop(stage, s, part, j), what)()
-
-    wden = jnp.broadcast_to(wden_ref[...].astype(F32), (smp, hid))
+            hop(stage, s, part, j).start()
+
+    def got_all(stage, s, part):
+        ref = recv1_ref if stage in (0, 3) else recv2_ref
+        arrived(ref.at[s, part], r_sem.at[stage, s, part])
+
     sample = lax.broadcasted_iota(jnp.int32, (smp, hid), 0)
+    pair = ray * 2
 
     def forward(s):
+        fetch(s).wait()
+        if s == 0:
+            for copy in weights[:4]:
+                copy.wait()
+        wden = jnp.broadcast_to(wden_ref[...].astype(F32), (smp, hid))
         sig = jnp.zeros((smp, ray), F32)
         for i in range(smp):
-            fetch(s, i).wait()
             pre = mm(f_ref[s, i], win_ref[...], NN)
             h = jnp.maximum(pre, 0.0).astype(BF16)
             hid_ref[s, i] = h
@@ -144,7 +154,7 @@
         soft = jnp.maximum(sig, 0.0) + jnp.log1p(jnp.exp(-jnp.abs(sig)))
         tau = soft * gate
         inner = running(tau, False)
-        t_all[s, me] = (inner + tau)[smp - 1:smp]
+        t_all[s // 2, me, :, s % 2 * ray:(s % 2 + 1) * ray] = (inner + tau)[smp - 1:smp]
         keep = jnp.exp(-tau)
         light = jnp.exp(-inner)
         lw = light * (1.0 - keep)
@@ -164,16 +174,21 @@
             hbar_ref[s, at] = total
             return 0
         lax.fori_loop(0, ray // 64, tile, 0)
+        if s == 0:
+            weights[4].wait()
         high, low = halves(hbar_ref[s])
         value = mm(high, wout_ref[...], NN) + mm(low, wout_ref[...], NN)
         p_ref[s] = value.reshape(2, RING, quarter, width)
 
     def reduce_near(s):
-        spread_wait(t_all, s, ts_sem, tr_sem)
-        before = jnp.zeros((1, ray), F32)
-        for b in range(BRICKS):
-            e_all[s, b] = jnp.exp(-before)
-            before = before + t_all[s, b]
+        if s % 2 == 0:
+            arrived(t_all.at[s // 2, pl.ds(0, BRICKS - 1)], tr_sem.at[s // 2])
+            before = jnp.zeros((1, pair), F32)
+            for b in range(BRICKS):
+                light = jnp.exp(-before)
+                e_all[s, b] = light[:, :ray]
+                e_all[s + 1, b] = light[:, ray:]
+                before = before + t_all[s // 2, b]
         row = lax.broadcasted_iota(jnp.int32, (smp, ray), 0)
         table = jnp.broadcast_to(e_all[s, me], (smp, ray))
         for part in range(2):
@@ -184,7 +199,7 @@
         for part in range(2):
             near = first[part]
             e = ecol_ref[s, part, near]
-            hops(0, s, part, "wait_recv")
+            got_all(0, s, part)
             total = None
             for j in range(RING):
                 got = p_ref[s, part, near] if j == 0 else recv1_ref[s, part, j - 1]
@@ -192,22 +207,23 @@
                 ps_ref[s, part, j] = got
                 total = got if j == 0 else total + got
             acc_ref[s, part] = total.reshape(RING, quarter // RING, width)
-            hops(1, s, part, "start")
+            send(1, s, part)
 
     def reduce_far(s):
-        for part in range(2):
-            fetch_target(s, part).wait()
-            hops(1, s, part, "wait_recv")
+        if s == 0:
+            arrived(tgt_ref, tgt_sem.at[0])
+        for part in range(2):
+            got_all(1, s, part)
             total = acc_ref[s, part, second[part]] - tgt_ref[s, part]
             for j in range(1, RING):
                 total = total + recv2_ref[s, part, j - 1]
             r_ref[s, part, first[part], second[part]] = total
-            hops(2, s, part, "start")
+            send(2, s, part)
 
     def gather_far(s):
         for part in range(2):
-            hops(2, s, part, "wait_recv")
-            hops(3, s, part, "start")
+            got_all(2, s, part)
+            send(3, s, part)
         for part in range(2):
             r = r_ref[s, part, first[part]].reshape(quarter, width)
             for j in range(RING):
@@ -215,14 +231,14 @@
         high, low = halves(prod_ref[...])
         ones = jnp.ones((smp, width), BF16)
         own_all[s, me] = (mm(ones, high, NT) + mm(ones, low, NT))[:1]
-        spread_start(own_all, s, os_sem, or_sem)
+        spread_start(own_all.at[s, me], os_sem.at[0], or_sem.at[s])
 
     def put_residual(s):
-        return pltpu.make_async_copy(r_ref.at[s], res_hbm.at[s], res_sem.at[s])
+        return pltpu.make_async_copy(r_ref.at[s], res_hbm.at[s], out_sem.at[0])
 
     def gather_near(s):
         for part in range(2):
-            hops(3, s, part, "wait_recv")
+            got_all(3, s, part)
         put_residual(s).start()
 
     def emissions(s):
@@ -231,8 +247,11 @@
         scaled = hbar_ref[s] * ecol_ref[s].reshape(ray, smp)[:, :1]
         b_high, b_low = halves(scaled)
         out = mm(b_high, r_high, TN) + mm(b_low, r_high, TN) + mm(b_high, r_low, TN)
-        out = out.reshape(COLS, slab, width)
-        go_ref[...] = out if s == 0 else go_ref[...] + out
+        for c in range(COLS):
+            mine = out[c * slab:(c + 1) * slab]
+            go_ref[c % 2, c // 2] = mine if s == 0 else go_ref[c % 2, c // 2] + mine
+        if s == STREAMS - 1:
+            pair_copy.start()
 
         def tile(t, _):
             at = pl.ds(pl.multiple_of(t * 64, 64), 64)
@@ -248,7 +267,7 @@
         return wt_ref[...].T
 
     def later_bricks(s):
-        spread_wait(own_all, s, os_sem, or_sem)
+        arrived(own_all.at[s, pl.ds(0, BRICKS - 1)], or_sem.at[s])
         lane = lax.broadcasted_iota(jnp.int32, (1, part_rays), 1)
         slot = lane // quarter
         out = []
@@ -290,6 +309,8 @@
                 dpre_ref[i, at] = jnp.where(h > 0.0, dh, 0.0).astype(BF16)
             return 0
         lax.fori_loop(0, ray // 32, tile, 0)
+        if s == STREAMS - 1:
+            share_out()
         g_in = mm(f_ref[s].reshape(smp * ray, -1), dpre_ref[...].reshape(smp * ray, hid), TN)
         d_high, d_low = halves(dsig)
         stacked = jnp.concatenate([d_high.astype(F32), d_low.astype(F32)], 0)
@@ -307,82 +328,98 @@
                 gi_ref[c, :slab] = gi_ref[c, :slab] + mine
                 gi_ref[c, slab:] = gi_ref[c, slab:] + g_den
 
-    def share(kind, j):
-        src, dst = ((gi_ref, gi_recv), (go_ref, go_recv))[kind]
+    x, core = col // 2, col % 2
+
+    def to_col(src, dst, send, recv, who):
+        return pltpu.make_async_remote_copy(
+            src_ref=src, dst_ref=dst, send_sem=send, recv_sem=recv,
+            device_id={"col": who}, device_id_type=mesh_id)
+
+    pair_copy = to_col(go_ref.at[1 - core], go_pair, gs_sem.at[0], gr_sem.at[0], x * 2 + 1 - core)
+
+    def share_out():
+        pair_copy.wait_recv()
+        go_sum[...] = go_ref[core] + go_pair[...]
+        for j in (2, 1, 3):
+            to = (x + j) % RING
+            to_col(go_sum.at[to], go_recv.at[j - 1], gs_sem.at[1], gr_sem.at[1], to * 2 + core).start()
+
+    def share_in(j, _):
         to = (col + j) % COLS
-        return pltpu.make_async_remote_copy(
-            src_ref=src.at[to], dst_ref=dst.at[j - 1], send_sem=gs_sem.at[kind, j],
-            recv_sem=gr_sem.at[kind, j], device_id={"col": to}, device_id_type=mesh_id)
-
-    def share_all(kind, wait):
-        def one(j, _):
-            if wait:
-                share(kind, j).wait()
-            else:
-                share(kind, j).start()
-            return 0
-        lax.fori_loop(1, COLS, one, 0)
+        to_col(gi_ref.at[to], gi_recv.at[j - 1], gs_sem.at[2], gr_sem.at[2], to).start()
+        return 0
 
     for s in range(STREAMS):
         forward(s)
         if s == 0:
             pl.semaphore_wait(barrier, BRICKS - 1 + COLS - 1)
-        spread_start(t_all, s, ts_sem, tr_sem)
+        if s % 2 == 1:
+            spread_start(t_all.at[s // 2, me], ts_sem.at[0], tr_sem.at[s // 2])
         weigh(s)
         for part in range(2):
-            hops(0, s, part, "start")
+            send(0, s, part)
     for step, s in ORDER:
         (reduce_near, reduce_far, gather_far)[step](s)
     for s in range(STREAMS):
         gather_near(s)
         em = emissions(s)
-        if s == STREAMS - 1:
-            share_all(1, False)
         gradients(s, em)
-    share_all(0, False)
-    share_all(1, True)
-    total = go_ref[col]
-    for j in range(COLS - 1):
+    lax.fori_loop(1, COLS, share_in, 0)
+    dens_copy = pltpu.make_async_copy(dens_ref, dens_hbm, out_sem.at[1])
+    dens_copy.start()
+    arrived(go_recv, gr_sem.at[1])
+    total = go_sum[x]
+    for j in range(RING - 1):
         total = total + go_recv[j]
     gout_ref[...] = total
-    for s in range(STREAMS):
-        for part in range(2):
-            for stage in range(4):
-                hops(stage, s, part, "wait_send")
-        put_residual(s).wait()
-    share_all(0, True)
+    gout_copy = pltpu.make_async_copy(gout_ref, gout_hbm, out_sem.at[2])
+    gout_copy.start()
+    arrived(recv1_ref, s_sem.at[0])
+    arrived(recv2_ref, s_sem.at[1])
+    arrived(recv2_ref, s_sem.at[2])
+    arrived(recv1_ref, s_sem.at[3])
+    arrived(t_all.at[:, pl.ds(0, BRICKS - 1)], ts_sem.at[0])
+    arrived(own_all.at[:, pl.ds(0, BRICKS - 1)], os_sem.at[0])
+    pair_copy.wait_send()
+    arrived(go_recv, gs_sem.at[1])
+    arrived(r_ref, out_sem.at[0])
+    dens_copy.wait()
+    arrived(gi_recv, gr_sem.at[2])
     total = gi_ref[col]
     for j in range(COLS - 1):
         total = total + gi_recv[j]
     gin_ref[...] = total
-
-
-def finish(res_in, dens_in, gin_in, gout_in, res_hbm, dens_ref, gin_ref, gden_ref, gout_ref, held, in_sem, out_sem):
+    gin_copy = pltpu.make_async_copy(gin_ref, gin_hbm, out_sem.at[3])
+    gin_copy.start()
+    arrived(gi_recv, gs_sem.at[2])
+    gout_copy.wait()
+    gin_copy.wait()
+
+
+def finish(res_in, dens_in, gin_in, gout_in, res_hbm, dens_hbm, gin_hbm, gden_hbm, gout_hbm,
+           held, dens_ref, gin_ref, gout_ref, gden_ref, in_sem, out_sem):
     parts = res_in.shape[0]
-
-    def take(i):
-        return pltpu.make_async_copy(res_in.at[i], held.at[i], in_sem.at[i])
-
-    def put(i):
-        return pltpu.make_async_copy(held.at[i], res_hbm.at[i], out_sem.at[i])
-
-    for i in range(parts):
-        take(i).start()
-    dens_ref[...] = dens_in[...]
-    gout_ref[...] = gout_in[...]
-    slab = gin_ref.shape[0]
-    gin_ref[...] = gin_in[:slab]
-    den = jnp.sum(gin_in[slab:], 0, keepdims=True)
+    slab = gin_hbm.shape[0]
+    take = [pltpu.make_async_copy(src, dst, in_sem.at[i]) for i, (src, dst) in enumerate(
+        [(gin_in, gin_ref), (dens_in, dens_ref), (gout_in, gout_ref)]
+        + [(res_in.at[i], held.at[i]) for i in range(parts)])]
+    put = [pltpu.make_async_copy(src, dst, out_sem.at[i]) for i, (src, dst) in enumerate(
+        [(gin_ref.at[pl.ds(0, slab)], gin_hbm), (dens_ref, dens_hbm), (gout_ref, gout_hbm)]
+        + [(held.at[i], res_hbm.at[i]) for i in range(parts)] + [(gden_ref, gden_hbm)])]
+    for copy in take:
+        copy.start()
+    for got, gone in zip(take, put):
+        got.wait()
+        gone.start()
+    den = jnp.sum(gin_ref[slab:], 0, keepdims=True)
     col = lax.axis_index("col")
     mine = den[:, :slab]
     for c in range(1, COLS):
         mine = jnp.where(col == c, den[:, c * slab:(c + 1) * slab], mine)
     gden_ref[...] = mine
-    for i in range(parts):
-        take(i).wait()
-        put(i).start()
-    for i in range(parts):
-        put(i).wait()
+    put[-1].start()
+    for copy in put:
+        copy.wait()
 
 
 def per_device(features, counts, steps, target, w_in, w_density, w_out):
@@ -392,11 +429,18 @@
     quarter = ray // 2 // RING
     piece = quarter // RING
     slab = din // COLS
-    vmem = pl.BlockSpec(memory_space=pltpu.VMEM)
     hbm = pl.BlockSpec(memory_space=pl.ANY)
     dma = pltpu.SemaphoreType.DMA
     split = (STREAMS, 2, RING, RING, piece, width)
     scratch = [
+        pltpu.VMEM((1, nray), jnp.int32),
+        pltpu.VMEM((1, nray), F32),
+        pltpu.VMEM((din, hid), BF16),
+        pltpu.VMEM((1, hid), BF16),
+        pltpu.VMEM((hid, width), BF16),
+        pltpu.VMEM((smp, nray), F32),
+        pltpu.VMEM((slab + smp, hid), F32),
+        pltpu.VMEM((slab, width), F32),
         pltpu.VMEM((STREAMS, smp, ray, din), BF16),
         pltpu.VMEM((STREAMS, smp, ray, hid), BF16),
         pltpu.VMEM((ray, smp), F32),
@@ -409,7 +453,7 @@
         pltpu.VMEM(split, F32),
         pltpu.VMEM((ray, width), F32),
         pltpu.VMEM((STREAMS, 2, piece, width), F32),
-        pltpu.VMEM((STREAMS, BRICKS, 1, ray), F32),
+        pltpu.VMEM((STREAMS // 2, BRICKS, 1, 2 * ray), F32),
         pltpu.VMEM((STREAMS, BRICKS, 1, ray), F32),
         pltpu.VMEM((STREAMS, BRICKS, 1, ray), F32),
         pltpu.VMEM((STREAMS, 2, RING, quarter, smp), F32),
@@ -419,13 +463,15 @@
         pltpu.VMEM((ray, smp), F32),
         pltpu.VMEM((smp, ray, hid), BF16),
         pltpu.VMEM((COLS, slab + smp, hid), F32),
-        pltpu.VMEM((COLS, slab, width), F32),
+        pltpu.VMEM((2, RING, slab, width), F32),
         pltpu.VMEM((COLS - 1, slab + smp, hid), F32),
-        pltpu.VMEM((COLS - 1, slab, width), F32),
-        dma((STREAMS, smp)), dma((STREAMS, 2)), dma((STREAMS,)),
-        dma((4, STREAMS, 2, RING)), dma((4, STREAMS, 2, RING)),
-        dma((STREAMS, BRICKS)), dma((STREAMS, BRICKS)), dma((STREAMS, BRICKS)), dma((STREAMS, BRICKS)),
-        dma((2, COLS)), dma((2, COLS)),
+        pltpu.VMEM((RING, slab, width), F32),
+        pltpu.VMEM((RING, slab, width), F32),
+        pltpu.VMEM((RING - 1, slab, width), F32),
+        dma((5,)), dma((STREAMS,)), dma((1,)), dma((4,)),
+        dma((4,)), dma((4, STREAMS, 2)),
+        dma((1,)), dma((STREAMS // 2,)), dma((1,)), dma((STREAMS,)),
+        dma((3,)), dma((3,)),
     ]
     residual, dens, g_in, g_out = pl.pallas_call(
         body,
@@ -435,8 +481,8 @@
             jax.ShapeDtypeStruct((slab + smp, hid), F32),
             jax.ShapeDtypeStruct((slab, width), F32),
         ),
-        in_specs=[hbm, vmem, vmem, hbm, vmem, vmem, vmem],
-        out_specs=(hbm, vmem, vmem, vmem),
+        in_specs=[hbm] * 7,
+        out_specs=(hbm,) * 4,
         scratch_shapes=scratch,
         compiler_params=pltpu.CompilerParams(
             collective_id=0, has_side_effects=True, vmem_limit_bytes=60 * 1024 * 1024),
@@ -451,9 +497,16 @@
             jax.ShapeDtypeStruct((1, slab), F32),
             jax.ShapeDtypeStruct((slab, width), F32),
         ),
-        in_specs=[hbm, vmem, vmem, vmem],
-        out_specs=(hbm, vmem, vmem, vmem, vmem),
-        scratch_shapes=[pltpu.VMEM((STREAMS, ray, width), F32), dma((STREAMS,)), dma((STREAMS,))],
+        in_specs=[hbm] * 4,
+        out_specs=(hbm,) * 5,
+        scratch_shapes=[
+            pltpu.VMEM((STREAMS, ray, width), F32),
+            pltpu.VMEM((smp, nray), F32),
+            pltpu.VMEM((slab + smp, hid), F32),
+            pltpu.VMEM((slab, width), F32),
+            pltpu.VMEM((1, slab), F32),
+            dma((3 + STREAMS,)), dma((4 + STREAMS,)),
+        ],
         name="brick_finish",
     )(residual.reshape(STREAMS, ray, width), dens, g_in, g_out)
     return residual.reshape(nray, width), dens[None], g_in[None], g_den, g_out[None]

time: 69.4 us -> 63 us (0.908)
  Pallas kernels: 68.6 us -> 62.3 us
    pallas_call x1, Pallas kernels: 64.6 us -> 59.5 us  [per_device(): pl.pallas_call(body, out_shape=(jax.ShapeDtypeStruct(split, F32), jax.Sha...]
    pallas_call x1, Pallas kernels: 3.96 us -> 2.79 us  [per_device(): pl.pallas_call(finish, out_shape=(jax.ShapeDtypeStruct((STREAMS, ray, wid...]
where the time goes in v4:
time: 63 us; the launch traced here: 62.9 us
  Pallas kernels  62.3 us (99%)
  between operations  0.64 us (1%)
    pallas_call x1, Pallas kernels, per_device(): pl.pallas_call(body, out_shape=(jax.ShapeDtypeStruct(split, F32), jax.Sha...  59.5 us
    pallas_call x1, Pallas kernels, per_device(): pl.pallas_call(finish, out_shape=(jax.ShapeDtypeStruct((STREAMS, ray, wid...  2.79 us

profile of v4, /device:TPU:1, one launch (start us, length us, event | category | flops | bytes accessed | tf_op | source)
XLA Modules:
  0.0 62.9 jit_solution(7899115599341351094)
XLA Ops:
  0.6 59.5 %brick_step.1 = (f32[4,2,4,4,8,512]{5,4,3,2,1,0:T(8,128)}, f32[8,1024]{1,0:T(8,128)}, f32[40,256]{1,0:T(8,128)}, f32[32,512]{1,0:T(8,128)}) custom-call(bf16[8,1024,256]{2,1,0:T(8,128)(2,1)} %bitcast.9, s32[1,1024]{1,0:T(1,128)} %cnt_hbm.1, f32[1,1024]{1,0:T(1,128)} %step_hbm.1, f32[4,2,4,4,8,512]{5,4,3,2,1,0:T(8,128)} %bitcast.11, ...), custom_call_target="tpu_custom_call" | custom-call | tf_op jit(solution)/shard_map/brick_step/pallas_call | solution.py:476
  60.1 2.8 %brick_finish.1 = (f32[4,256,512]{2,1,0:T(8,128)}, f32[8,1024]{1,0:T(8,128)}, f32[32,256]{1,0:T(8,128)}, f32[1,32]{1,0:T(1,128)}, f32[32,512]{1,0:T(8,128)}) custom-call(f32[4,256,512]{2,1,0:T(8,128)} %bitcast.10, f32[8,1024]{1,0:T(8,128)} %get-tuple-element.15.dens_in, f32[40,256]{1,0:T(8,128)} %get-tuple-element.16.gin_in, f32[32,512]{1,0:T(8,128)} %get-tuple-element.17.gout_in), custom_call_target="tpu_custom_call" | custom-call | tf_op jit(solution)/shard_map/brick_finish/pallas_call | solution.py:491

commit v5 on v4

--- a/solution.py
+++ b/solution.py
@@ -11,7 +11,11 @@
 RING = 4
 BRICKS = 16
 COLS = 8
-ORDER = ((0, 0), (0, 1), (0, 2), (1, 0), (0, 3), (1, 1), (1, 2), (2, 0), (1, 3), (2, 1), (2, 2), (2, 3))
+PARTS = 4
+LANES = 128
+ORDER = ((0, 0), (0, 1), (1, 0), (0, 2), (1, 1), (0, 3), (1, 2), (2, 0), (1, 3), (2, 1), (2, 2), (3, 0),
+         (2, 3), (3, 1), (4, 0), (3, 2), (4, 1), (3, 3), (4, 2), (5, 0), (4, 3), (6, 0), (5, 1), (7, 0),
+         (5, 2), (6, 1), (7, 1), (5, 3), (6, 2), (7, 2), (6, 3), (7, 3))
 F32 = jnp.float32
 BF16 = jnp.bfloat16
 NT = (((1,), (1,)), ((), ()))
@@ -26,6 +30,20 @@
 def halves(x):
     high = x.astype(BF16)
     return high, (x - high.astype(F32)).astype(BF16)
+
+
+def place(part, block):
+    at = 0
+    for turn in range(4):
+        at = at * 2 + (block // 2 ** ((part + turn) % 4)) % 2
+    return at
+
+
+def block_at(part, at):
+    block = 0
+    for turn in range(4):
+        block = block + (at // 2 ** (3 - turn)) % 2 * 2 ** ((part + turn) % 4)
+    return block
 
 
 def running(x, reverse):
@@ -43,19 +61,29 @@
 
 def body(f_hbm, cnt_hbm, step_hbm, tgt_hbm, win_hbm, wden_hbm, wout_hbm,
          res_hbm, dens_hbm, gin_hbm, gout_hbm,
-         cnt_ref, step_ref, win_ref, wden_ref, wout_ref, dens_ref, gin_ref, gout_ref, f_ref, hid_ref, lwt_ref, hbar_ref, p_ref, ps_ref, acc_ref, recv1_ref, recv2_ref, r_ref, prod_ref, tgt_ref,
+         cnt_ref, step_ref, win_ref, wden_ref, wout_ref, dens_ref, gin_ref, gout_ref, f_ref, hid_ref, lwt_ref, hbar_ref, p_ref, acc_ref, recv_ref, r_ref, res_ref, emt_ref, tgt_ref,
          t_all, e_all, own_all, ecol_ref, keep_ref, v_ref, wt_ref, dt_ref, dpre_ref,
          gi_ref, go_ref, gi_recv, go_pair, go_sum, go_recv,
          in_sem, f_sem, tgt_sem, out_sem, s_sem, r_sem, ts_sem, tr_sem, os_sem, or_sem, gs_sem, gr_sem):
     smp, ray = f_ref.shape[1], f_ref.shape[2]
     hid, width = win_ref.shape[1], wout_ref.shape[1]
-    part_rays = ray // 2
-    quarter = part_rays // RING
+    rows = ray // BRICKS
     slab = gout_ref.shape[0]
     me = lax.axis_index("depth")
     col = lax.axis_index("col")
     y, z = me % RING, me // RING
-    first, second = (y, z), (z, y)
+    bits = ((y // 2 + y % 2) % 2, y // 2, (z // 2 + z % 2) % 2, z // 2)
+    home = bits[0] + 2 * bits[1] + 4 * bits[2] + 8 * bits[3]
+
+    def moved(at, low, high):
+        if low and high:
+            return (at + 2) % RING
+        return RING - 1 - at if high else at + 1 - 2 * (at % 2) if low else at
+
+    def other(*dims):
+        return (moved(z, 2 in dims, 3 in dims) * RING
+                + moved(y, 0 in dims, 1 in dims))
+
     mesh_id = pl.DeviceIdType.MESH
 
     barrier = pltpu.get_barrier_semaphore()
@@ -81,9 +109,8 @@
     def fetch(s):
         return pltpu.make_async_copy(f_hbm.at[:, pl.ds(s * ray, ray)], f_ref.at[s], f_sem.at[s])
 
-    def fetch_target(s, part):
-        return pltpu.make_async_copy(
-            tgt_hbm.at[s, part, first[part], second[part]], tgt_ref.at[s, part], tgt_sem.at[0])
+    def fetch_target(s):
+        return pltpu.make_async_copy(tgt_hbm.at[s, home], tgt_ref.at[s], tgt_sem.at[0])
 
     fetch(0).start()
     for copy in weights:
@@ -91,8 +118,7 @@
     for s in range(1, STREAMS):
         fetch(s).start()
     for s in range(STREAMS):
-        for part in range(2):
-            fetch_target(s, part).start()
+        fetch_target(s).start()
 
     def arrived(ref, sem):
         pltpu.make_async_copy(ref, ref, sem).wait()
@@ -108,30 +134,48 @@
             return 0
         lax.fori_loop(1, BRICKS, one, 0)
 
-    def along(axis, j):
-        at = (first[axis] + j) % RING
-        return at, (z * RING + at if axis == 0 else at * RING + y)
-
-    def hop(stage, s, part, j):
-        near, far = first[part], second[part]
-        at, who = along(part if stage in (0, 3) else 1 - part, j)
+    spans = (pl.ds(0, 8), pl.ds(8, 4), pl.ds(12, 3), pl.ds(12, 3), pl.ds(8, 4), pl.ds(0, 8))
+
+    def spots(p):
+        half = 8 * bits[p]
+        fourth = half + 4 * bits[(p + 1) % 4]
+        return half, fourth, fourth + 2 * bits[(p + 2) % 4] + bits[(p + 3) % 4]
+
+    def hops(stage, s, p):
+        half, fourth, mine = spots(p)
+        d = [(p + t) % 4 for t in range(4)]
+
+        def hop(src, dst, *dims):
+            return to_depth(src, dst, s_sem.at[stage], r_sem.at[stage, s], other(*dims))
+
         if stage == 0:
-            src, dst = p_ref.at[s, part, at], recv1_ref.at[s, part, j - 1]
-        elif stage == 1:
-            src, dst = acc_ref.at[s, part, at], recv2_ref.at[s, part, j - 1]
-        elif stage == 2:
-            src = dst = r_ref.at[s, part, near, far]
-        else:
-            src = dst = r_ref.at[s, part, near]
-        return to_depth(src, dst, s_sem.at[stage], r_sem.at[stage, s, part], who)
-
-    def send(stage, s, part):
-        for j in (2, 1, 3):
-            hop(stage, s, part, j).start()
-
-    def got_all(stage, s, part):
-        ref = recv1_ref if stage in (0, 3) else recv2_ref
-        arrived(ref.at[s, part], r_sem.at[stage, s, part])
+            return [hop(p_ref.at[s, p, pl.ds(8 - half, 8)], recv_ref.at[s, p, spans[0]], d[0])]
+        if stage == 1:
+            return [hop(acc_ref.at[s, p, pl.ds(4 - (fourth - half), 4)], recv_ref.at[s, p, spans[1]], d[1])]
+        if stage == 4:
+            ref = r_ref.at[s, p, pl.ds(fourth, 4)]
+            return [hop(ref, ref, d[1])]
+        if stage == 5:
+            ref = r_ref.at[s, p, pl.ds(half, 8)]
+            return [hop(ref, ref, d[0])]
+        out = []
+        for k in (3, 1, 2):
+            dims = [d[2]] * (k // 2) + [d[3]] * (k % 2)
+            if stage == 2:
+                there = [1 - bits[e] if e in dims else bits[e] for e in d[2:]]
+                out.append(hop(acc_ref.at[s, p, fourth - half + 2 * there[0] + there[1]],
+                               recv_ref.at[s, p, 11 + k], *dims))
+            else:
+                ref = r_ref.at[s, p, mine]
+                out.append(hop(ref, ref, *dims))
+        return out
+
+    def send(stage, s, p):
+        for copy in hops(stage, s, p):
+            copy.start()
+
+    def got_all(stage, s):
+        arrived(recv_ref.at[s, :, spans[stage]], r_sem.at[stage, s])
 
     sample = lax.broadcasted_iota(jnp.int32, (smp, hid), 0)
     pair = ray * 2
@@ -178,9 +222,11 @@
             weights[4].wait()
         high, low = halves(hbar_ref[s])
         value = mm(high, wout_ref[...], NN) + mm(low, wout_ref[...], NN)
-        p_ref[s] = value.reshape(2, RING, quarter, width)
-
-    def reduce_near(s):
+        for n in range(BRICKS):
+            for p in range(PARTS):
+                p_ref[s, p, place(p, n)] = value[n * rows:(n + 1) * rows, p * LANES:(p + 1) * LANES]
+
+    def reduce_half(s):
         if s % 2 == 0:
             arrived(t_all.at[s // 2, pl.ds(0, BRICKS - 1)], tr_sem.at[s // 2])
             before = jnp.zeros((1, pair), F32)
@@ -191,59 +237,72 @@
                 before = before + t_all[s // 2, b]
         row = lax.broadcasted_iota(jnp.int32, (smp, ray), 0)
         table = jnp.broadcast_to(e_all[s, me], (smp, ray))
-        for part in range(2):
-            for j in range(1, RING):
-                mine = e_all[s, along(part, RING - j)[1]]
-                table = jnp.where(row == part * RING + j, jnp.broadcast_to(mine, (smp, ray)), table)
-        ecol_ref[s] = table.T.reshape(2, RING, quarter, smp)
-        for part in range(2):
-            near = first[part]
-            e = ecol_ref[s, part, near]
-            got_all(0, s, part)
-            total = None
-            for j in range(RING):
-                got = p_ref[s, part, near] if j == 0 else recv1_ref[s, part, j - 1]
-                got = e[:, part * RING + j:part * RING + j + 1] * got
-                ps_ref[s, part, j] = got
-                total = got if j == 0 else total + got
-            acc_ref[s, part] = total.reshape(RING, quarter // RING, width)
-            send(1, s, part)
-
-    def reduce_far(s):
+        for d in range(4):
+            table = jnp.where(row == d + 1, jnp.broadcast_to(e_all[s, other(d)], (smp, ray)), table)
+        ecol_ref[s] = table.T.reshape(BRICKS, rows, smp)
+        got_all(0, s)
+        for p in range(PARTS):
+            half = spots(p)[0]
+            for i in range(8):
+                e = ecol_ref[s, block_at(p, half + i)]
+                acc_ref[s, p, i] = (e[:, :1] * p_ref[s, p, half + i]
+                                    + e[:, p + 1:p + 2] * recv_ref[s, p, i])
+            send(1, s, p)
+
+    def reduce_fourth(s):
+        got_all(1, s)
+        for p in range(PARTS):
+            half, fourth, _ = spots(p)
+            here = pl.ds(fourth - half, 4)
+            acc_ref[s, p, here] = acc_ref[s, p, here] + recv_ref[s, p, spans[1]]
+            send(2, s, p)
+
+    def reduce_block(s):
         if s == 0:
             arrived(tgt_ref, tgt_sem.at[0])
-        for part in range(2):
-            got_all(1, s, part)
-            total = acc_ref[s, part, second[part]] - tgt_ref[s, part]
-            for j in range(1, RING):
-                total = total + recv2_ref[s, part, j - 1]
-            r_ref[s, part, first[part], second[part]] = total
-            send(2, s, part)
-
-    def gather_far(s):
-        for part in range(2):
-            got_all(2, s, part)
-            send(3, s, part)
-        for part in range(2):
-            r = r_ref[s, part, first[part]].reshape(quarter, width)
-            for j in range(RING):
-                prod_ref[pl.ds((part * RING + j) * quarter, quarter)] = ps_ref[s, part, j] * r
-        high, low = halves(prod_ref[...])
-        ones = jnp.ones((smp, width), BF16)
-        own_all[s, me] = (mm(ones, high, NT) + mm(ones, low, NT))[:1]
+        got_all(2, s)
+        for p in range(PARTS):
+            half, _, mine = spots(p)
+            total = acc_ref[s, p, mine - half] - tgt_ref[s, :, p * LANES:(p + 1) * LANES]
+            for k in range(12, 15):
+                total = total + recv_ref[s, p, k]
+            r_ref[s, p, mine] = total
+            send(3, s, p)
+
+    def gather_fourth(s):
+        got_all(3, s)
+        for p in range(PARTS):
+            send(4, s, p)
+
+    def gather_half(s):
+        got_all(4, s)
+        for p in range(PARTS):
+            send(5, s, p)
+
+    def put_residual(s):
+        return pltpu.make_async_copy(res_ref.at[s], res_hbm.at[s], out_sem.at[0])
+
+    def own_terms(s):
+        got_all(5, s)
+        for n in range(BRICKS):
+            total = None
+            for p in range(PARTS):
+                at = place(p, n)
+                r = r_ref[s, p, at]
+                res_ref[s, n * rows:(n + 1) * rows, p * LANES:(p + 1) * LANES] = r
+                term = r * p_ref[s, p, at]
+                total = term if p == 0 else total + term
+            emt_ref[n * rows:(n + 1) * rows] = total
+        put_residual(s).start()
+        high, low = halves(emt_ref[...])
+        ones = jnp.ones((smp, LANES), BF16)
+        own = (mm(ones, high, NT) + mm(ones, low, NT))[:1] * e_all[s, me]
+        own_all[s, me] = own
         spread_start(own_all.at[s, me], os_sem.at[0], or_sem.at[s])
 
-    def put_residual(s):
-        return pltpu.make_async_copy(r_ref.at[s], res_hbm.at[s], out_sem.at[0])
-
-    def gather_near(s):
-        for part in range(2):
-            got_all(3, s, part)
-        put_residual(s).start()
-
     def emissions(s):
-        r_high, r_low = halves(r_ref[s].reshape(ray, width))
-        v_ref[...] = mm(r_high, wout_ref[...], NT) + mm(r_low, wout_ref[...], NT)
+        r_high, r_low = halves(res_ref[s])
+        v_ref[s] = mm(r_high, wout_ref[...], NT) + mm(r_low, wout_ref[...], NT)
         scaled = hbar_ref[s] * ecol_ref[s].reshape(ray, smp)[:, :1]
         b_high, b_low = halves(scaled)
         out = mm(b_high, r_high, TN) + mm(b_low, r_high, TN) + mm(b_high, r_low, TN)
@@ -255,7 +314,7 @@
 
         def tile(t, _):
             at = pl.ds(pl.multiple_of(t * 64, 64), 64)
-            v = v_ref[at]
+            v = v_ref[s, at]
             lane = lax.broadcasted_iota(jnp.int32, (64, smp), 1)
             found = jnp.zeros((64, smp), F32)
             for i in range(smp):
@@ -264,33 +323,17 @@
             wt_ref[at] = found
             return 0
         lax.fori_loop(0, ray // 64, tile, 0)
-        return wt_ref[...].T
-
-    def later_bricks(s):
+        keep_ref[s, 4] = wt_ref[...].T
+
+    def gradients(s):
         arrived(own_all.at[s, pl.ds(0, BRICKS - 1)], or_sem.at[s])
-        lane = lax.broadcasted_iota(jnp.int32, (1, part_rays), 1)
-        slot = lane // quarter
-        out = []
-        for part in range(2):
-            whole = jnp.zeros((1, part_rays), F32)
-            for near in range(RING):
-                total = jnp.zeros((1, part_rays), F32)
-                for far in range(RING):
-                    source = (near + RING * far, near * RING + far)[part]
-                    from_near = (near - slot + RING) % RING
-                    brick = (far * RING + from_near, from_near * RING + far)[part]
-                    term = own_all[s, source][:, part * part_rays:(part + 1) * part_rays]
-                    total = total + jnp.where(brick > me, term, 0.0)
-                total = total + pltpu.roll(total, quarter, 1)
-                total = total + pltpu.roll(total, 2 * quarter, 1)
-                whole = jnp.where(slot == near, total, whole)
-            out.append(whole)
-        return jnp.concatenate(out, 1)
-
-    def gradients(s, em):
+        after = jnp.zeros((1, ray), F32)
+        for b in range(1, BRICKS):
+            after = after + jnp.where(b > me, own_all[s, b], 0.0)
+        em = keep_ref[s, 4]
         e = jnp.broadcast_to(e_all[s, me], (smp, ray))
         wgt = keep_ref[s, 0] * e
-        later = running(wgt * em, True) + later_bricks(s)
+        later = running(wgt * em, True) + after
         dens = (keep_ref[s, 1] * e * em - later) * keep_ref[s, 3]
         dens_ref[:, pl.ds(s * ray, ray)] = dens
         dsig = dens / (1.0 + jnp.exp(-keep_ref[s, 2]))
@@ -300,7 +343,7 @@
 
         def tile(t, _):
             at = pl.ds(pl.multiple_of(t * 32, 32), 32)
-            v = v_ref[at]
+            v = v_ref[s, at]
             w = wt_ref[at]
             d = dt_ref[at]
             for i in range(smp):
@@ -356,14 +399,11 @@
         if s % 2 == 1:
             spread_start(t_all.at[s // 2, me], ts_sem.at[0], tr_sem.at[s // 2])
         weigh(s)
-        for part in range(2):
-            send(0, s, part)
+        for p in range(PARTS):
+            send(0, s, p)
     for step, s in ORDER:
-        (reduce_near, reduce_far, gather_far)[step](s)
-    for s in range(STREAMS):
-        gather_near(s)
-        em = emissions(s)
-        gradients(s, em)
+        (reduce_half, reduce_fourth, reduce_block, gather_fourth, gather_half,
+         own_terms, emissions, gradients)[step](s)
     lax.fori_loop(1, COLS, share_in, 0)
     dens_copy = pltpu.make_async_copy(dens_ref, dens_hbm, out_sem.at[1])
     dens_copy.start()
@@ -374,15 +414,13 @@
     gout_ref[...] = total
     gout_copy = pltpu.make_async_copy(gout_ref, gout_hbm, out_sem.at[2])
     gout_copy.start()
-    arrived(recv1_ref, s_sem.at[0])
-    arrived(recv2_ref, s_sem.at[1])
-    arrived(recv2_ref, s_sem.at[2])
-    arrived(recv1_ref, s_sem.at[3])
+    for stage in range(6):
+        arrived(recv_ref.at[:, :, spans[stage]], s_sem.at[stage])
     arrived(t_all.at[:, pl.ds(0, BRICKS - 1)], ts_sem.at[0])
     arrived(own_all.at[:, pl.ds(0, BRICKS - 1)], os_sem.at[0])
     pair_copy.wait_send()
     arrived(go_recv, gs_sem.at[1])
-    arrived(r_ref, out_sem.at[0])
+    arrived(res_ref, out_sem.at[0])
     dens_copy.wait()
     arrived(gi_recv, gr_sem.at[2])
     total = gi_ref[col]
@@ -426,12 +464,11 @@
     _, smp, nray, din = features.shape
     hid, width = w_out.shape[1:]
     ray = nray // STREAMS
-    quarter = ray // 2 // RING
-    piece = quarter // RING
+    rows = ray // BRICKS
     slab = din // COLS
     hbm = pl.BlockSpec(memory_space=pl.ANY)
     dma = pltpu.SemaphoreType.DMA
-    split = (STREAMS, 2, RING, RING, piece, width)
+    stage = (STREAMS, PARTS)
     scratch = [
         pltpu.VMEM((1, nray), jnp.int32),
         pltpu.VMEM((1, nray), F32),
@@ -445,20 +482,19 @@
         pltpu.VMEM((STREAMS, smp, ray, hid), BF16),
         pltpu.VMEM((ray, smp), F32),
         pltpu.VMEM((STREAMS, ray, hid), F32),
-        pltpu.VMEM((STREAMS, 2, RING, quarter, width), F32),
-        pltpu.VMEM((STREAMS, 2, RING, quarter, width), F32),
-        pltpu.VMEM((STREAMS, 2, RING, piece, width), F32),
-        pltpu.VMEM((STREAMS, 2, RING - 1, quarter, width), F32),
-        pltpu.VMEM((STREAMS, 2, RING - 1, piece, width), F32),
-        pltpu.VMEM(split, F32),
-        pltpu.VMEM((ray, width), F32),
-        pltpu.VMEM((STREAMS, 2, piece, width), F32),
+        pltpu.VMEM((*stage, BRICKS, rows, LANES), F32),
+        pltpu.VMEM((*stage, BRICKS // 2, rows, LANES), F32),
+        pltpu.VMEM((*stage, BRICKS - 1, rows, LANES), F32),
+        pltpu.VMEM((*stage, BRICKS, rows, LANES), F32),
+        pltpu.VMEM((STREAMS, ray, width), F32),
+        pltpu.VMEM((ray, LANES), F32),
+        pltpu.VMEM((STREAMS, rows, width), F32),
         pltpu.VMEM((STREAMS // 2, BRICKS, 1, 2 * ray), F32),
         pltpu.VMEM((STREAMS, BRICKS, 1, ray), F32),
         pltpu.VMEM((STREAMS, BRICKS, 1, ray), F32),
-        pltpu.VMEM((STREAMS, 2, RING, quarter, smp), F32),
-        pltpu.VMEM((STREAMS, 4, smp, ray), F32),
-        pltpu.VMEM((ray, hid), F32),
+        pltpu.VMEM((STREAMS, BRICKS, rows, smp), F32),
+        pltpu.VMEM((STREAMS, 5, smp, ray), F32),
+        pltpu.VMEM((STREAMS, ray, hid), F32),
         pltpu.VMEM((ray, smp), F32),
         pltpu.VMEM((ray, smp), F32),
         pltpu.VMEM((smp, ray, hid), BF16),
@@ -469,14 +505,14 @@
         pltpu.VMEM((RING, slab, width), F32),
         pltpu.VMEM((RING - 1, slab, width), F32),
         dma((5,)), dma((STREAMS,)), dma((1,)), dma((4,)),
-        dma((4,)), dma((4, STREAMS, 2)),
+        dma((6,)), dma((6, STREAMS)),
         dma((1,)), dma((STREAMS // 2,)), dma((1,)), dma((STREAMS,)),
         dma((3,)), dma((3,)),
     ]
     residual, dens, g_in, g_out = pl.pallas_call(
         body,
         out_shape=(
-            jax.ShapeDtypeStruct(split, F32),
+            jax.ShapeDtypeStruct((STREAMS, ray, width), F32),
             jax.ShapeDtypeStruct((smp, nray), F32),
             jax.ShapeDtypeStruct((slab + smp, hid), F32),
             jax.ShapeDtypeStruct((slab, width), F32),
@@ -487,7 +523,7 @@
         compiler_params=pltpu.CompilerParams(
             collective_id=0, has_side_effects=True, vmem_limit_bytes=60 * 1024 * 1024),
         name="brick_step",
-    )(features[0], counts, steps, target.reshape(split), w_in[0], w_density, w_out[0])
+    )(features[0], counts, steps, target.reshape(STREAMS, BRICKS, rows, width), w_in[0], w_density, w_out[0])
     residual, dens, g_in, g_den, g_out = pl.pallas_call(
         finish,
         out_shape=(
@@ -508,7 +544,7 @@
             dma((3 + STREAMS,)), dma((4 + STREAMS,)),
         ],
         name="brick_finish",
-    )(residual.reshape(STREAMS, ray, width), dens, g_in, g_out)
+    )(residual, dens, g_in, g_out)
     return residual.reshape(nray, width), dens[None], g_in[None], g_den, g_out[None]
 
 

time: 63 us -> 69.2 us (1.098)
  Pallas kernels: 62.3 us -> 68.4 us
    pallas_call x1, Pallas kernels: 59.5 us -> 65.7 us  [per_device(): pl.pallas_call(body, out_shape=(jax.ShapeDtypeStruct((STREAMS, ray, width...]
where the time goes in v5:
time: 69.2 us; the launch traced here: 69.1 us
  Pallas kernels  68.4 us (99%)
    pallas_call x1, Pallas kernels, per_device(): pl.pallas_call(body, out_shape=(jax.ShapeDtypeStruct((STREAMS, ray, width...  65.7 us
    pallas_call x1, Pallas kernels, per_device(): pl.pallas_call(finish, out_shape=(jax.ShapeDtypeStruct((STREAMS, ray, wid...  2.79 us

profile of v5, /device:TPU:1, one launch (start us, length us, event | category | flops | bytes accessed | tf_op | source)
XLA Modules:
  0.0 69.1 jit_solution(17472552270784303794)
XLA Ops:
  0.6 65.7 %brick_step.1 = (f32[4,256,512]{2,1,0:T(8,128)}, f32[8,1024]{1,0:T(8,128)}, f32[40,256]{1,0:T(8,128)}, f32[32,512]{1,0:T(8,128)}) custom-call(bf16[8,1024,256]{2,1,0:T(8,128)(2,1)} %bitcast.8, s32[1,1024]{1,0:T(1,128)} %cnt_hbm.1, f32[1,1024]{1,0:T(1,128)} %step_hbm.1, f32[4,16,16,512]{3,2,1,0:T(8,128)} %bitcast.9, bf16[256,256]{1,0:T(8,128)(2,1)} %bitcast.11, ...), custom_call_target="tpu_custom_call" | custom-call | tf_op jit(solution)/shard_map/brick_step/pallas_call | solution.py:512
  66.3 2.8 %brick_finish.1 = (f32[4,256,512]{2,1,0:T(8,128)}, f32[8,1024]{1,0:T(8,128)}, f32[32,256]{1,0:T(8,128)}, f32[1,32]{1,0:T(1,128)}, f32[32,512]{1,0:T(8,128)}) custom-call(f32[4,256,512]{2,1,0:T(8,128)} %get-tuple-element.14.res_in, f32[8,1024]{1,0:T(8,128)} %get-tuple-element.15.dens_in, f32[40,256]{1,0:T(8,128)} %get-tuple-element.16.gin_in, ...), custom_call_target="tpu_custom_call" | custom-call | tf_op jit(solution)/shard_map/brick_finish/pallas_call | solution.py:527

commit v6 on v4

--- a/solution.py
+++ b/solution.py
@@ -11,7 +11,9 @@
 RING = 4
 BRICKS = 16
 COLS = 8
-ORDER = ((0, 0), (0, 1), (0, 2), (1, 0), (0, 3), (1, 1), (1, 2), (2, 0), (1, 3), (2, 1), (2, 2), (2, 3))
+LANES = 128
+ORDER = ((0, 0), (0, 1), (1, 0), (0, 2), (1, 1), (0, 3), (2, 0), (1, 2), (2, 1), (1, 3), (2, 2),
+         (3, 0), (4, 0), (2, 3), (3, 1), (4, 1), (3, 2), (4, 2), (3, 3), (4, 3))
 F32 = jnp.float32
 BF16 = jnp.bfloat16
 NT = (((1,), (1,)), ((), ()))
@@ -43,12 +45,12 @@
 
 def body(f_hbm, cnt_hbm, step_hbm, tgt_hbm, win_hbm, wden_hbm, wout_hbm,
          res_hbm, dens_hbm, gin_hbm, gout_hbm,
-         cnt_ref, step_ref, win_ref, wden_ref, wout_ref, dens_ref, gin_ref, gout_ref, f_ref, hid_ref, lwt_ref, hbar_ref, p_ref, ps_ref, acc_ref, recv1_ref, recv2_ref, r_ref, prod_ref, tgt_ref,
-         t_all, e_all, own_all, ecol_ref, keep_ref, v_ref, wt_ref, dt_ref, dpre_ref,
+         cnt_ref, step_ref, win_ref, wden_ref, wout_ref, dens_ref, gin_ref, gout_ref, wint_ref, wcol_ref, f_ref, hid_ref, hbar_ref, p_ref, ps_ref, acc_ref, recv1_ref, recv2_ref, r_ref, prod_ref, tgt_ref,
+         t_all, e_all, own_all, ecol_ref, keep_ref, v_ref, dpre_ref, gt_ref, gd_ref,
          gi_ref, go_ref, gi_recv, go_pair, go_sum, go_recv,
          in_sem, f_sem, tgt_sem, out_sem, s_sem, r_sem, ts_sem, tr_sem, os_sem, or_sem, gs_sem, gr_sem):
     smp, ray = f_ref.shape[1], f_ref.shape[2]
-    hid, width = win_ref.shape[1], wout_ref.shape[1]
+    hid, width = wout_ref.shape
     part_rays = ray // 2
     quarter = part_rays // RING
     slab = gout_ref.shape[0]
@@ -141,13 +143,15 @@
         if s == 0:
             for copy in weights[:4]:
                 copy.wait()
+            wint_ref[...] = win_ref[...].astype(F32).T.astype(BF16)
+            wcol_ref[...] = jnp.broadcast_to(wden_ref[...].astype(F32), (LANES, hid)).T
         wden = jnp.broadcast_to(wden_ref[...].astype(F32), (smp, hid))
         sig = jnp.zeros((smp, ray), F32)
         for i in range(smp):
-            pre = mm(f_ref[s, i], win_ref[...], NN)
+            pre = mm(wint_ref[...], f_ref[s, i], NT)
             h = jnp.maximum(pre, 0.0).astype(BF16)
             hid_ref[s, i] = h
-            sig = sig + mm(jnp.where(sample == i, wden, 0.0).astype(BF16), h, NT)
+            sig = sig + mm(jnp.where(sample == i, wden, 0.0).astype(BF16), h, NN)
         here = pl.ds(s * ray, ray)
         row = lax.broadcasted_iota(jnp.int32, (smp, ray), 0)
         gate = jnp.where(row < cnt_ref[:, here], jnp.broadcast_to(step_ref[:, here], (smp, ray)), 0.0)
@@ -162,22 +166,19 @@
         keep_ref[s, 1] = light * keep
         keep_ref[s, 2] = sig
         keep_ref[s, 3] = gate
-        lwt_ref[...] = lw.T
 
     def weigh(s):
-        def tile(t, _):
-            at = pl.ds(pl.multiple_of(t * 64, 64), 64)
-            w = lwt_ref[at]
-            total = jnp.zeros((64, hid), F32)
+        lw = keep_ref[s, 0]
+        for t in range(0, hid, 32):
+            total = None
             for i in range(smp):
-                total = total + w[:, i:i + 1] * hid_ref[s, i, at].astype(F32)
-            hbar_ref[s, at] = total
-            return 0
-        lax.fori_loop(0, ray // 64, tile, 0)
+                term = lw[i:i + 1] * hid_ref[s, i, t:t + 32].astype(F32)
+                total = term if i == 0 else total + term
+            hbar_ref[s, t:t + 32] = total
         if s == 0:
             weights[4].wait()
         high, low = halves(hbar_ref[s])
-        value = mm(high, wout_ref[...], NN) + mm(low, wout_ref[...], NN)
+        value = mm(high, wout_ref[...], TN) + mm(low, wout_ref[...], TN)
         p_ref[s] = value.reshape(2, RING, quarter, width)
 
     def reduce_near(s):
@@ -242,29 +243,26 @@
         put_residual(s).start()
 
     def emissions(s):
+        gather_near(s)
         r_high, r_low = halves(r_ref[s].reshape(ray, width))
-        v_ref[...] = mm(r_high, wout_ref[...], NT) + mm(r_low, wout_ref[...], NT)
-        scaled = hbar_ref[s] * ecol_ref[s].reshape(ray, smp)[:, :1]
-        b_high, b_low = halves(scaled)
-        out = mm(b_high, r_high, TN) + mm(b_low, r_high, TN) + mm(b_high, r_low, TN)
+        v_ref[s] = mm(wout_ref[...], r_high, NT) + mm(wout_ref[...], r_low, NT)
+        b_high, b_low = halves(hbar_ref[s] * e_all[s, me])
+        out = mm(b_high, r_high, NN) + mm(b_low, r_high, NN) + mm(b_high, r_low, NN)
         for c in range(COLS):
             mine = out[c * slab:(c + 1) * slab]
             go_ref[c % 2, c // 2] = mine if s == 0 else go_ref[c % 2, c // 2] + mine
         if s == STREAMS - 1:
             pair_copy.start()
 
-        def tile(t, _):
-            at = pl.ds(pl.multiple_of(t * 64, 64), 64)
-            v = v_ref[at]
-            lane = lax.broadcasted_iota(jnp.int32, (64, smp), 1)
-            found = jnp.zeros((64, smp), F32)
+        row = lax.broadcasted_iota(jnp.int32, (smp, LANES), 0)
+        for at in range(0, ray, LANES):
+            here = slice(at, at + LANES)
+            v = v_ref[s, :, here]
+            em = jnp.zeros((smp, LANES), F32)
             for i in range(smp):
-                e = jnp.sum(v * hid_ref[s, i, at].astype(F32), 1, keepdims=True)
-                found = jnp.where(lane == i, e, found)
-            wt_ref[at] = found
-            return 0
-        lax.fori_loop(0, ray // 64, tile, 0)
-        return wt_ref[...].T
+                e = jnp.sum(v * hid_ref[s, i, :, here].astype(F32), 0, keepdims=True)
+                em = jnp.where(row == i, e, em)
+            keep_ref[s, 4, :, here] = em
 
     def later_bricks(s):
         arrived(own_all.at[s, pl.ds(0, BRICKS - 1)], or_sem.at[s])
@@ -287,46 +285,42 @@
             out.append(whole)
         return jnp.concatenate(out, 1)
 
-    def gradients(s, em):
+    def gradients(s):
         e = jnp.broadcast_to(e_all[s, me], (smp, ray))
+        em = keep_ref[s, 4]
         wgt = keep_ref[s, 0] * e
         later = running(wgt * em, True) + later_bricks(s)
         dens = (keep_ref[s, 1] * e * em - later) * keep_ref[s, 3]
         dens_ref[:, pl.ds(s * ray, ray)] = dens
         dsig = dens / (1.0 + jnp.exp(-keep_ref[s, 2]))
-        wt_ref[...] = wgt.T
-        dt_ref[...] = dsig.T
-        wden_row = wden_ref[...].astype(F32)
-
-        def tile(t, _):
-            at = pl.ds(pl.multiple_of(t * 32, 32), 32)
-            v = v_ref[at]
-            w = wt_ref[at]
-            d = dt_ref[at]
-            for i in range(smp):
-                dh = w[:, i:i + 1] * v + d[:, i:i + 1] * wden_row
-                h = hid_ref[s, i, at].astype(F32)
-                dpre_ref[i, at] = jnp.where(h > 0.0, dh, 0.0).astype(BF16)
-            return 0
-        lax.fori_loop(0, ray // 32, tile, 0)
+        for at in range(0, ray, LANES):
+            here = slice(at, at + LANES)
+            for t in range(0, hid, 64):
+                down = slice(t, t + 64)
+                v = v_ref[s, down, here]
+                wden = wcol_ref[down]
+                for i in range(smp):
+                    dh = wgt[i:i + 1, here] * v + dsig[i:i + 1, here] * wden
+                    dpre_ref[down, i * ray + at:i * ray + at + LANES] = jnp.where(
+                        hid_ref[s, i, down, here] > 0, dh.astype(BF16), jnp.zeros((), BF16))
         if s == STREAMS - 1:
             share_out()
-        g_in = mm(f_ref[s].reshape(smp * ray, -1), dpre_ref[...].reshape(smp * ray, hid), TN)
+        g_in = mm(dpre_ref[...], f_ref[s].reshape(smp * ray, -1), NN)
+        gt_ref[...] = g_in if s == 0 else gt_ref[...] + g_in
         d_high, d_low = halves(dsig)
         stacked = jnp.concatenate([d_high.astype(F32), d_low.astype(F32)], 0)
         row = lax.broadcasted_iota(jnp.int32, stacked.shape, 0)
-        g_den = jnp.zeros((2 * smp, hid), F32)
+        g_den = jnp.zeros((hid, 2 * smp), F32)
         for i in range(smp):
-            g_den = g_den + mm(jnp.where(row % smp == i, stacked, 0.0).astype(BF16), hid_ref[s, i], NN)
-        g_den = g_den[:smp] + g_den[smp:]
-        for c in range(COLS):
-            mine = g_in[c * slab:(c + 1) * slab]
-            if s == 0:
-                gi_ref[c, :slab] = mine
-                gi_ref[c, slab:] = g_den
-            else:
-                gi_ref[c, :slab] = gi_ref[c, :slab] + mine
-                gi_ref[c, slab:] = gi_ref[c, slab:] + g_den
+            g_den = g_den + mm(hid_ref[s, i], jnp.where(row % smp == i, stacked, 0.0).astype(BF16), NT)
+        gd_ref[...] = g_den if s == 0 else gd_ref[...] + g_den
+        if s == STREAMS - 1:
+            turned = gt_ref[...].T
+            den = gd_ref[...].T
+            den = den[:smp] + den[smp:]
+            for c in range(COLS):
+                gi_ref[c, :slab] = turned[c * slab:(c + 1) * slab]
+                gi_ref[c, slab:] = den
 
     x, core = col // 2, col % 2
 
@@ -359,11 +353,7 @@
         for part in range(2):
             send(0, s, part)
     for step, s in ORDER:
-        (reduce_near, reduce_far, gather_far)[step](s)
-    for s in range(STREAMS):
-        gather_near(s)
-        em = emissions(s)
-        gradients(s, em)
+        (reduce_near, reduce_far, gather_far, emissions, gradients)[step](s)
     lax.fori_loop(1, COLS, share_in, 0)
     dens_copy = pltpu.make_async_copy(dens_ref, dens_hbm, out_sem.at[1])
     dens_copy.start()
@@ -441,10 +431,11 @@
         pltpu.VMEM((smp, nray), F32),
         pltpu.VMEM((slab + smp, hid), F32),
         pltpu.VMEM((slab, width), F32),
+        pltpu.VMEM((hid, din), BF16),
+        pltpu.VMEM((hid, LANES), F32),
         pltpu.VMEM((STREAMS, smp, ray, din), BF16),
-        pltpu.VMEM((STREAMS, smp, ray, hid), BF16),
-        pltpu.VMEM((ray, smp), F32),
-        pltpu.VMEM((STREAMS, ray, hid), F32),
+        pltpu.VMEM((STREAMS, smp, hid, ray), BF16),
+        pltpu.VMEM((STREAMS, hid, ray), F32),
         pltpu.VMEM((STREAMS, 2, RING, quarter, width), F32),
         pltpu.VMEM((STREAMS, 2, RING, quarter, width), F32),
         pltpu.VMEM((STREAMS, 2, RING, piece, width), F32),
@@ -457,11 +448,11 @@
         pltpu.VMEM((STREAMS, BRICKS, 1, ray), F32),
         pltpu.VMEM((STREAMS, BRICKS, 1, ray), F32),
         pltpu.VMEM((STREAMS, 2, RING, quarter, smp), F32),
-        pltpu.VMEM((STREAMS, 4, smp, ray), F32),
-        pltpu.VMEM((ray, hid), F32),
-        pltpu.VMEM((ray, smp), F32),
-        pltpu.VMEM((ray, smp), F32),
-        pltpu.VMEM((smp, ray, hid), BF16),
+        pltpu.VMEM((STREAMS, 5, smp, ray), F32),
+        pltpu.VMEM((STREAMS, hid, ray), F32),
+        pltpu.VMEM((hid, smp * ray), BF16),
+        pltpu.VMEM((hid, din), F32),
+        pltpu.VMEM((hid, 2 * smp), F32),
         pltpu.VMEM((COLS, slab + smp, hid), F32),
         pltpu.VMEM((2, RING, slab, width), F32),
         pltpu.VMEM((COLS - 1, slab + smp, hid), F32),

time: 63 us -> 59.3 us (0.941)
  Pallas kernels: 62.3 us -> 58.5 us
    pallas_call x1, Pallas kernels: 59.5 us -> 55.7 us  [per_device(): pl.pallas_call(body, out_shape=(jax.ShapeDtypeStruct(split, F32), jax.Sha...]
where the time goes in v6:
time: 59.3 us; the launch traced here: 59.1 us
  Pallas kernels  58.5 us (99%)
  between operations  0.64 us (1%)
    pallas_call x1, Pallas kernels, per_device(): pl.pallas_call(body, out_shape=(jax.ShapeDtypeStruct(split, F32), jax.Sha...  55.7 us
    pallas_call x1, Pallas kernels, per_device(): pl.pallas_call(finish, out_shape=(jax.ShapeDtypeStruct((STREAMS, ray, wid...  2.79 us

profile of v6, /device:TPU:1, one launch (start us, length us, event | category | flops | bytes accessed | tf_op | source)
XLA Modules:
  0.0 59.1 jit_solution(10839806666900540430)
XLA Ops:
  0.6 55.7 %brick_step.1 = (f32[4,2,4,4,8,512]{5,4,3,2,1,0:T(8,128)}, f32[8,1024]{1,0:T(8,128)}, f32[40,256]{1,0:T(8,128)}, f32[32,512]{1,0:T(8,128)}) custom-call(bf16[8,1024,256]{2,1,0:T(8,128)(2,1)} %bitcast.9, s32[1,1024]{1,0:T(1,128)} %cnt_hbm.1, f32[1,1024]{1,0:T(1,128)} %step_hbm.1, f32[4,2,4,4,8,512]{5,4,3,2,1,0:T(8,128)} %bitcast.11, ...), custom_call_target="tpu_custom_call" | custom-call | tf_op jit(solution)/shard_map/brick_step/pallas_call | solution.py:467
  56.3 2.8 %brick_finish.1 = (f32[4,256,512]{2,1,0:T(8,128)}, f32[8,1024]{1,0:T(8,128)}, f32[32,256]{1,0:T(8,128)}, f32[1,32]{1,0:T(1,128)}, f32[32,512]{1,0:T(8,128)}) custom-call(f32[4,256,512]{2,1,0:T(8,128)} %bitcast.10, f32[8,1024]{1,0:T(8,128)} %get-tuple-element.15.dens_in, f32[40,256]{1,0:T(8,128)} %get-tuple-element.16.gin_in, f32[32,512]{1,0:T(8,128)} %get-tuple-element.17.gout_in), custom_call_target="tpu_custom_call" | custom-call | tf_op jit(solution)/shard_map/brick_finish/pallas_call | solution.py:482

commit v7 on v6

--- a/solution.py
+++ b/solution.py
@@ -12,8 +12,8 @@
 BRICKS = 16
 COLS = 8
 LANES = 128
-ORDER = ((0, 0), (0, 1), (1, 0), (0, 2), (1, 1), (0, 3), (2, 0), (1, 2), (2, 1), (1, 3), (2, 2),
-         (3, 0), (4, 0), (2, 3), (3, 1), (4, 1), (3, 2), (4, 2), (3, 3), (4, 3))
+ORDER = ((0, 0), (0, 1), (0, 2), (0, 3), (1, 0), (1, 1), (1, 2), (1, 3), (2, 0), (2, 1), (2, 2), (2, 3),
+         (3, 0), (4, 0), (3, 1), (4, 1), (3, 2), (4, 2), (3, 3), (4, 3))
 F32 = jnp.float32
 BF16 = jnp.bfloat16
 NT = (((1,), (1,)), ((), ()))
@@ -52,12 +52,32 @@
     smp, ray = f_ref.shape[1], f_ref.shape[2]
     hid, width = wout_ref.shape
     part_rays = ray // 2
-    quarter = part_rays // RING
+    half_rays = part_rays // 2
+    half_width = width // 2
+    parts = [(rp, cp) for rp in range(2) for cp in range(2)]
     slab = gout_ref.shape[0]
     me = lax.axis_index("depth")
     col = lax.axis_index("col")
     y, z = me % RING, me // RING
-    first, second = (y, z), (z, y)
+    bits = ((y // 2 + y % 2) % 2, y // 2, (z // 2 + z % 2) % 2, z // 2)
+
+    def moved(at, low, high):
+        if low and high:
+            return (at + 2) % RING
+        return RING - 1 - at if high else at + 1 - 2 * (at % 2) if low else at
+
+    def other(*dims):
+        return (moved(z, 2 in dims, 3 in dims) * RING
+                + moved(y, 0 in dims, 1 in dims))
+
+    def spot(rp, cp, flipped=()):
+        d = 2 * rp + cp
+        block = 0
+        for e in range(4):
+            if e != d:
+                block = block * 2 + (1 - bits[e] if e in flipped else bits[e])
+        return d, bits[d], block
+
     mesh_id = pl.DeviceIdType.MESH
 
     barrier = pltpu.get_barrier_semaphore()
@@ -83,9 +103,11 @@
     def fetch(s):
         return pltpu.make_async_copy(f_hbm.at[:, pl.ds(s * ray, ray)], f_ref.at[s], f_sem.at[s])
 
-    def fetch_target(s, part):
+    def fetch_target(s, rp, cp):
+        _, half, block = spot(rp, cp)
         return pltpu.make_async_copy(
-            tgt_hbm.at[s, part, first[part], second[part]], tgt_ref.at[s, part], tgt_sem.at[0])
+            tgt_hbm.at[s, rp, half, block, :, pl.ds(cp * half_width, half_width)],
+            tgt_ref.at[s, rp, cp], tgt_sem.at[0])
 
     fetch(0).start()
     for copy in weights:
@@ -93,8 +115,8 @@
     for s in range(1, STREAMS):
         fetch(s).start()
     for s in range(STREAMS):
-        for part in range(2):
-            fetch_target(s, part).start()
+        for rp, cp in parts:
+            fetch_target(s, rp, cp).start()
 
     def arrived(ref, sem):
         pltpu.make_async_copy(ref, ref, sem).wait()
@@ -110,30 +132,36 @@
             return 0
         lax.fori_loop(1, BRICKS, one, 0)
 
-    def along(axis, j):
-        at = (first[axis] + j) % RING
-        return at, (z * RING + at if axis == 0 else at * RING + y)
-
-    def hop(stage, s, part, j):
-        near, far = first[part], second[part]
-        at, who = along(part if stage in (0, 3) else 1 - part, j)
+    def hops(stage, s, rp, cp):
+        d, half, block = spot(rp, cp)
+
+        def hop(src, dst, *dims):
+            return to_depth(src, dst, s_sem.at[stage], r_sem.at[stage, s], other(*dims))
+
         if stage == 0:
-            src, dst = p_ref.at[s, part, at], recv1_ref.at[s, part, j - 1]
-        elif stage == 1:
-            src, dst = acc_ref.at[s, part, at], recv2_ref.at[s, part, j - 1]
-        elif stage == 2:
-            src = dst = r_ref.at[s, part, near, far]
-        else:
-            src = dst = r_ref.at[s, part, near]
-        return to_depth(src, dst, s_sem.at[stage], r_sem.at[stage, s, part], who)
-
-    def send(stage, s, part):
-        for j in (2, 1, 3):
-            hop(stage, s, part, j).start()
-
-    def got_all(stage, s, part):
+            return [hop(p_ref.at[s, cp, rp, 1 - half], recv1_ref.at[s, rp, cp], d)]
+        if stage == 3:
+            ref = r_ref.at[s, cp, rp, half]
+            return [hop(ref, ref, d)]
+        out = []
+        rest = [e for e in range(4) if e != d]
+        for k in (7, 6, 5, 3, 4, 2, 1):
+            dims = [e for i, e in enumerate(rest) if k // 2 ** i % 2]
+            if stage == 1:
+                out.append(hop(acc_ref.at[s, rp, cp, spot(rp, cp, dims)[2]],
+                               recv2_ref.at[s, rp, cp, k - 1], *dims))
+            else:
+                ref = r_ref.at[s, cp, rp, half, block]
+                out.append(hop(ref, ref, *dims))
+        return out
+
+    def send(stage, s, rp, cp):
+        for copy in hops(stage, s, rp, cp):
+            copy.start()
+
+    def got_all(stage, s):
         ref = recv1_ref if stage in (0, 3) else recv2_ref
-        arrived(ref.at[s, part], r_sem.at[stage, s, part])
+        arrived(ref.at[s], r_sem.at[stage, s])
 
     sample = lax.broadcasted_iota(jnp.int32, (smp, hid), 0)
     pair = ray * 2
@@ -179,7 +207,8 @@
             weights[4].wait()
         high, low = halves(hbar_ref[s])
         value = mm(high, wout_ref[...], TN) + mm(low, wout_ref[...], TN)
-        p_ref[s] = value.reshape(2, RING, quarter, width)
+        for cp in range(2):
+            p_ref[s, cp] = value[:, cp * half_width:(cp + 1) * half_width].reshape(p_ref.shape[2:])
 
     def reduce_near(s):
         if s % 2 == 0:
@@ -192,62 +221,67 @@
                 before = before + t_all[s // 2, b]
         row = lax.broadcasted_iota(jnp.int32, (smp, ray), 0)
         table = jnp.broadcast_to(e_all[s, me], (smp, ray))
-        for part in range(2):
-            for j in range(1, RING):
-                mine = e_all[s, along(part, RING - j)[1]]
-                table = jnp.where(row == part * RING + j, jnp.broadcast_to(mine, (smp, ray)), table)
-        ecol_ref[s] = table.T.reshape(2, RING, quarter, smp)
-        for part in range(2):
-            near = first[part]
-            e = ecol_ref[s, part, near]
-            got_all(0, s, part)
-            total = None
-            for j in range(RING):
-                got = p_ref[s, part, near] if j == 0 else recv1_ref[s, part, j - 1]
-                got = e[:, part * RING + j:part * RING + j + 1] * got
-                ps_ref[s, part, j] = got
-                total = got if j == 0 else total + got
-            acc_ref[s, part] = total.reshape(RING, quarter // RING, width)
-            send(1, s, part)
+        for d in range(4):
+            table = jnp.where(row == d + 1, jnp.broadcast_to(e_all[s, other(d)], (smp, ray)), table)
+        ecol_ref[s] = table.T.reshape(2, 2, half_rays, smp)
+        got_all(0, s)
+        for rp, cp in parts:
+            d, half, _ = spot(rp, cp)
+            e = ecol_ref[s, rp, half]
+            own = e[:, :1] * p_ref[s, cp, rp, half].reshape(half_rays, half_width)
+            got = e[:, d + 1:d + 2] * recv1_ref[s, rp, cp].reshape(half_rays, half_width)
+            ps_ref[s, rp, cp, 0] = own
+            ps_ref[s, rp, cp, 1] = got
+            acc_ref[s, rp, cp] = (own + got).reshape(acc_ref.shape[3:])
+            send(1, s, rp, cp)
 
     def reduce_far(s):
         if s == 0:
             arrived(tgt_ref, tgt_sem.at[0])
-        for part in range(2):
-            got_all(1, s, part)
-            total = acc_ref[s, part, second[part]] - tgt_ref[s, part]
-            for j in range(1, RING):
-                total = total + recv2_ref[s, part, j - 1]
-            r_ref[s, part, first[part], second[part]] = total
-            send(2, s, part)
+        got_all(1, s)
+        for rp, cp in parts:
+            _, half, block = spot(rp, cp)
+            total = acc_ref[s, rp, cp, block] - tgt_ref[s, rp, cp]
+            for k in range(7):
+                total = total + recv2_ref[s, rp, cp, k]
+            r_ref[s, cp, rp, half, block] = total
+            send(2, s, rp, cp)
 
     def gather_far(s):
-        for part in range(2):
-            got_all(2, s, part)
-            send(3, s, part)
-        for part in range(2):
-            r = r_ref[s, part, first[part]].reshape(quarter, width)
-            for j in range(RING):
-                prod_ref[pl.ds((part * RING + j) * quarter, quarter)] = ps_ref[s, part, j] * r
+        got_all(2, s)
+        for rp, cp in parts:
+            send(3, s, rp, cp)
+        for i, (rp, cp) in enumerate(parts):
+            r = r_ref[s, cp, rp, spot(rp, cp)[1]].reshape(half_rays, half_width)
+            for j in range(2):
+                prod_ref[pl.ds((2 * i + j) * half_rays, half_rays)] = ps_ref[s, rp, cp, j] * r
         high, low = halves(prod_ref[...])
-        ones = jnp.ones((smp, width), BF16)
+        ones = jnp.ones((smp, half_width), BF16)
         own_all[s, me] = (mm(ones, high, NT) + mm(ones, low, NT))[:1]
         spread_start(own_all.at[s, me], os_sem.at[0], or_sem.at[s])
 
-    def put_residual(s):
-        return pltpu.make_async_copy(r_ref.at[s], res_hbm.at[s], out_sem.at[0])
+    def put_residual(s, cp):
+        return pltpu.make_async_copy(
+            r_ref.at[s, cp], res_hbm.at[s, :, :, :, :, pl.ds(cp * half_width, half_width)], out_sem.at[0])
 
     def gather_near(s):
-        for part in range(2):
-            got_all(3, s, part)
-        put_residual(s).start()
+        got_all(3, s)
+        for cp in range(2):
+            put_residual(s, cp).start()
 
     def emissions(s):
         gather_near(s)
-        r_high, r_low = halves(r_ref[s].reshape(ray, width))
-        v_ref[s] = mm(wout_ref[...], r_high, NT) + mm(wout_ref[...], r_low, NT)
         b_high, b_low = halves(hbar_ref[s] * e_all[s, me])
-        out = mm(b_high, r_high, NN) + mm(b_low, r_high, NN) + mm(b_high, r_low, NN)
+        v = None
+        out = []
+        for cp in range(2):
+            r_high, r_low = halves(r_ref[s, cp].reshape(ray, half_width))
+            w = wout_ref[:, cp * half_width:(cp + 1) * half_width]
+            term = mm(w, r_high, NT) + mm(w, r_low, NT)
+            v = term if cp == 0 else v + term
+            out.append(mm(b_high, r_high, NN) + mm(b_low, r_high, NN) + mm(b_high, r_low, NN))
+        v_ref[s] = v
+        out = jnp.concatenate(out, 1)
         for c in range(COLS):
             mine = out[c * slab:(c + 1) * slab]
             go_ref[c % 2, c // 2] = mine if s == 0 else go_ref[c % 2, c // 2] + mine
@@ -266,22 +300,24 @@
 
     def later_bricks(s):
         arrived(own_all.at[s, pl.ds(0, BRICKS - 1)], or_sem.at[s])
-        lane = lax.broadcasted_iota(jnp.int32, (1, part_rays), 1)
-        slot = lane // quarter
+        side = lax.broadcasted_iota(jnp.int32, (1, part_rays), 1) // half_rays
         out = []
-        for part in range(2):
+        for rp in range(2):
             whole = jnp.zeros((1, part_rays), F32)
-            for near in range(RING):
-                total = jnp.zeros((1, part_rays), F32)
-                for far in range(RING):
-                    source = (near + RING * far, near * RING + far)[part]
-                    from_near = (near - slot + RING) % RING
-                    brick = (far * RING + from_near, from_near * RING + far)[part]
-                    term = own_all[s, source][:, part * part_rays:(part + 1) * part_rays]
-                    total = total + jnp.where(brick > me, term, 0.0)
-                total = total + pltpu.roll(total, quarter, 1)
-                total = total + pltpu.roll(total, 2 * quarter, 1)
-                whole = jnp.where(slot == near, total, whole)
+            for cp in range(2):
+                d = 2 * rp + cp
+                totals = [jnp.zeros((1, part_rays), F32) for _ in range(2)]
+                for source in range(BRICKS):
+                    at = (source % RING, source // RING)
+                    code = (at[0] ^ at[0] // 2) + RING * (at[1] ^ at[1] // 2)
+                    mate = (moved(at[1], d == 2, d == 3) * RING
+                            + moved(at[0], d == 0, d == 1))
+                    term = own_all[s, source][:, d * part_rays:(d + 1) * part_rays]
+                    brick = jnp.where(side == 0, source, mate)
+                    half = code >> d & 1
+                    totals[half] = totals[half] + jnp.where(brick > me, term, 0.0)
+                totals = [t + pltpu.roll(t, half_rays, 1) for t in totals]
+                whole = whole + jnp.where(side == 0, totals[0], totals[1])
             out.append(whole)
         return jnp.concatenate(out, 1)
 
@@ -303,8 +339,6 @@
                     dh = wgt[i:i + 1, here] * v + dsig[i:i + 1, here] * wden
                     dpre_ref[down, i * ray + at:i * ray + at + LANES] = jnp.where(
                         hid_ref[s, i, down, here] > 0, dh.astype(BF16), jnp.zeros((), BF16))
-        if s == STREAMS - 1:
-            share_out()
         g_in = mm(dpre_ref[...], f_ref[s].reshape(smp * ray, -1), NN)
         gt_ref[...] = g_in if s == 0 else gt_ref[...] + g_in
         d_high, d_low = halves(dsig)
@@ -350,11 +384,12 @@
         if s % 2 == 1:
             spread_start(t_all.at[s // 2, me], ts_sem.at[0], tr_sem.at[s // 2])
         weigh(s)
-        for part in range(2):
-            send(0, s, part)
+        for rp, cp in parts:
+            send(0, s, rp, cp)
     for step, s in ORDER:
         (reduce_near, reduce_far, gather_far, emissions, gradients)[step](s)
     lax.fori_loop(1, COLS, share_in, 0)
+    share_out()
     dens_copy = pltpu.make_async_copy(dens_ref, dens_hbm, out_sem.at[1])
     dens_copy.start()
     arrived(go_recv, gr_sem.at[1])
@@ -416,12 +451,14 @@
     _, smp, nray, din = features.shape
     hid, width = w_out.shape[1:]
     ray = nray // STREAMS
-    quarter = ray // 2 // RING
-    piece = quarter // RING
+    half_rays = ray // 4
+    half_width = width // 2
+    block = half_rays // 8
     slab = din // COLS
     hbm = pl.BlockSpec(memory_space=pl.ANY)
     dma = pltpu.SemaphoreType.DMA
-    split = (STREAMS, 2, RING, RING, piece, width)
+    split = (STREAMS, 2, 2, 8, block, width)
+    quads = (STREAMS, 2, 2)
     scratch = [
         pltpu.VMEM((1, nray), jnp.int32),
         pltpu.VMEM((1, nray), F32),
@@ -436,18 +473,18 @@
         pltpu.VMEM((STREAMS, smp, ray, din), BF16),
         pltpu.VMEM((STREAMS, smp, hid, ray), BF16),
         pltpu.VMEM((STREAMS, hid, ray), F32),
-        pltpu.VMEM((STREAMS, 2, RING, quarter, width), F32),
-        pltpu.VMEM((STREAMS, 2, RING, quarter, width), F32),
-        pltpu.VMEM((STREAMS, 2, RING, piece, width), F32),
-        pltpu.VMEM((STREAMS, 2, RING - 1, quarter, width), F32),
-        pltpu.VMEM((STREAMS, 2, RING - 1, piece, width), F32),
-        pltpu.VMEM(split, F32),
-        pltpu.VMEM((ray, width), F32),
-        pltpu.VMEM((STREAMS, 2, piece, width), F32),
+        pltpu.VMEM((*quads, 2, 8, block, half_width), F32),
+        pltpu.VMEM((*quads, 2, half_rays, half_width), F32),
+        pltpu.VMEM((*quads, 8, block, half_width), F32),
+        pltpu.VMEM((*quads, 8, block, half_width), F32),
+        pltpu.VMEM((*quads, 7, block, half_width), F32),
+        pltpu.VMEM((*quads, 2, 8, block, half_width), F32),
+        pltpu.VMEM((2 * ray, half_width), F32),
+        pltpu.VMEM((*quads, block, half_width), F32),
         pltpu.VMEM((STREAMS // 2, BRICKS, 1, 2 * ray), F32),
         pltpu.VMEM((STREAMS, BRICKS, 1, ray), F32),
-        pltpu.VMEM((STREAMS, BRICKS, 1, ray), F32),
-        pltpu.VMEM((STREAMS, 2, RING, quarter, smp), F32),
+        pltpu.VMEM((STREAMS, BRICKS, 1, 2 * ray), F32),
+        pltpu.VMEM((STREAMS, 2, 2, half_rays, smp), F32),
         pltpu.VMEM((STREAMS, 5, smp, ray), F32),
         pltpu.VMEM((STREAMS, hid, ray), F32),
         pltpu.VMEM((hid, smp * ray), BF16),
@@ -460,7 +497,7 @@
         pltpu.VMEM((RING, slab, width), F32),
         pltpu.VMEM((RING - 1, slab, width), F32),
         dma((5,)), dma((STREAMS,)), dma((1,)), dma((4,)),
-        dma((4,)), dma((4, STREAMS, 2)),
+        dma((4,)), dma((4, STREAMS)),
         dma((1,)), dma((STREAMS // 2,)), dma((1,)), dma((STREAMS,)),
         dma((3,)), dma((3,)),
     ]

time: 59.3 us -> 56.8 us (0.958); the launches traced: 59.1 us -> 56 us
  Pallas kernels: 58.5 us -> 55.3 us
    pallas_call x1, Pallas kernels: 55.7 us -> 52.5 us  [per_device(): pl.pallas_call(body, out_shape=(jax.ShapeDtypeStruct(split, F32), jax.Sha...]
where the time goes in v7:
time: 56.8 us; the launch traced here: 56 us
  Pallas kernels  55.3 us (97%)
  between operations  0.64 us (1%)
    pallas_call x1, Pallas kernels, per_device(): pl.pallas_call(body, out_shape=(jax.ShapeDtypeStruct(split, F32), jax.Sha...  52.5 us
    pallas_call x1, Pallas kernels, per_device(): pl.pallas_call(finish, out_shape=(jax.ShapeDtypeStruct((STREAMS, ray, wid...  2.79 us

profile of v7, /device:TPU:1, one launch (start us, length us, event | category | flops | bytes accessed | tf_op | source)
XLA Modules:
  0.0 56.0 jit_solution(17930048226197918903)
XLA Ops:
  0.6 52.5 %brick_step.1 = (f32[4,2,2,8,8,512]{5,4,3,2,1,0:T(8,128)}, f32[8,1024]{1,0:T(8,128)}, f32[40,256]{1,0:T(8,128)}, f32[32,512]{1,0:T(8,128)}) custom-call(bf16[8,1024,256]{2,1,0:T(8,128)(2,1)} %bitcast.9, s32[1,1024]{1,0:T(1,128)} %cnt_hbm.1, f32[1,1024]{1,0:T(1,128)} %step_hbm.1, f32[4,2,2,8,8,512]{5,4,3,2,1,0:T(8,128)} %bitcast.11, ...), custom_call_target="tpu_custom_call" | custom-call | tf_op jit(solution)/shard_map/brick_step/pallas_call | solution.py:504
  53.2 2.8 %brick_finish.1 = (f32[4,256,512]{2,1,0:T(8,128)}, f32[8,1024]{1,0:T(8,128)}, f32[32,256]{1,0:T(8,128)}, f32[1,32]{1,0:T(1,128)}, f32[32,512]{1,0:T(8,128)}) custom-call(f32[4,256,512]{2,1,0:T(8,128)} %bitcast.10, f32[8,1024]{1,0:T(8,128)} %get-tuple-element.15.dens_in, f32[40,256]{1,0:T(8,128)} %get-tuple-element.16.gin_in, f32[32,512]{1,0:T(8,128)} %get-tuple-element.17.gout_in), custom_call_target="tpu_custom_call" | custom-call | tf_op jit(solution)/shard_map/brick_finish/pallas_call | solution.py:519

commit v8 on v7

--- a/solution.py
+++ b/solution.py
@@ -47,7 +47,7 @@
          res_hbm, dens_hbm, gin_hbm, gout_hbm,
          cnt_ref, step_ref, win_ref, wden_ref, wout_ref, dens_ref, gin_ref, gout_ref, wint_ref, wcol_ref, f_ref, hid_ref, hbar_ref, p_ref, ps_ref, acc_ref, recv1_ref, recv2_ref, r_ref, prod_ref, tgt_ref,
          t_all, e_all, own_all, ecol_ref, keep_ref, v_ref, dpre_ref, gt_ref, gd_ref,
-         gi_ref, go_ref, gi_recv, go_pair, go_sum, go_recv,
+         gi_ref, go_ref, gi_recv, gr_ref, gr_recv, go_pair, go_sum, go_recv,
          in_sem, f_sem, tgt_sem, out_sem, s_sem, r_sem, ts_sem, tr_sem, os_sem, or_sem, gs_sem, gr_sem):
     smp, ray = f_ref.shape[1], f_ref.shape[2]
     hid, width = wout_ref.shape
@@ -80,19 +80,6 @@
 
     mesh_id = pl.DeviceIdType.MESH
 
-    barrier = pltpu.get_barrier_semaphore()
-
-    def greet_depth(j, _):
-        pl.semaphore_signal(barrier, inc=1, device_id={"depth": (me + j) % BRICKS}, device_id_type=mesh_id)
-        return 0
-
-    def greet_col(j, _):
-        pl.semaphore_signal(barrier, inc=1, device_id={"col": (col + j) % COLS}, device_id_type=mesh_id)
-        return 0
-
-    lax.fori_loop(1, BRICKS, greet_depth, 0)
-    lax.fori_loop(1, COLS, greet_col, 0)
-
     weights = [
         pltpu.make_async_copy(src, dst, in_sem.at[i])
         for i, (src, dst) in enumerate((
@@ -109,9 +96,24 @@
             tgt_hbm.at[s, rp, half, block, :, pl.ds(cp * half_width, half_width)],
             tgt_ref.at[s, rp, cp], tgt_sem.at[0])
 
+    weights[0].start()
     fetch(0).start()
-    for copy in weights:
+    for copy in weights[1:]:
         copy.start()
+
+    barrier = pltpu.get_barrier_semaphore()
+
+    def greet_depth(j, _):
+        pl.semaphore_signal(barrier, inc=1, device_id={"depth": (me + j) % BRICKS}, device_id_type=mesh_id)
+        return 0
+
+    def greet_col(j, _):
+        pl.semaphore_signal(barrier, inc=1, device_id={"col": (col + j) % COLS}, device_id_type=mesh_id)
+        return 0
+
+    lax.fori_loop(1, BRICKS, greet_depth, 0)
+    lax.fori_loop(1, COLS, greet_col, 0)
+
     for s in range(1, STREAMS):
         fetch(s).start()
     for s in range(STREAMS):
@@ -163,23 +165,24 @@
         ref = recv1_ref if stage in (0, 3) else recv2_ref
         arrived(ref.at[s], r_sem.at[stage, s])
 
-    sample = lax.broadcasted_iota(jnp.int32, (smp, hid), 0)
     pair = ray * 2
 
     def forward(s):
+        if s == 0:
+            weights[0].wait()
+            wint_ref[...] = win_ref[...].astype(F32).T.astype(BF16)
+            for copy in weights[1:4]:
+                copy.wait()
+            wcol_ref[...] = jnp.broadcast_to(wden_ref[...].astype(F32), (LANES, hid)).T
         fetch(s).wait()
-        if s == 0:
-            for copy in weights[:4]:
-                copy.wait()
-            wint_ref[...] = win_ref[...].astype(F32).T.astype(BF16)
-            wcol_ref[...] = jnp.broadcast_to(wden_ref[...].astype(F32), (LANES, hid)).T
-        wden = jnp.broadcast_to(wden_ref[...].astype(F32), (smp, hid))
+        place = lax.broadcasted_iota(jnp.int32, (smp, ray), 0)
         sig = jnp.zeros((smp, ray), F32)
         for i in range(smp):
             pre = mm(wint_ref[...], f_ref[s, i], NT)
             h = jnp.maximum(pre, 0.0).astype(BF16)
             hid_ref[s, i] = h
-            sig = sig + mm(jnp.where(sample == i, wden, 0.0).astype(BF16), h, NN)
+            dense = jnp.sum(h.astype(F32) * jnp.concatenate([wcol_ref[...]] * (ray // LANES), 1), 0, keepdims=True)
+            sig = jnp.where(place == i, dense, sig)
         here = pl.ds(s * ray, ray)
         row = lax.broadcasted_iota(jnp.int32, (smp, ray), 0)
         gate = jnp.where(row < cnt_ref[:, here], jnp.broadcast_to(step_ref[:, here], (smp, ray)), 0.0)
@@ -279,7 +282,7 @@
             w = wout_ref[:, cp * half_width:(cp + 1) * half_width]
             term = mm(w, r_high, NT) + mm(w, r_low, NT)
             v = term if cp == 0 else v + term
-            out.append(mm(b_high, r_high, NN) + mm(b_low, r_high, NN) + mm(b_high, r_low, NN))
+            out.append(mm(b_high, r_high, NN) + mm(b_low, r_high, NN))
         v_ref[s] = v
         out = jnp.concatenate(out, 1)
         for c in range(COLS):
@@ -351,10 +354,8 @@
         if s == STREAMS - 1:
             turned = gt_ref[...].T
             den = gd_ref[...].T
-            den = den[:smp] + den[smp:]
-            for c in range(COLS):
-                gi_ref[c, :slab] = turned[c * slab:(c + 1) * slab]
-                gi_ref[c, slab:] = den
+            gr_ref[...] = jnp.sum(den, 0, keepdims=True)
+            gi_ref[...] = turned.reshape(gi_ref.shape)
 
     x, core = col // 2, col % 2
 
@@ -375,6 +376,7 @@
     def share_in(j, _):
         to = (col + j) % COLS
         to_col(gi_ref.at[to], gi_recv.at[j - 1], gs_sem.at[2], gr_sem.at[2], to).start()
+        to_col(gr_ref, gr_recv.at[j - 1], gs_sem.at[3], gr_sem.at[3], to).start()
         return 0
 
     for s in range(STREAMS):
@@ -413,10 +415,16 @@
     total = gi_ref[col]
     for j in range(COLS - 1):
         total = total + gi_recv[j]
-    gin_ref[...] = total
+    gin_ref[:slab] = total
+    arrived(gr_recv, gr_sem.at[3])
+    total = gr_ref[...]
+    for j in range(COLS - 1):
+        total = total + gr_recv[j]
+    gin_ref[slab:] = jnp.broadcast_to(total, (smp, hid))
     gin_copy = pltpu.make_async_copy(gin_ref, gin_hbm, out_sem.at[3])
     gin_copy.start()
     arrived(gi_recv, gs_sem.at[2])
+    arrived(gr_recv, gs_sem.at[3])
     gout_copy.wait()
     gin_copy.wait()
 
@@ -436,7 +444,7 @@
     for got, gone in zip(take, put):
         got.wait()
         gone.start()
-    den = jnp.sum(gin_ref[slab:], 0, keepdims=True)
+    den = gin_ref[slab:slab + 1]
     col = lax.axis_index("col")
     mine = den[:, :slab]
     for c in range(1, COLS):
@@ -490,16 +498,18 @@
         pltpu.VMEM((hid, smp * ray), BF16),
         pltpu.VMEM((hid, din), F32),
         pltpu.VMEM((hid, 2 * smp), F32),
-        pltpu.VMEM((COLS, slab + smp, hid), F32),
+        pltpu.VMEM((COLS, slab, hid), F32),
         pltpu.VMEM((2, RING, slab, width), F32),
-        pltpu.VMEM((COLS - 1, slab + smp, hid), F32),
+        pltpu.VMEM((COLS - 1, slab, hid), F32),
+        pltpu.VMEM((1, hid), F32),
+        pltpu.VMEM((COLS - 1, 1, hid), F32),
         pltpu.VMEM((RING, slab, width), F32),
         pltpu.VMEM((RING, slab, width), F32),
         pltpu.VMEM((RING - 1, slab, width), F32),
         dma((5,)), dma((STREAMS,)), dma((1,)), dma((4,)),
         dma((4,)), dma((4, STREAMS)),
         dma((1,)), dma((STREAMS // 2,)), dma((1,)), dma((STREAMS,)),
-        dma((3,)), dma((3,)),
+        dma((4,)), dma((4,)),
     ]
     residual, dens, g_in, g_out = pl.pallas_call(
         body,
@@ -519,7 +529,7 @@
     residual, dens, g_in, g_den, g_out = pl.pallas_call(
         finish,
         out_shape=(
-            jax.ShapeDtypeStruct((STREAMS, ray, width), F32),
+            jax.ShapeDtypeStruct((8, nray // 8, width), F32),
             jax.ShapeDtypeStruct((smp, nray), F32),
             jax.ShapeDtypeStruct((slab, hid), F32),
             jax.ShapeDtypeStruct((1, slab), F32),
@@ -528,15 +538,15 @@
         in_specs=[hbm] * 4,
         out_specs=(hbm,) * 5,
         scratch_shapes=[
-            pltpu.VMEM((STREAMS, ray, width), F32),
+            pltpu.VMEM((8, nray // 8, width), F32),
             pltpu.VMEM((smp, nray), F32),
             pltpu.VMEM((slab + smp, hid), F32),
             pltpu.VMEM((slab, width), F32),
             pltpu.VMEM((1, slab), F32),
-            dma((3 + STREAMS,)), dma((4 + STREAMS,)),
+            dma((11,)), dma((12,)),
         ],
         name="brick_finish",
-    )(residual.reshape(STREAMS, ray, width), dens, g_in, g_out)
+    )(residual.reshape(8, nray // 8, width), dens, g_in, g_out)
     return residual.reshape(nray, width), dens[None], g_in[None], g_den, g_out[None]
 
 

time: 56.8 us -> 55.1 us (0.970)
  Pallas kernels: 55.3 us -> 53.8 us
    pallas_call x1, Pallas kernels: 52.5 us -> 51.2 us  [per_device(): pl.pallas_call(body, out_shape=(jax.ShapeDtypeStruct(split, F32), jax.Sha...]
where the time goes in v8:
time: 55.1 us; the launch traced here: 54.5 us
  Pallas kernels  53.8 us (98%)
  between operations  0.64 us (1%)
    pallas_call x1, Pallas kernels, per_device(): pl.pallas_call(body, out_shape=(jax.ShapeDtypeStruct(split, F32), jax.Sha...  51.2 us
    pallas_call x1, Pallas kernels, per_device(): pl.pallas_call(finish, out_shape=(jax.ShapeDtypeStruct((8, nray // 8, wid...  2.57 us

profile of v8, /device:TPU:1, one launch (start us, length us, event | category | flops | bytes accessed | tf_op | source)
XLA Modules:
  0.0 54.5 jit_solution(18399009504815526797)
XLA Ops:
  0.6 51.2 %brick_step.1 = (f32[4,2,2,8,8,512]{5,4,3,2,1,0:T(8,128)}, f32[8,1024]{1,0:T(8,128)}, f32[40,256]{1,0:T(8,128)}, f32[32,512]{1,0:T(8,128)}) custom-call(bf16[8,1024,256]{2,1,0:T(8,128)(2,1)} %bitcast.9, s32[1,1024]{1,0:T(1,128)} %cnt_hbm.1, f32[1,1024]{1,0:T(1,128)} %step_hbm.1, f32[4,2,2,8,8,512]{5,4,3,2,1,0:T(8,128)} %bitcast.11, ...), custom_call_target="tpu_custom_call" | custom-call | tf_op jit(solution)/shard_map/brick_step/pallas_call | solution.py:514
  51.9 2.6 %brick_finish.1 = (f32[8,128,512]{2,1,0:T(8,128)}, f32[8,1024]{1,0:T(8,128)}, f32[32,256]{1,0:T(8,128)}, f32[1,32]{1,0:T(1,128)}, f32[32,512]{1,0:T(8,128)}) custom-call(f32[8,128,512]{2,1,0:T(8,128)} %bitcast.10, f32[8,1024]{1,0:T(8,128)} %get-tuple-element.15.dens_in, f32[40,256]{1,0:T(8,128)} %get-tuple-element.16.gin_in, f32[32,512]{1,0:T(8,128)} %get-tuple-element.17.gout_in), custom_call_target="tpu_custom_call" | custom-call | tf_op jit(solution)/shard_map/brick_finish/pallas_call | solution.py:529

commit v9 on v8

--- a/solution.py
+++ b/solution.py
@@ -165,7 +165,6 @@
         ref = recv1_ref if stage in (0, 3) else recv2_ref
         arrived(ref.at[s], r_sem.at[stage, s])
 
-    pair = ray * 2
 
     def forward(s):
         if s == 0:
@@ -189,7 +188,10 @@
         soft = jnp.maximum(sig, 0.0) + jnp.log1p(jnp.exp(-jnp.abs(sig)))
         tau = soft * gate
         inner = running(tau, False)
-        t_all[s // 2, me, :, s % 2 * ray:(s % 2 + 1) * ray] = (inner + tau)[smp - 1:smp]
+        t_all[s, me] = (inner + tau)[smp - 1:smp]
+        if s == 0:
+            pl.semaphore_wait(barrier, BRICKS - 1 + COLS - 1)
+        spread_start(t_all.at[s, me], ts_sem.at[0], tr_sem.at[s])
         keep = jnp.exp(-tau)
         light = jnp.exp(-inner)
         lw = light * (1.0 - keep)
@@ -214,14 +216,11 @@
             p_ref[s, cp] = value[:, cp * half_width:(cp + 1) * half_width].reshape(p_ref.shape[2:])
 
     def reduce_near(s):
-        if s % 2 == 0:
-            arrived(t_all.at[s // 2, pl.ds(0, BRICKS - 1)], tr_sem.at[s // 2])
-            before = jnp.zeros((1, pair), F32)
-            for b in range(BRICKS):
-                light = jnp.exp(-before)
-                e_all[s, b] = light[:, :ray]
-                e_all[s + 1, b] = light[:, ray:]
-                before = before + t_all[s // 2, b]
+        arrived(t_all.at[s, pl.ds(0, BRICKS - 1)], tr_sem.at[s])
+        before = jnp.zeros((1, ray), F32)
+        for b in range(BRICKS):
+            e_all[s, b] = jnp.exp(-before)
+            before = before + t_all[s, b]
         row = lax.broadcasted_iota(jnp.int32, (smp, ray), 0)
         table = jnp.broadcast_to(e_all[s, me], (smp, ray))
         for d in range(4):
@@ -381,10 +380,6 @@
 
     for s in range(STREAMS):
         forward(s)
-        if s == 0:
-            pl.semaphore_wait(barrier, BRICKS - 1 + COLS - 1)
-        if s % 2 == 1:
-            spread_start(t_all.at[s // 2, me], ts_sem.at[0], tr_sem.at[s // 2])
         weigh(s)
         for rp, cp in parts:
             send(0, s, rp, cp)
@@ -489,7 +484,7 @@
         pltpu.VMEM((*quads, 2, 8, block, half_width), F32),
         pltpu.VMEM((2 * ray, half_width), F32),
         pltpu.VMEM((*quads, block, half_width), F32),
-        pltpu.VMEM((STREAMS // 2, BRICKS, 1, 2 * ray), F32),
+        pltpu.VMEM((STREAMS, BRICKS, 1, ray), F32),
         pltpu.VMEM((STREAMS, BRICKS, 1, ray), F32),
         pltpu.VMEM((STREAMS, BRICKS, 1, 2 * ray), F32),
         pltpu.VMEM((STREAMS, 2, 2, half_rays, smp), F32),
@@ -508,7 +503,7 @@
         pltpu.VMEM((RING - 1, slab, width), F32),
         dma((5,)), dma((STREAMS,)), dma((1,)), dma((4,)),
         dma((4,)), dma((4, STREAMS)),
-        dma((1,)), dma((STREAMS // 2,)), dma((1,)), dma((STREAMS,)),
+        dma((1,)), dma((STREAMS,)), dma((1,)), dma((STREAMS,)),
         dma((4,)), dma((4,)),
     ]
     residual, dens, g_in, g_out = pl.pallas_call(

time: 55.1 us -> 54.6 us (level)
  Pallas kernels: 53.8 us -> 53.1 us
    pallas_call x1, Pallas kernels: 51.2 us -> 50.5 us  [per_device(): pl.pallas_call(body, out_shape=(jax.ShapeDtypeStruct(split, F32), jax.Sha...]
where the time goes in v9:
time: 54.6 us; the launch traced here: 53.8 us
  Pallas kernels  53.1 us (97%)
  between operations  0.64 us (1%)
    pallas_call x1, Pallas kernels, per_device(): pl.pallas_call(body, out_shape=(jax.ShapeDtypeStruct(split, F32), jax.Sha...  50.5 us
    pallas_call x1, Pallas kernels, per_device(): pl.pallas_call(finish, out_shape=(jax.ShapeDtypeStruct((8, nray // 8, wid...  2.57 us

profile of v9, /device:TPU:1, one launch (start us, length us, event | category | flops | bytes accessed | tf_op | source)
XLA Modules:
  0.0 53.8 jit_solution(11515111581422125677)
XLA Ops:
  0.6 50.5 %brick_step.1 = (f32[4,2,2,8,8,512]{5,4,3,2,1,0:T(8,128)}, f32[8,1024]{1,0:T(8,128)}, f32[40,256]{1,0:T(8,128)}, f32[32,512]{1,0:T(8,128)}) custom-call(bf16[8,1024,256]{2,1,0:T(8,128)(2,1)} %bitcast.9, s32[1,1024]{1,0:T(1,128)} %cnt_hbm.1, f32[1,1024]{1,0:T(1,128)} %step_hbm.1, f32[4,2,2,8,8,512]{5,4,3,2,1,0:T(8,128)} %bitcast.11, ...), custom_call_target="tpu_custom_call" | custom-call | tf_op jit(solution)/shard_map/brick_step/pallas_call | solution.py:509
  51.2 2.6 %brick_finish.1 = (f32[8,128,512]{2,1,0:T(8,128)}, f32[8,1024]{1,0:T(8,128)}, f32[32,256]{1,0:T(8,128)}, f32[1,32]{1,0:T(1,128)}, f32[32,512]{1,0:T(8,128)}) custom-call(f32[8,128,512]{2,1,0:T(8,128)} %bitcast.10, f32[8,1024]{1,0:T(8,128)} %get-tuple-element.15.dens_in, f32[40,256]{1,0:T(8,128)} %get-tuple-element.16.gin_in, f32[32,512]{1,0:T(8,128)} %get-tuple-element.17.gout_in), custom_call_target="tpu_custom_call" | custom-call | tf_op jit(solution)/shard_map/brick_finish/pallas_call | solution.py:524

commit v10 on v9

--- a/solution.py
+++ b/solution.py
@@ -160,6 +160,11 @@
     def send(stage, s, rp, cp):
         for copy in hops(stage, s, rp, cp):
             copy.start()
+
+    def send_mixed(stage, s):
+        for group in zip(*(hops(stage, s, rp, cp) for rp, cp in parts)):
+            for copy in group:
+                copy.start()
 
     def got_all(stage, s):
         ref = recv1_ref if stage in (0, 3) else recv2_ref
@@ -235,7 +240,7 @@
             ps_ref[s, rp, cp, 0] = own
             ps_ref[s, rp, cp, 1] = got
             acc_ref[s, rp, cp] = (own + got).reshape(acc_ref.shape[3:])
-            send(1, s, rp, cp)
+        send_mixed(1, s)
 
     def reduce_far(s):
         if s == 0:
@@ -247,7 +252,7 @@
             for k in range(7):
                 total = total + recv2_ref[s, rp, cp, k]
             r_ref[s, cp, rp, half, block] = total
-            send(2, s, rp, cp)
+        send_mixed(2, s)
 
     def gather_far(s):
         got_all(2, s)
@@ -385,7 +390,8 @@
             send(0, s, rp, cp)
     for step, s in ORDER:
         (reduce_near, reduce_far, gather_far, emissions, gradients)[step](s)
-    lax.fori_loop(1, COLS, share_in, 0)
+    for j in (4, 3, 5, 2, 6, 1, 7):
+        share_in(j, 0)
     share_out()
     dens_copy = pltpu.make_async_copy(dens_ref, dens_hbm, out_sem.at[1])
     dens_copy.start()

time: 54.6 us -> 54.4 us (level)
  no operation moved by 1% of the time
where the time goes in v10:
time: 54.4 us; the launch traced here: 53.6 us
  Pallas kernels  53 us (97%)
  between operations  0.64 us (1%)
    pallas_call x1, Pallas kernels, per_device(): pl.pallas_call(body, out_shape=(jax.ShapeDtypeStruct(split, F32), jax.Sha...  50.4 us
    pallas_call x1, Pallas kernels, per_device(): pl.pallas_call(finish, out_shape=(jax.ShapeDtypeStruct((8, nray // 8, wid...  2.57 us

profile of v10, /device:TPU:1, one launch (start us, length us, event | category | flops | bytes accessed | tf_op | source)
XLA Modules:
  0.0 53.6 jit_solution(15127417865028933427)
XLA Ops:
  0.6 50.4 %brick_step.1 = (f32[4,2,2,8,8,512]{5,4,3,2,1,0:T(8,128)}, f32[8,1024]{1,0:T(8,128)}, f32[40,256]{1,0:T(8,128)}, f32[32,512]{1,0:T(8,128)}) custom-call(bf16[8,1024,256]{2,1,0:T(8,128)(2,1)} %bitcast.9, s32[1,1024]{1,0:T(1,128)} %cnt_hbm.1, f32[1,1024]{1,0:T(1,128)} %step_hbm.1, f32[4,2,2,8,8,512]{5,4,3,2,1,0:T(8,128)} %bitcast.11, ...), custom_call_target="tpu_custom_call" | custom-call | tf_op jit(solution)/shard_map/brick_step/pallas_call | solution.py:515
  51.0 2.6 %brick_finish.1 = (f32[8,128,512]{2,1,0:T(8,128)}, f32[8,1024]{1,0:T(8,128)}, f32[32,256]{1,0:T(8,128)}, f32[1,32]{1,0:T(1,128)}, f32[32,512]{1,0:T(8,128)}) custom-call(f32[8,128,512]{2,1,0:T(8,128)} %bitcast.10, f32[8,1024]{1,0:T(8,128)} %get-tuple-element.15.dens_in, f32[40,256]{1,0:T(8,128)} %get-tuple-element.16.gin_in, f32[32,512]{1,0:T(8,128)} %get-tuple-element.17.gout_in), custom_call_target="tpu_custom_call" | custom-call | tf_op jit(solution)/shard_map/brick_finish/pallas_call | solution.py:530

commit v11 on v10

--- a/solution.py
+++ b/solution.py
@@ -130,7 +130,7 @@
 
     def spread_start(row, send, recv):
         def one(j, _):
-            to_depth(row, row, send, recv, (me + j) % BRICKS).start()
+            to_depth(row, row, send, recv, (me + 1 + (j + 6) % (BRICKS - 1)) % BRICKS).start()
             return 0
         lax.fori_loop(1, BRICKS, one, 0)
 

time: 54.4 us -> 54.6 us (level)
  no operation moved by 1% of the time
where the time goes in v11:
time: 54.6 us; the launch traced here: 53.9 us
  Pallas kernels  53.3 us (98%)
  between operations  0.64 us (1%)
    pallas_call x1, Pallas kernels, per_device(): pl.pallas_call(body, out_shape=(jax.ShapeDtypeStruct(split, F32), jax.Sha...  50.7 us
    pallas_call x1, Pallas kernels, per_device(): pl.pallas_call(finish, out_shape=(jax.ShapeDtypeStruct((8, nray // 8, wid...  2.57 us

profile of v11, /device:TPU:1, one launch (start us, length us, event | category | flops | bytes accessed | tf_op | source)
XLA Modules:
  0.0 53.9 jit_solution(14697326894091193183)
XLA Ops:
  0.6 50.7 %brick_step.1 = (f32[4,2,2,8,8,512]{5,4,3,2,1,0:T(8,128)}, f32[8,1024]{1,0:T(8,128)}, f32[40,256]{1,0:T(8,128)}, f32[32,512]{1,0:T(8,128)}) custom-call(bf16[8,1024,256]{2,1,0:T(8,128)(2,1)} %bitcast.9, s32[1,1024]{1,0:T(1,128)} %cnt_hbm.1, f32[1,1024]{1,0:T(1,128)} %step_hbm.1, f32[4,2,2,8,8,512]{5,4,3,2,1,0:T(8,128)} %bitcast.11, ...), custom_call_target="tpu_custom_call" | custom-call | tf_op jit(solution)/shard_map/brick_step/pallas_call | solution.py:515
  51.4 2.6 %brick_finish.1 = (f32[8,128,512]{2,1,0:T(8,128)}, f32[8,1024]{1,0:T(8,128)}, f32[32,256]{1,0:T(8,128)}, f32[1,32]{1,0:T(1,128)}, f32[32,512]{1,0:T(8,128)}) custom-call(f32[8,128,512]{2,1,0:T(8,128)} %bitcast.10, f32[8,1024]{1,0:T(8,128)} %get-tuple-element.15.dens_in, f32[40,256]{1,0:T(8,128)} %get-tuple-element.16.gin_in, f32[32,512]{1,0:T(8,128)} %get-tuple-element.17.gout_in), custom_call_target="tpu_custom_call" | custom-call | tf_op jit(solution)/shard_map/brick_finish/pallas_call | solution.py:530
